TPU v7x, 128 devices: a whole 4x4x4 slice. The times are simulated.
128 devices in a mesh: section: 4 (over x_lo, core), ctx: 8 (over x_hi, z), tp: 4 (over y).
Axes of the slice: x: 4 (x_hi: 2, x_lo: 2; x = x_hi * 2 + x_lo), y: 4, z: 4, core: 2. Of those that a mesh axis runs over, the one named last changes fastest.
Arguments:
- stretch_order: int32 [8, 2], replicated, may hold values from 0 to 15, as said below
- queries: bfloat16 [4, 4096, 2048], P('section', 'ctx', 'tp'), may hold values from -60 to 60
- key_rows: bfloat16 [4, 4096, 512], P('section', 'ctx', 'tp'), may hold values from -7 to 7
- value_rows: bfloat16 [4, 4096, 512], P('section', 'ctx', 'tp'), may hold values from -5 to 5
- out_grad: bfloat16 [4, 4096, 4096], P('section', ('ctx', 'tp')), may hold values from -6 to 6
- query_weight: bfloat16 [4, 4096, 2048], P('section', None, 'tp'), may hold values from -0.09375 to 0.09375
- key_weight: bfloat16 [4, 4096, 512], P('section', None, 'tp'), may hold values from -0.09375 to 0.09375
- value_weight: bfloat16 [4, 4096, 512], P('section', None, 'tp'), may hold values from -0.09375 to 0.09375
- output_weight: bfloat16 [4, 2048, 4096], P('section', 'tp'), may hold values from -0.125 to 0.125
Outputs:
- sent_grad: bfloat16 [4, 4096, 4096], P('section', ('ctx', 'tp'))
- key_grad: bfloat16 [4, 4096, 512], P('section', 'ctx', 'tp')
- value_grad: bfloat16 [4, 4096, 512], P('section', 'ctx', 'tp')
Inputs may be any that keep to these rules, and one draw needn't show every extreme that they name: `stretch_order`: row c lists the ids of the two blocks of 256 consecutive positions stored, in that order, at ctx index c; the two ids of a row sum to 15 and every id occurs once.
All inputs are finite; a program needn't handle non-finite values.
Results may differ from a plain program's by a relative error of at most 0.015.
Values may be sent and summed in bfloat16 or wider, within the bound.
No kernel may reach another device: no remote copies, remote signals or barrier semaphores. Data moves between devices by JAX's collectives and lax.ppermute only.
A program may use at most 128 MiB of HBM per device.

v0:
```python
import jax
import jax.numpy as jnp
from jax import lax
from jax.experimental import pallas as pl
from jax.experimental.pallas import tpu as pltpu
from jax.sharding import PartitionSpec as P

HD = 128
BLK = 256
GROUP = 4
STEPS = 17
SCALE = HD ** (-0.5)
EXP2_SCALE = SCALE * 1.4426950408889634
NEG_LARGE = -1e30

VMEM_WHOLE = pl.BlockSpec(memory_space=pltpu.VMEM)
PARAMS = pltpu.CompilerParams(vmem_limit_bytes=36 << 20)


def dot_nt(lhs, rhs):
    return lax.dot_general(lhs, rhs, (((1,), (1,)), ((), ())), preferred_element_type=jnp.float32)


def dot_nn(lhs, rhs):
    return lax.dot_general(lhs, rhs, (((1,), (0,)), ((), ())), preferred_element_type=jnp.float32)


def ring(size, shift):
    return [(i, (i + shift) % size) for i in range(size)]


def z_ring(shift):
    return [(x * 4 + z, x * 4 + (z + shift) % 4) for x in range(2) for z in range(4)]


X_SWAP = [(x * 4 + z, (1 - x) * 4 + z) for x in range(2) for z in range(4)]


def joint_ring(shift):
    return [(s * 4 + t, ((s - 1) % 4) * 4 + (t + shift) % 4) for s in range(4) for t in range(4)]


def step_block(step, split):
    half = (step > split).astype(jnp.int32)
    return half, step - half * (split + 1)


def step_args(step, split):
    half, kb = step_block(step, split)
    diag = ((step == split) | (step == STEPS - 1)).astype(jnp.int32)
    return half, kb, diag


def forward_kernel(split_ref, ids_ref, *refs):
    kv_refs = refs[:8]
    (
        q_ref, p_ref, out_ref, stat_ref, hist_ref, kvs_ref,
        max_ref, acc_ref, bias_ref, even_ref, odd_ref, even_top_ref, odd_top_ref,
    ) = refs[8:]
    step = pl.program_id(0)
    split = split_ref[0]
    _, kb, diag = step_args(step, split)

    def score_step(at, score_ref, top_ref):
        at_half, at_kb, at_diag = step_args(at, split)
        start = pl.multiple_of(at_half * BLK, BLK)
        key_blk = kvs_ref[at_kb, :, :HD]
        for h in range(GROUP):
            query = q_ref[pl.ds(start, BLK), h * HD : (h + 1) * HD]
            scores = dot_nt(key_blk, query) + bias_ref[at_diag]
            score_ref[h] = scores
            top_ref[0:1, h * BLK : (h + 1) * BLK] = jnp.max(scores, axis=0, keepdims=True)

    @pl.when(step == 0)
    def _():
        for j in range(8):
            for r in range(2):
                kvs_ref[ids_ref[2 * j + r]] = kv_refs[j][r * BLK : (r + 1) * BLK, :]
        gap = lax.broadcasted_iota(jnp.int32, (BLK, BLK), 0) - lax.broadcasted_iota(
            jnp.int32, (BLK, BLK), 1
        )
        bias_ref[0] = jnp.zeros((BLK, BLK), jnp.float32)
        bias_ref[1] = jnp.where(gap <= 0, 0.0, NEG_LARGE)
        max_ref[...] = jnp.full_like(max_ref, NEG_LARGE)
        acc_ref[...] = jnp.zeros_like(acc_ref)
        score_step(step, even_ref, even_top_ref)

    def softmax_step(now, now_top, later, later_top):
        score_step(jnp.minimum(step + 1, STEPS - 1), later, later_top)
        value_t = jnp.transpose(kvs_ref[kb, :, HD:].astype(jnp.float32)).astype(jnp.bfloat16)
        lhs = jnp.concatenate([value_t, jnp.ones((16, BLK), jnp.bfloat16)], axis=0)
        for h in range(GROUP):
            cols = slice(h * BLK, (h + 1) * BLK)
            old_max = jnp.where(kb == 0, NEG_LARGE, max_ref[0:1, cols])
            new_max = jnp.maximum(old_max, now_top[0:1, cols])
            probs = jnp.exp2((now[h] - new_max) * EXP2_SCALE).astype(jnp.bfloat16)
            p_ref[step, h] = probs
            factor = jnp.exp2((old_max - new_max) * EXP2_SCALE)
            acc_ref[:, cols] = acc_ref[:, cols] * factor + dot_nn(lhs, probs)
            max_ref[0:1, cols] = new_max
            hist_ref[0, 0:1, cols] = new_max

    @pl.when(step % 2 == 0)
    def _():
        softmax_step(even_ref, even_top_ref, odd_ref, odd_top_ref)

    @pl.when(step % 2 == 1)
    def _():
        softmax_step(odd_ref, odd_top_ref, even_ref, even_top_ref)

    @pl.when(diag == 1)
    def _():
        inv = 1.0 / acc_ref[HD : HD + 1, :]
        out_ref[0] = acc_ref[:HD, :] * inv
        stat_ref[0, 0:1, :] = max_ref[0:1, :]
        stat_ref[0, 1:2, :] = inv


def half_of(step, split_ref):
    return (step > split_ref[0]).astype(jnp.int32)


def block_of(step, split_ref):
    return step - half_of(step, split_ref) * (split_ref[0] + 1)


def forward_call(split, ids, kv_chunks, queries):
    whole = pl.BlockSpec((2 * BLK, 2 * HD), lambda i, s, d: (0, 0))
    wide = GROUP * BLK
    return pl.pallas_call(
        forward_kernel,
        grid_spec=pltpu.PrefetchScalarGridSpec(
            num_scalar_prefetch=2,
            grid=(STEPS,),
            in_specs=[whole] * 8 + [pl.BlockSpec((2 * BLK, GROUP * HD), lambda i, s, d: (0, 0))],
            out_specs=[
                VMEM_WHOLE,
                pl.BlockSpec((1, HD, wide), lambda i, s, d: (half_of(i, s), 0, 0)),
                pl.BlockSpec((1, 8, wide), lambda i, s, d: (half_of(i, s), 0, 0)),
                pl.BlockSpec((1, 1, wide), lambda i, s, d: (i, 0, 0)),
                pl.BlockSpec((16, BLK, 2 * HD), lambda i, s, d: (0, 0, 0)),
            ],
            scratch_shapes=[
                pltpu.VMEM((8, wide), jnp.float32),
                pltpu.VMEM((HD + 16, wide), jnp.float32),
                pltpu.VMEM((2, BLK, BLK), jnp.float32),
                pltpu.VMEM((GROUP, BLK, BLK), jnp.float32),
                pltpu.VMEM((GROUP, BLK, BLK), jnp.float32),
                pltpu.VMEM((8, wide), jnp.float32),
                pltpu.VMEM((8, wide), jnp.float32),
            ],
        ),
        out_shape=[
            jax.ShapeDtypeStruct((STEPS, GROUP, BLK, BLK), jnp.bfloat16),
            jax.ShapeDtypeStruct((2, HD, wide), jnp.float32),
            jax.ShapeDtypeStruct((2, 8, wide), jnp.float32),
            jax.ShapeDtypeStruct((STEPS, 1, wide), jnp.float32),
            jax.ShapeDtypeStruct((16, BLK, 2 * HD), jnp.bfloat16),
        ],
        compiler_params=PARAMS,
        cost_estimate=pl.CostEstimate(
            flops=2 * 2 * STEPS * wide * BLK * HD,
            bytes_accessed=13 << 20,
            transcendentals=STEPS * wide * BLK,
        ),
        name="attn_forward",
    )(split, ids, *kv_chunks, queries)


def grad_kernel(rows_ref, *refs):
    pieces = refs[:5]
    weight_ref, out_ref, lhs_ref, acc_ref = refs[5:]
    step = pl.program_id(0)
    depth = lhs_ref.shape[1]

    @pl.when(step == 0)
    def _():
        acc_ref[...] = jnp.zeros_like(acc_ref)

    for j, piece in enumerate(pieces):
        size = piece.shape[0]
        lhs_ref[pl.ds(pl.multiple_of(rows_ref[j], 64), size), :] = piece[...]
    start = pl.multiple_of(step * depth, depth)
    acc_ref[...] += dot_nt(lhs_ref[...], weight_ref[:, pl.ds(start, depth)])

    @pl.when(step == pl.num_programs(0) - 1)
    def _():
        out_ref[...] = acc_ref[...].astype(jnp.bfloat16)


def grad_call(rows, pieces, out_weight):
    depth = 512
    total = out_weight.shape[0]
    return pl.pallas_call(
        grad_kernel,
        grid_spec=pltpu.PrefetchScalarGridSpec(
            num_scalar_prefetch=1,
            grid=(out_weight.shape[1] // depth,),
            in_specs=[pl.BlockSpec((p.shape[0], depth), lambda i, w: (0, i)) for p in pieces]
            + [VMEM_WHOLE],
            out_specs=pl.BlockSpec((2 * BLK, total), lambda i, w: (0, 0)),
            scratch_shapes=[
                pltpu.VMEM((2 * BLK, depth), jnp.bfloat16),
                pltpu.VMEM((2 * BLK, total), jnp.float32),
            ],
        ),
        out_shape=jax.ShapeDtypeStruct((2 * BLK, total), jnp.bfloat16),
        compiler_params=PARAMS,
        cost_estimate=pl.CostEstimate(
            flops=2 * 2 * BLK * total * out_weight.shape[1],
            bytes_accessed=9 << 20,
            transcendentals=0,
        ),
        name="attn_grad",
    )(rows, *pieces, out_weight)


def norm_of(hist_ref, stat_ref, cols):
    gap = (hist_ref[0, 0:1, cols] - stat_ref[0, 0:1, cols]) * EXP2_SCALE
    return jnp.exp2(gap) * stat_ref[0, 1:2, cols]


def write_groups(ids_ref, total_ref, group_refs, scale):
    for g, g_ref in enumerate(group_refs):
        for x in range(2):
            for r in range(2):
                block = ids_ref[4 * g + 2 * x + r]
                g_ref[x, r * BLK : (r + 1) * BLK, :] = (total_ref[block] * scale).astype(
                    jnp.bfloat16
                )


def value_kernel(split_ref, ids_ref, grad_ref, p_ref, stat_ref, hist_ref, *refs):
    group_refs = refs[:4]
    total_ref = refs[4]
    step = pl.program_id(0)
    half, kb, _ = step_args(step, split_ref[0])

    @pl.when(step == 0)
    def _():
        total_ref[...] = jnp.zeros_like(total_ref)

    start = pl.multiple_of(half * BLK, BLK)
    dv = jnp.zeros((BLK, HD), jnp.float32)
    for h in range(GROUP):
        norm = norm_of(hist_ref, stat_ref, slice(h * BLK, (h + 1) * BLK))
        probs = (p_ref[step, h].astype(jnp.float32) * norm).astype(jnp.bfloat16)
        dv = dv + dot_nn(probs, grad_ref[pl.ds(start, BLK), h * HD : (h + 1) * HD])
    total_ref[kb] += dv

    @pl.when(step == STEPS - 1)
    def _():
        write_groups(ids_ref, total_ref, group_refs, 1.0)


def value_call(split, ids, grad, saved):
    probs, _, stats, hist, _ = saved
    wide = GROUP * BLK
    group_spec = pl.BlockSpec((2, 2 * BLK, HD), lambda i, s, d: (0, 0, 0))
    return pl.pallas_call(
        value_kernel,
        grid_spec=pltpu.PrefetchScalarGridSpec(
            num_scalar_prefetch=2,
            grid=(STEPS,),
            in_specs=[
                pl.BlockSpec((2 * BLK, GROUP * HD), lambda i, s, d: (0, 0)),
                VMEM_WHOLE,
                pl.BlockSpec((1, 8, wide), lambda i, s, d: (half_of(i, s), 0, 0)),
                pl.BlockSpec((1, 1, wide), lambda i, s, d: (i, 0, 0)),
            ],
            out_specs=[group_spec] * 4,
            scratch_shapes=[pltpu.VMEM((16, BLK, HD), jnp.float32)],
        ),
        out_shape=[jax.ShapeDtypeStruct((2, 2 * BLK, HD), jnp.bfloat16)] * 4,
        compiler_params=PARAMS,
        cost_estimate=pl.CostEstimate(
            flops=2 * STEPS * wide * BLK * HD, bytes_accessed=11 << 20, transcendentals=0
        ),
        name="attn_value_grad",
    )(split, ids, grad, probs, stats, hist)


def key_kernel(split_ref, ids_ref, grad_ref, q_ref, p_ref, kv_ref, next_ref, out_ref, stat_ref,
               hist_ref, *refs):
    dq_ref = refs[0]
    group_refs = refs[1:5]
    delta_ref, dqt_ref, total_ref, even_ref, odd_ref = refs[5:]
    step = pl.program_id(0)
    split = split_ref[0]
    half, kb, diag = step_args(step, split)

    def grad_probs_step(at, value_blk, gp_ref):
        at_half = (at > split).astype(jnp.int32)
        start = pl.multiple_of(at_half * BLK, BLK)
        for h in range(GROUP):
            gp_ref[h] = dot_nt(
                value_blk, grad_ref[pl.ds(start, BLK), h * HD : (h + 1) * HD]
            )

    @pl.when(step == 0)
    def _():
        total_ref[...] = jnp.zeros_like(total_ref)
        dqt_ref[...] = jnp.zeros_like(dqt_ref)
        grad_probs_step(step, kv_ref[0, :, HD:], even_ref)

    start = pl.multiple_of(half * BLK, BLK)

    @pl.when(kb == 0)
    def _():
        for h in range(GROUP):
            cols = slice(h * BLK, (h + 1) * BLK)
            grad = grad_ref[pl.ds(start, BLK), h * HD : (h + 1) * HD]
            grad_t = jnp.transpose(grad.astype(jnp.float32))
            delta_ref[0:1, cols] = jnp.sum(out_ref[0, :, cols] * grad_t, axis=0, keepdims=True)

    def main_step(now, later):
        grad_probs_step(jnp.minimum(step + 1, STEPS - 1), next_ref[0, :, HD:], later)
        key_t = jnp.transpose(kv_ref[0, :, :HD].astype(jnp.float32)).astype(jnp.bfloat16)
        keep = jnp.where(kb == 0, 0.0, 1.0)
        dk = jnp.zeros((BLK, HD), jnp.float32)
        for h in range(GROUP):
            cols = slice(h * BLK, (h + 1) * BLK)
            probs = p_ref[step, h].astype(jnp.float32) * norm_of(hist_ref, stat_ref, cols)
            dscore = (probs * (now[h] - delta_ref[0:1, cols])).astype(jnp.bfloat16)
            dk = dk + dot_nn(dscore, q_ref[pl.ds(start, BLK), h * HD : (h + 1) * HD])
            dqt_ref[:, cols] = dqt_ref[:, cols] * keep + dot_nn(key_t, dscore)
        total_ref[kb] += dk

    @pl.when(step % 2 == 0)
    def _():
        main_step(even_ref, odd_ref)

    @pl.when(step % 2 == 1)
    def _():
        main_step(odd_ref, even_ref)

    @pl.when(diag == 1)
    def _():
        for h in range(GROUP):
            cols = slice(h * BLK, (h + 1) * BLK)
            dq_ref[:, h * HD : (h + 1) * HD] = jnp.transpose(dqt_ref[:, cols] * SCALE).astype(
                jnp.bfloat16
            )

    @pl.when(step == STEPS - 1)
    def _():
        write_groups(ids_ref, total_ref, group_refs, SCALE)


def key_call(split, ids, grad, saved, queries):
    probs, outs, stats, hist, kv_sorted = saved
    wide = GROUP * BLK
    group_spec = pl.BlockSpec((2, 2 * BLK, HD), lambda i, s, d: (0, 0, 0))
    whole = pl.BlockSpec((2 * BLK, GROUP * HD), lambda i, s, d: (0, 0))

    def next_block(i, s, d):
        return (block_of(jnp.minimum(i + 1, STEPS - 1), s), 0, 0)

    return pl.pallas_call(
        key_kernel,
        grid_spec=pltpu.PrefetchScalarGridSpec(
            num_scalar_prefetch=2,
            grid=(STEPS,),
            in_specs=[
                whole,
                whole,
                VMEM_WHOLE,
                pl.BlockSpec((1, BLK, 2 * HD), lambda i, s, d: (block_of(i, s), 0, 0)),
                pl.BlockSpec((1, BLK, 2 * HD), next_block),
                pl.BlockSpec((1, HD, wide), lambda i, s, d: (half_of(i, s), 0, 0)),
                pl.BlockSpec((1, 8, wide), lambda i, s, d: (half_of(i, s), 0, 0)),
                pl.BlockSpec((1, 1, wide), lambda i, s, d: (i, 0, 0)),
            ],
            out_specs=[pl.BlockSpec((BLK, GROUP * HD), lambda i, s, d: (half_of(i, s), 0))]
            + [group_spec] * 4,
            scratch_shapes=[
                pltpu.VMEM((8, wide), jnp.float32),
                pltpu.VMEM((HD, wide), jnp.float32),
                pltpu.VMEM((16, BLK, HD), jnp.float32),
                pltpu.VMEM((GROUP, BLK, BLK), jnp.float32),
                pltpu.VMEM((GROUP, BLK, BLK), jnp.float32),
            ],
        ),
        out_shape=[jax.ShapeDtypeStruct((2 * BLK, GROUP * HD), jnp.bfloat16)]
        + [jax.ShapeDtypeStruct((2, 2 * BLK, HD), jnp.bfloat16)] * 4,
        compiler_params=PARAMS,
        cost_estimate=pl.CostEstimate(
            flops=2 * 3 * STEPS * wide * BLK * HD, bytes_accessed=14 << 20, transcendentals=0
        ),
        name="attn_key_grad",
    )(split, ids, grad, queries, probs, kv_sorted, kv_sorted, outs, stats, hist)


def per_device(
    stretch_order,
    queries,
    key_rows,
    value_rows,
    out_grad,
    query_weight,
    key_weight,
    value_weight,
    output_weight,
):
    send = lax.ppermute
    tp = lax.axis_index("tp")
    ctx = lax.axis_index("ctx")
    own_x, own_z = ctx // 4, ctx % 4
    bf16 = jnp.bfloat16

    kv_own = jnp.concatenate([key_rows[0], value_rows[0]], axis=1)
    kv_pair = send(kv_own, "ctx", X_SWAP)

    chunk = out_grad[0]
    half_rows = chunk.shape[0] // 2
    left_chunk = send(chunk, "tp", ring(4, 1))
    right_chunk = send(chunk, "tp", ring(4, -1))
    far_top = send(left_chunk[:half_rows], "tp", ring(4, 1))
    far_low = send(right_chunk[half_rows:], "tp", ring(4, -1))

    kv_chunks = [kv_own, kv_pair]
    for shift in (-1, 2, 1):
        kv_chunks.append(send(kv_own, "ctx", z_ring(shift)))
        kv_chunks.append(send(kv_pair, "ctx", z_ring(shift)))

    index = jnp.arange(8, dtype=jnp.int32)
    source = ((own_x + index % 2) % 2) * 4 + (own_z + index // 2) % 4
    table = jnp.arange(8, dtype=jnp.int32)
    ids = jnp.sum(
        jnp.where(source[:, None, None] == table[None, :, None], stretch_order[None], 0), axis=1
    ).reshape(16)
    split = ids[:1]
    saved = forward_call(split, ids, kv_chunks, queries[0])

    left, right, far = (tp + 3) % 4, (tp + 1) % 4, (tp + 2) % 4
    pieces = (chunk, left_chunk, right_chunk, far_top, far_low)
    places = (2 * tp, 2 * left, 2 * right, 2 * far, 2 * far + 1)
    grad = grad_call(
        (jnp.stack(places) * half_rows).astype(jnp.int32), pieces, output_weight[0]
    )

    f32 = jnp.float32

    def along_z(groups):
        total = groups[0].astype(f32)
        for distance, shift in ((1, 1), (2, 2), (3, -1)):
            received = send(groups[distance], "ctx", z_ring(shift))
            total = total + received.astype(f32)
        return total

    groups, grad = lax.optimization_barrier((value_call(split, ids, grad, saved), grad))
    value_sum = along_z(groups)
    query_grad, *groups = key_call(split, ids, grad, saved, queries[0])
    key_sum = along_z(groups)
    for_pair = jnp.concatenate([key_sum[1], value_sum[1]], axis=1).astype(bf16)
    own_sum = jnp.concatenate([key_sum[0], value_sum[0]], axis=1)
    kv_grad = (own_sum + send(for_pair, "ctx", X_SWAP).astype(f32)).astype(bf16)

    stacked = jnp.concatenate([query_grad, kv_grad], axis=1)
    weights = jnp.concatenate([query_weight[0], key_weight[0], value_weight[0]], axis=1)

    def term_of(distance):
        start = ((tp + distance) % 4) * 128
        return dot_nt(lax.dynamic_slice_in_dim(stacked, start, 128, 0), weights).astype(bf16)

    far = term_of(2)
    from_left = send(far[:half_rows], "tp", ring(4, 1))
    from_right = send(far[half_rows:], "tp", ring(4, -1))
    own_term = term_of(0)
    own = send(own_term, "section", ring(4, -1))
    right, left = lax.optimization_barrier((term_of(1), term_of(3)))
    empty = jnp.zeros_like(from_left, dtype=f32)
    right = (right.astype(f32) + jnp.concatenate([from_left.astype(f32), empty])).astype(bf16)
    left = (left.astype(f32) + jnp.concatenate([empty, from_right.astype(f32)])).astype(bf16)
    joint = ("section", "tp")
    part_a = send(right, joint, joint_ring(1))
    part_b = send(left, joint, joint_ring(-1))
    sent = (own.astype(f32) + part_a.astype(f32) + part_b.astype(f32)).astype(bf16)
    return (sent[None], kv_grad[None, :, :HD], kv_grad[None, :, HD:])


def solution(mesh):
    placed = (
        P(),
        P("section", "ctx", "tp"),
        P("section", "ctx", "tp"),
        P("section", "ctx", "tp"),
        P("section", ("ctx", "tp"), None),
        P("section", None, "tp"),
        P("section", None, "tp"),
        P("section", None, "tp"),
        P("section", "tp", None),
    )

    return jax.shard_map(
        per_device,
        mesh=mesh,
        in_specs=placed,
        out_specs=(
            P("section", ("ctx", "tp"), None),
            P("section", "ctx", "tp"),
            P("section", "ctx", "tp"),
        ),
        check_vma=False,
    )
```

profile of v0, /device:TPU:1, one launch (start us, length us, event | category | flops | bytes accessed | tf_op | source)
XLA Modules:
  0.0 171.7 jit_solution(7738815662111172970)
XLA Ops:
  0.6 3.6 %collective-permute-start.1 = (bf16[128,4096]{1,0:T(8,128)(2,1)}, bf16[128,4096]{1,0:T(8,128)(2,1)S(1)}, u32[]{:S(2)}, u32[]{:S(2)}) collective-permute-start(bf16[128,4096]{1,0:T(8,128)(2,1)} %bitcast.29), channel_id=1, source_target_pairs={{0,3},{1,0},{2,1},{3,2},{4,7},{5,4},{6,5},{7,6},{8,11},{9,8},{10,9... | collective-permute-start | bytes 3145736 | tf_op jit(solution)/shard_map/ppermute | solution.py:417
  5.3 2.8 %collective-permute-start.4 = (bf16[512,256]{1,0:T(8,128)(2,1)S(1)}, bf16[512,256]{1,0:T(8,128)(2,1)}, u32[]{:S(2)}, u32[]{:S(2)}) collective-permute-start(bf16[512,256]{1,0:T(8,128)(2,1)S(1)} %pad_maximum_fusion.1.refs_0_), channel_id=1, source_target_pairs={{0,16},{4,20},{8,24},{12,28},{16,0},{20,4},{24,8},{28,12},{1,17},{... | collective-permute-start | bytes 786440 | tf_op jit(solution)/shard_map/ppermute | solution.py:412
  9.7 3.3 %collective-permute-start.7 = (bf16[512,256]{1,0:T(8,128)(2,1)S(1)}, bf16[512,256]{1,0:T(8,128)(2,1)}, u32[]{:S(2)}, u32[]{:S(2)}) collective-permute-start(bf16[512,256]{1,0:T(8,128)(2,1)S(1)} %pad_maximum_fusion.1.refs_0_), channel_id=1, source_target_pairs={{0,8},{4,12},{8,0},{12,4},{16,24},{20,28},{24,16},{28,20},{1,9},{5... | collective-permute-start | bytes 786440 | tf_op jit(solution)/shard_map/ppermute | solution.py:423
  13.9 3.8 %collective-permute-start.5 = (bf16[512,256]{1,0:T(8,128)(2,1)S(1)}, bf16[512,256]{1,0:T(8,128)(2,1)S(1)}, u32[]{:S(2)}, u32[]{:S(2)}) collective-permute-start(bf16[512,256]{1,0:T(8,128)(2,1)S(1)} %pad_maximum_fusion.1.refs_0_), channel_id=1, source_target_pairs={{0,12},{4,0},{8,4},{12,8},{16,28},{20,16},{24,20},{28,24},{1,13},{... | collective-permute-start | bytes 786440 | tf_op jit(solution)/shard_map/ppermute | solution.py:423
  17.7 8.7 %collective-permute-done.1.refs_2_ = bf16[128,4096]{1,0:T(8,128)(2,1)S(1)} collective-permute-done((bf16[128,4096]{1,0:T(8,128)(2,1)}, bf16[128,4096]{1,0:T(8,128)(2,1)S(1)}, u32[]{:S(2)}, u32[]{:S(2)}) %collective-permute-start.1) | collective-permute-done | bytes 1048608 | tf_op jit(solution)/shard_map/ppermute | solution.py:417
  29.4 3.6 %collective-permute-start.8 = (bf16[512,256]{1,0:T(8,128)(2,1)}, bf16[512,256]{1,0:T(8,128)(2,1)}, u32[]{:S(2)}, u32[]{:S(2)}) collective-permute-start(bf16[512,256]{1,0:T(8,128)(2,1)} %collective-permute-done.4.refs_1_), channel_id=1, source_target_pairs={{0,8},{4,12},{8,0},{12,4},{16,24},{20,28},{24,16},{28,20},{1,9},{5... | collective-permute-start | bytes 786440 | tf_op jit(solution)/shard_map/ppermute | solution.py:424
  34.3 2.7 %collective-permute-start.3 = (bf16[64,4096]{1,0:T(8,128)(2,1)}, bf16[64,4096]{1,0:T(8,128)(2,1)}, u32[]{:S(2)}, u32[]{:S(2)}) collective-permute-start(bf16[64,4096]{1,0:T(8,128)(2,1)} %slice.47), channel_id=1, source_target_pairs={{0,3},{1,0},{2,1},{3,2},{4,7},{5,4},{6,5},{7,6},{8,11},{9,8},{10,9... | collective-permute-start | bytes 1572872 | tf_op jit(solution)/shard_map/ppermute | solution.py:419
  38.9 3.3 %collective-permute-done.8.refs_5_ = bf16[512,256]{1,0:T(8,128)(2,1)} collective-permute-done((bf16[512,256]{1,0:T(8,128)(2,1)}, bf16[512,256]{1,0:T(8,128)(2,1)}, u32[]{:S(2)}, u32[]{:S(2)}) %collective-permute-start.8) | collective-permute-done | bytes 262176 | tf_op jit(solution)/shard_map/ppermute | solution.py:424
  42.2 3.3 %collective-permute-done.6.refs_3_ = bf16[512,256]{1,0:T(8,128)(2,1)} collective-permute-done((bf16[512,256]{1,0:T(8,128)(2,1)}, bf16[512,256]{1,0:T(8,128)(2,1)}, u32[]{:S(2)}, u32[]{:S(2)}) %collective-permute-start.6) | collective-permute-done | bytes 262176 | tf_op jit(solution)/shard_map/ppermute | solution.py:424
  47.5 11.0 %attn_forward.1 = (bf16[17,4,256,256]{3,2,1,0:T(8,128)(2,1)S(1)}, f32[2,128,1024]{2,1,0:T(8,128)S(1)}, f32[2,8,1024]{2,1,0:T(8,128)S(1)}, f32[17,1,1024]{2,1,0:T(1,128)S(1)}, bf16[16,256,256]{2,1,0:T(8,128)(2,1)S(1)}) custom-call(s32[1]{0:T(128)S(1)} %bitcast.34, s32[16]{0:T(128)S(1)} %reshape.80.ids_ref, bf16[512,256]{1,0:T(8,128)(2,1)S(1)} %pad_maximum_fusion.1.refs_0_, ...), custom_call_target="tpu_custom_call" | custom-call | flops 2281701376 | bytes 13631488 | tf_op jit(solution)/shard_map/attn_forward/pallas_call | solution.py:130
  58.5 6.9 %attn_grad.1.grad_ref = bf16[512,512]{1,0:T(8,128)(2,1)S(1)} custom-call(s32[5]{0:T(128)S(1)} %broadcast_multiply_fusion.rows_ref, bf16[128,4096]{1,0:T(8,128)(2,1)S(1)} %bitcast.31, bf16[128,4096]{1,0:T(8,128)(2,1)S(1)} %collective-permute-done.refs_1_, bf16[128,4096]{1,0:T(8,128)(2,1)S(1)} %collective-permute-done.1.refs_2_, ...), custom_call_target="tpu_custom_call" | custom-call | flops 2147483648 | bytes 9437184 | tf_op jit(solution)/shard_map/attn_grad/pallas_call | solution.py:194
  65.4 6.2 %attn_value_grad.1 = (bf16[2,512,128]{2,1,0:T(8,128)(2,1)S(1)}, bf16[2,512,128]{2,1,0:T(8,128)(2,1)S(1)}, bf16[2,512,128]{2,1,0:T(8,128)(2,1)S(1)}, bf16[2,512,128]{2,1,0:T(8,128)(2,1)S(1)}) custom-call(s32[1]{0:T(128)S(1)} %bitcast.35, s32[16]{0:T(128)S(1)} %reshape.80.ids_ref, bf16[512,512]{1,0:T(8,128)(2,1)S(1)} %attn_grad.1.grad_ref, ...), custom_call_target="tpu_custom_call" | custom-call | flops 1140850688 | bytes 11534336 | tf_op jit(solution)/shard_map/attn_value_grad/pallas_call | solution.py:260
  71.6 11.8 %attn_key_grad.1 = (bf16[512,512]{1,0:T(8,128)(2,1)S(1)}, bf16[2,512,128]{2,1,0:T(8,128)(2,1)S(1)}, bf16[2,512,128]{2,1,0:T(8,128)(2,1)S(1)}, bf16[2,512,128]{2,1,0:T(8,128)(2,1)S(1)}, bf16[2,512,128]{2,1,0:T(8,128)(2,1)S(1)}) custom-call(s32[1]{0:T(128)S(1)} %bitcast.36, s32[16]{0:T(128)S(1)} %reshape.80.ids_ref, bf16[512,512]{1,0:T(8,128)(2,1)S(1)} %attn_grad.1.grad_ref, ...), custom_call_target="tpu_custom_call" | custom-call | flops 3422552064 | bytes 14680064 | tf_op jit(solution)/shard_map/attn_key_grad/pallas_call | solution.py:359
  84.2 3.8 %collective-permute-start.12 = (bf16[2,512,128]{2,1,0:T(8,128)(2,1)S(1)}, bf16[2,512,128]{2,1,0:T(8,128)(2,1)S(1)}, u32[]{:S(2)}, u32[]{:S(2)}) collective-permute-start(bf16[2,512,128]{2,1,0:T(8,128)(2,1)S(1)} %get-tuple-element.37), channel_id=1, source_target_pairs={{0,8},{4,12},{8,0},{12,4},{16,24},{20,28},{24,16},{28,20},{1,9},{5... | collective-permute-start | bytes 786440 | tf_op jit(solution)/shard_map/ppermute | solution.py:447
  89.5 2.9 %collective-permute-done.11 = bf16[2,512,128]{2,1,0:T(8,128)(2,1)S(1)} collective-permute-done((bf16[2,512,128]{2,1,0:T(8,128)(2,1)S(1)}, bf16[2,512,128]{2,1,0:T(8,128)(2,1)S(1)}, u32[]{:S(2)}, u32[]{:S(2)}) %collective-permute-start.11) | collective-permute-done | bytes 262176 | tf_op jit(solution)/shard_map/ppermute | solution.py:447
  92.4 1.8 %collective-permute-start.16 = (bf16[2,512,128]{2,1,0:T(8,128)(2,1)S(1)}, bf16[2,512,128]{2,1,0:T(8,128)(2,1)S(1)}, u32[]{:S(2)}, u32[]{:S(2)}) collective-permute-start(bf16[2,512,128]{2,1,0:T(8,128)(2,1)S(1)} %get-tuple-element.42), channel_id=1, source_target_pairs={{0,12},{4,0},{8,4},{12,8},{16,28},{20,16},{24,20},{28,24},{1,13},{... | collective-permute-start | bytes 786440 | tf_op jit(solution)/shard_map/ppermute | solution.py:447
  94.2 5.4 %collective-permute-done.12 = bf16[2,512,128]{2,1,0:T(8,128)(2,1)S(1)} collective-permute-done((bf16[2,512,128]{2,1,0:T(8,128)(2,1)S(1)}, bf16[2,512,128]{2,1,0:T(8,128)(2,1)S(1)}, u32[]{:S(2)}, u32[]{:S(2)}) %collective-permute-start.12) | collective-permute-done | bytes 262176 | tf_op jit(solution)/shard_map/ppermute | solution.py:447
  99.9 3.8 %collective-permute-done.14 = bf16[2,512,128]{2,1,0:T(8,128)(2,1)S(1)} collective-permute-done((bf16[2,512,128]{2,1,0:T(8,128)(2,1)S(1)}, bf16[2,512,128]{2,1,0:T(8,128)(2,1)S(1)}, u32[]{:S(2)}, u32[]{:S(2)}) %collective-permute-start.14) | collective-permute-done | bytes 262176 | tf_op jit(solution)/shard_map/ppermute | solution.py:447
  103.7 7.2 %collective-permute-done.15 = bf16[2,512,128]{2,1,0:T(8,128)(2,1)S(1)} collective-permute-done((bf16[2,512,128]{2,1,0:T(8,128)(2,1)S(1)}, bf16[2,512,128]{2,1,0:T(8,128)(2,1)S(1)}, u32[]{:S(2)}, u32[]{:S(2)}) %collective-permute-start.15) | collective-permute-done | bytes 262176 | tf_op jit(solution)/shard_map/ppermute | solution.py:447
  111.0 3.1 %collective-permute-start.17 = (bf16[512,256]{1,0:T(8,128)(2,1)S(1)}, bf16[512,256]{1,0:T(8,128)(2,1)S(1)}, u32[]{:S(2)}, u32[]{:S(2)}) collective-permute-start(bf16[512,256]{1,0:T(8,128)(2,1)S(1)} %pad_maximum_fusion.2), channel_id=1, source_target_pairs={{0,16},{4,20},{8,24},{12,28},{16,0},{20,4},{24,8},{28,12},{1,17},{... | collective-permute-start | bytes 786440 | tf_op jit(solution)/shard_map/ppermute | solution.py:457
  114.1 5.2 %collective-permute-done.17 = bf16[512,256]{1,0:T(8,128)(2,1)S(1)} collective-permute-done((bf16[512,256]{1,0:T(8,128)(2,1)S(1)}, bf16[512,256]{1,0:T(8,128)(2,1)S(1)}, u32[]{:S(2)}, u32[]{:S(2)}) %collective-permute-start.17) | collective-permute-done | bytes 262176 | tf_op jit(solution)/shard_map/ppermute | solution.py:457
  119.4 2.3 %convolution_convert_fusion.2 = bf16[128,4096]{1,0:T(8,128)(2,1)S(1)} fusion(s32[]{:T(128)S(6)} %select_n.96, bf16[512,512]{1,0:T(8,128)(2,1)S(1)} %get-tuple-element.34, bf16[512,256]{1,0:T(8,128)(2,1)S(1)} %fusion.1, bf16[4096,128]{1,0:T(8,128)(2,1)S(1)} %bitcast.43, bf16[4096,128]{1,0:T(8,128)(2,1)S(1)} %bitcast.47, bf16[4096,512]{1,0:T(8,128)(2,1)S(1)} %bitcast.39), kind=kOutput, calls=%fused_computation.3 | convolution fusion | flops 825098240 | bytes 8126468 | tf_op jit(solution)/shard_map/dot_general | solution.py:21
  121.7 2.3 %convolution_convert_fusion = bf16[128,4096]{1,0:T(8,128)(2,1)S(1)} fusion(s32[]{:T(128)S(6)} %select_n.98, bf16[512,512]{1,0:T(8,128)(2,1)S(1)} %get-tuple-element.34, bf16[512,256]{1,0:T(8,128)(2,1)S(1)} %fusion.1, bf16[4096,128]{1,0:T(8,128)(2,1)S(1)} %bitcast.44, bf16[4096,128]{1,0:T(8,128)(2,1)S(1)} %bitcast.48, bf16[4096,512]{1,0:T(8,128)(2,1)S(1)} %bitcast.40), kind=kOutput, calls=%fused_computation.1 | convolution fusion | flops 825098240 | bytes 8126468 | tf_op jit(solution)/shard_map/dot_general | solution.py:21
  124.2 2.3 %convolution_convert_fusion.1 = bf16[128,4096]{1,0:T(8,128)(2,1)S(1)} fusion(s32[]{:T(128)S(6)} %select_n.97, bf16[512,512]{1,0:T(8,128)(2,1)S(1)} %get-tuple-element.34, bf16[512,256]{1,0:T(8,128)(2,1)S(1)} %fusion.1, bf16[4096,128]{1,0:T(8,128)(2,1)S(1)} %bitcast.45, bf16[4096,128]{1,0:T(8,128)(2,1)S(1)} %bitcast.49, bf16[4096,512]{1,0:T(8,128)(2,1)S(1)} %bitcast.41), kind=kOutput, calls=%fused_computation.2 | convolution fusion | flops 825098240 | bytes 8126468 | tf_op jit(solution)/shard_map/dot_general | solution.py:21
  128.1 2.3 %convolution_convert_fusion.3 = bf16[128,4096]{1,0:T(8,128)(2,1)S(1)} fusion(s32[]{:T(128)S(6)} %select_n.95, bf16[512,512]{1,0:T(8,128)(2,1)S(1)} %get-tuple-element.34, bf16[512,256]{1,0:T(8,128)(2,1)S(1)} %fusion.1, bf16[4096,128]{1,0:T(8,128)(2,1)S(1)} %bitcast.46, bf16[4096,128]{1,0:T(8,128)(2,1)S(1)} %bitcast.50, bf16[4096,512]{1,0:T(8,128)(2,1)S(1)} %bitcast.42), kind=kOutput, calls=%fused_computation.4 | convolution fusion | flops 825098240 | bytes 8126468 | tf_op jit(solution)/shard_map/dot_general | solution.py:21
  130.4 2.9 %collective-permute-start.18 = (bf16[128,4096]{1,0:T(8,128)(2,1)S(1)}, bf16[128,4096]{1,0:T(8,128)(2,1)S(1)}, u32[]{:S(2)}, u32[]{:S(2)}) collective-permute-start(bf16[128,4096]{1,0:T(8,128)(2,1)S(1)} %convolution_convert_fusion.3), channel_id=1, source_target_pairs={{0,96},{32,0},{64,32},{96,64},{1,97},{33,1},{65,33},{97,65},{2,98}... | collective-permute-start | bytes 3145736 | tf_op jit(solution)/shard_map/ppermute | solution.py:470
  133.2 2.2 %collective-permute-done.21 = bf16[64,4096]{1,0:T(8,128)(2,1)S(1)} collective-permute-done((bf16[64,4096]{1,0:T(8,128)(2,1)S(1)}, bf16[64,4096]{1,0:T(8,128)(2,1)S(1)}, u32[]{:S(2)}, u32[]{:S(2)}) %collective-permute-start.21) | collective-permute-done | bytes 524320 | tf_op jit(solution)/shard_map/ppermute | solution.py:468
  135.6 4.3 %collective-permute-start.22 = (bf16[128,4096]{1,0:T(8,128)(2,1)S(1)}, bf16[128,4096]{1,0:T(8,128)(2,1)S(1)}, u32[]{:S(2)}, u32[]{:S(2)}) collective-permute-start(bf16[128,4096]{1,0:T(8,128)(2,1)S(1)} %add_convert_fusion.1), channel_id=1, source_target_pairs={{0,99},{1,96},{2,97},{3,98},{32,3},{33,0},{34,1},{35,2},{64,35},{6... | collective-permute-start | bytes 3145736 | tf_op jit(solution)/shard_map/ppermute | solution.py:477
  140.0 2.4 %collective-permute-start.20 = (bf16[128,4096]{1,0:T(8,128)(2,1)S(1)}, bf16[128,4096]{1,0:T(8,128)(2,1)S(1)}, u32[]{:S(2)}, u32[]{:S(2)}) collective-permute-start(bf16[128,4096]{1,0:T(8,128)(2,1)S(1)} %add_convert_fusion.2), channel_id=1, source_target_pairs={{0,97},{1,98},{2,99},{3,96},{32,1},{33,2},{34,3},{35,0},{64,33},{6... | collective-permute-start | bytes 3145736 | tf_op jit(solution)/shard_map/ppermute | solution.py:476
  143.2 3.9 %collective-permute-done.18 = bf16[128,4096]{1,0:T(8,128)(2,1)S(1)} collective-permute-done((bf16[128,4096]{1,0:T(8,128)(2,1)S(1)}, bf16[128,4096]{1,0:T(8,128)(2,1)S(1)}, u32[]{:S(2)}, u32[]{:S(2)}) %collective-permute-start.18) | collective-permute-done | bytes 1048608 | tf_op jit(solution)/shard_map/ppermute | solution.py:470
  147.1 15.8 %collective-permute-done.22 = bf16[128,4096]{1,0:T(8,128)(2,1)S(1)} collective-permute-done((bf16[128,4096]{1,0:T(8,128)(2,1)S(1)}, bf16[128,4096]{1,0:T(8,128)(2,1)S(1)}, u32[]{:S(2)}, u32[]{:S(2)}) %collective-permute-start.22) | collective-permute-done | bytes 1048608 | tf_op jit(solution)/shard_map/ppermute | solution.py:477
  162.9 7.3 %collective-permute-done.20 = bf16[128,4096]{1,0:T(8,128)(2,1)S(1)} collective-permute-done((bf16[128,4096]{1,0:T(8,128)(2,1)S(1)}, bf16[128,4096]{1,0:T(8,128)(2,1)S(1)}, u32[]{:S(2)}, u32[]{:S(2)}) %collective-permute-start.20) | collective-permute-done | bytes 1048608 | tf_op jit(solution)/shard_map/ppermute | solution.py:476
  (61 shorter events, 18.6 us)
Async XLA Ops:
  0.6 57.9 %copy-start.1 = (bf16[1,128,4096]{2,1,0:T(8,128)(2,1)S(1)}, bf16[1,128,4096]{2,1,0:T(8,128)(2,1)}, u32[]{:S(2)}) copy-start(bf16[1,128,4096]{2,1,0:T(8,128)(2,1)} %param.13) | copy-start | bytes 3145732
  0.6 25.8 %collective-permute-start.1 = (bf16[128,4096]{1,0:T(8,128)(2,1)}, bf16[128,4096]{1,0:T(8,128)(2,1)S(1)}, u32[]{:S(2)}, u32[]{:S(2)}) collective-permute-start(bf16[128,4096]{1,0:T(8,128)(2,1)} %bitcast.29), channel_id=1, source_target_pairs={{0,3},{1,0},{2,1},{3,2},{4,7},{5,4},{6,5},{7,6},{8,11},{9,8},{10,9... | collective-permute-start | bytes 3145736 | tf_op jit(solution)/shard_map/ppermute | solution.py:417
  4.3 25.2 %collective-permute-start = (bf16[128,4096]{1,0:T(8,128)(2,1)}, bf16[128,4096]{1,0:T(8,128)(2,1)S(1)}, u32[]{:S(2)}, u32[]{:S(2)}) collective-permute-start(bf16[128,4096]{1,0:T(8,128)(2,1)} %bitcast.30), channel_id=1, source_target_pairs={{0,1},{1,2},{2,3},{3,0},{4,5},{5,6},{6,7},{7,4},{8,9},{9,10},{10,1... | collective-permute-start | bytes 3145736 | tf_op jit(solution)/shard_map/ppermute | solution.py:416
  5.3 8.6 %collective-permute-start.4 = (bf16[512,256]{1,0:T(8,128)(2,1)S(1)}, bf16[512,256]{1,0:T(8,128)(2,1)}, u32[]{:S(2)}, u32[]{:S(2)}) collective-permute-start(bf16[512,256]{1,0:T(8,128)(2,1)S(1)} %pad_maximum_fusion.1.refs_0_), channel_id=1, source_target_pairs={{0,16},{4,20},{8,24},{12,28},{16,0},{20,4},{24,8},{28,12},{1,17},{... | collective-permute-start | bytes 786440 | tf_op jit(solution)/shard_map/ppermute | solution.py:412
  8.1 25.8 %collective-permute-start.9 = (bf16[512,256]{1,0:T(8,128)(2,1)S(1)}, bf16[512,256]{1,0:T(8,128)(2,1)}, u32[]{:S(2)}, u32[]{:S(2)}) collective-permute-start(bf16[512,256]{1,0:T(8,128)(2,1)S(1)} %pad_maximum_fusion.1.refs_0_), channel_id=1, source_target_pairs={{0,4},{4,8},{8,12},{12,0},{16,20},{20,24},{24,28},{28,16},{1,5},{5... | collective-permute-start | bytes 786440 | tf_op jit(solution)/shard_map/ppermute | solution.py:423
  9.7 24.6 %collective-permute-start.7 = (bf16[512,256]{1,0:T(8,128)(2,1)S(1)}, bf16[512,256]{1,0:T(8,128)(2,1)}, u32[]{:S(2)}, u32[]{:S(2)}) collective-permute-start(bf16[512,256]{1,0:T(8,128)(2,1)S(1)} %pad_maximum_fusion.1.refs_0_), channel_id=1, source_target_pairs={{0,8},{4,12},{8,0},{12,4},{16,24},{20,28},{24,16},{28,20},{1,9},{5... | collective-permute-start | bytes 786440 | tf_op jit(solution)/shard_map/ppermute | solution.py:423
  13.9 23.2 %collective-permute-start.5 = (bf16[512,256]{1,0:T(8,128)(2,1)S(1)}, bf16[512,256]{1,0:T(8,128)(2,1)S(1)}, u32[]{:S(2)}, u32[]{:S(2)}) collective-permute-start(bf16[512,256]{1,0:T(8,128)(2,1)S(1)} %pad_maximum_fusion.1.refs_0_), channel_id=1, source_target_pairs={{0,12},{4,0},{8,4},{12,8},{16,28},{20,16},{24,20},{28,24},{1,13},{... | collective-permute-start | bytes 786440 | tf_op jit(solution)/shard_map/ppermute | solution.py:423
  26.4 12.4 %collective-permute-start.10 = (bf16[512,256]{1,0:T(8,128)(2,1)}, bf16[512,256]{1,0:T(8,128)(2,1)}, u32[]{:S(2)}, u32[]{:S(2)}) collective-permute-start(bf16[512,256]{1,0:T(8,128)(2,1)} %collective-permute-done.4.refs_1_), channel_id=1, source_target_pairs={{0,4},{4,8},{8,12},{12,0},{16,20},{20,24},{24,28},{28,16},{1,5},{5... | collective-permute-start | bytes 786440 | tf_op jit(solution)/shard_map/ppermute | solution.py:424
  29.4 12.7 %collective-permute-start.8 = (bf16[512,256]{1,0:T(8,128)(2,1)}, bf16[512,256]{1,0:T(8,128)(2,1)}, u32[]{:S(2)}, u32[]{:S(2)}) collective-permute-start(bf16[512,256]{1,0:T(8,128)(2,1)} %collective-permute-done.4.refs_1_), channel_id=1, source_target_pairs={{0,8},{4,12},{8,0},{12,4},{16,24},{20,28},{24,16},{28,20},{1,9},{5... | collective-permute-start | bytes 786440 | tf_op jit(solution)/shard_map/ppermute | solution.py:424
  33.9 11.6 %collective-permute-start.6 = (bf16[512,256]{1,0:T(8,128)(2,1)}, bf16[512,256]{1,0:T(8,128)(2,1)}, u32[]{:S(2)}, u32[]{:S(2)}) collective-permute-start(bf16[512,256]{1,0:T(8,128)(2,1)} %collective-permute-done.4.refs_1_), channel_id=1, source_target_pairs={{0,12},{4,0},{8,4},{12,8},{16,28},{20,16},{24,20},{28,24},{1,13},{... | collective-permute-start | bytes 786440 | tf_op jit(solution)/shard_map/ppermute | solution.py:424
  34.3 24.2 %collective-permute-start.3 = (bf16[64,4096]{1,0:T(8,128)(2,1)}, bf16[64,4096]{1,0:T(8,128)(2,1)}, u32[]{:S(2)}, u32[]{:S(2)}) collective-permute-start(bf16[64,4096]{1,0:T(8,128)(2,1)} %slice.47), channel_id=1, source_target_pairs={{0,3},{1,0},{2,1},{3,2},{4,7},{5,4},{6,5},{7,6},{8,11},{9,8},{10,9... | collective-permute-start | bytes 1572872 | tf_op jit(solution)/shard_map/ppermute | solution.py:419
  37.1 0.7 copy-start.3
  37.8 20.8 %collective-permute-start.2 = (bf16[64,4096]{1,0:T(8,128)(2,1)}, bf16[64,4096]{1,0:T(8,128)(2,1)}, u32[]{:S(2)}, u32[]{:S(2)}) collective-permute-start(bf16[64,4096]{1,0:T(8,128)(2,1)} %slice.46), channel_id=1, source_target_pairs={{0,1},{1,2},{2,3},{3,0},{4,5},{5,6},{6,7},{7,4},{8,9},{9,10},{10,1... | collective-permute-start | bytes 1572872 | tf_op jit(solution)/shard_map/ppermute | solution.py:418
  38.9 19.7 %copy-start = (bf16[1,512,4096]{2,1,0:T(8,128)(2,1)S(1)}, bf16[1,512,4096]{2,1,0:T(8,128)(2,1)}, u32[]{:S(2)}) copy-start(bf16[1,512,4096]{2,1,0:T(8,128)(2,1)} %param.17) | copy-start | bytes 12582916
  45.5 1.0 copy-start.2
  46.5 0.9 copy-start.4
  83.4 9.0 %collective-permute-start.11 = (bf16[2,512,128]{2,1,0:T(8,128)(2,1)S(1)}, bf16[2,512,128]{2,1,0:T(8,128)(2,1)S(1)}, u32[]{:S(2)}, u32[]{:S(2)}) collective-permute-start(bf16[2,512,128]{2,1,0:T(8,128)(2,1)S(1)} %get-tuple-element.36), channel_id=1, source_target_pairs={{0,4},{4,8},{8,12},{12,0},{16,20},{20,24},{24,28},{28,16},{1,5},{5... | collective-permute-start | bytes 786440 | tf_op jit(solution)/shard_map/ppermute | solution.py:447
  84.2 15.4 %collective-permute-start.12 = (bf16[2,512,128]{2,1,0:T(8,128)(2,1)S(1)}, bf16[2,512,128]{2,1,0:T(8,128)(2,1)S(1)}, u32[]{:S(2)}, u32[]{:S(2)}) collective-permute-start(bf16[2,512,128]{2,1,0:T(8,128)(2,1)S(1)} %get-tuple-element.37), channel_id=1, source_target_pairs={{0,8},{4,12},{8,0},{12,4},{16,24},{20,28},{24,16},{28,20},{1,9},{5... | collective-permute-start | bytes 786440 | tf_op jit(solution)/shard_map/ppermute | solution.py:447
  88.1 11.7 %collective-permute-start.13 = (bf16[2,512,128]{2,1,0:T(8,128)(2,1)S(1)}, bf16[2,512,128]{2,1,0:T(8,128)(2,1)S(1)}, u32[]{:S(2)}, u32[]{:S(2)}) collective-permute-start(bf16[2,512,128]{2,1,0:T(8,128)(2,1)S(1)} %get-tuple-element.38), channel_id=1, source_target_pairs={{0,12},{4,0},{8,4},{12,8},{16,28},{20,16},{24,20},{28,24},{1,13},{... | collective-permute-start | bytes 786440 | tf_op jit(solution)/shard_map/ppermute | solution.py:447
  88.1 31.3 %copy-start.5 = (bf16[1,4096,512]{2,1,0:T(8,128)(2,1)S(1)}, bf16[1,4096,512]{2,1,0:T(8,128)(2,1)}, u32[]{:S(2)}) copy-start(bf16[1,4096,512]{2,1,0:T(8,128)(2,1)} %param.14) | copy-start | bytes 12582916
  88.1 31.3 %copy-start.6 = (bf16[1,4096,128]{2,1,0:T(8,128)(2,1)S(1)}, bf16[1,4096,128]{2,1,0:T(8,128)(2,1)}, u32[]{:S(2)}) copy-start(bf16[1,4096,128]{2,1,0:T(8,128)(2,1)} %param.16) | copy-start | bytes 3145732
  88.1 31.3 %copy-start.7 = (bf16[1,4096,128]{2,1,0:T(8,128)(2,1)S(1)}, bf16[1,4096,128]{2,1,0:T(8,128)(2,1)}, u32[]{:S(2)}) copy-start(bf16[1,4096,128]{2,1,0:T(8,128)(2,1)} %param.15) | copy-start | bytes 3145732
  88.1 15.6 %collective-permute-start.14 = (bf16[2,512,128]{2,1,0:T(8,128)(2,1)S(1)}, bf16[2,512,128]{2,1,0:T(8,128)(2,1)S(1)}, u32[]{:S(2)}, u32[]{:S(2)}) collective-permute-start(bf16[2,512,128]{2,1,0:T(8,128)(2,1)S(1)} %get-tuple-element.40), channel_id=1, source_target_pairs={{0,4},{4,8},{8,12},{12,0},{16,20},{20,24},{24,28},{28,16},{1,5},{5... | collective-permute-start | bytes 786440 | tf_op jit(solution)/shard_map/ppermute | solution.py:447
  89.5 21.3 %collective-permute-start.15 = (bf16[2,512,128]{2,1,0:T(8,128)(2,1)S(1)}, bf16[2,512,128]{2,1,0:T(8,128)(2,1)S(1)}, u32[]{:S(2)}, u32[]{:S(2)}) collective-permute-start(bf16[2,512,128]{2,1,0:T(8,128)(2,1)S(1)} %get-tuple-element.41), channel_id=1, source_target_pairs={{0,8},{4,12},{8,0},{12,4},{16,24},{20,28},{24,16},{28,20},{1,9},{5... | collective-permute-start | bytes 786440 | tf_op jit(solution)/shard_map/ppermute | solution.py:447
  92.4 18.4 %collective-permute-start.16 = (bf16[2,512,128]{2,1,0:T(8,128)(2,1)S(1)}, bf16[2,512,128]{2,1,0:T(8,128)(2,1)S(1)}, u32[]{:S(2)}, u32[]{:S(2)}) collective-permute-start(bf16[2,512,128]{2,1,0:T(8,128)(2,1)S(1)} %get-tuple-element.42), channel_id=1, source_target_pairs={{0,12},{4,0},{8,4},{12,8},{16,28},{20,16},{24,20},{28,24},{1,13},{... | collective-permute-start | bytes 786440 | tf_op jit(solution)/shard_map/ppermute | solution.py:447
  111.0 8.3 %collective-permute-start.17 = (bf16[512,256]{1,0:T(8,128)(2,1)S(1)}, bf16[512,256]{1,0:T(8,128)(2,1)S(1)}, u32[]{:S(2)}, u32[]{:S(2)}) collective-permute-start(bf16[512,256]{1,0:T(8,128)(2,1)S(1)} %pad_maximum_fusion.2), channel_id=1, source_target_pairs={{0,16},{4,20},{8,24},{12,28},{16,0},{20,4},{24,8},{28,12},{1,17},{... | collective-permute-start | bytes 786440 | tf_op jit(solution)/shard_map/ppermute | solution.py:457
  124.1 11.3 %collective-permute-start.21 = (bf16[64,4096]{1,0:T(8,128)(2,1)S(1)}, bf16[64,4096]{1,0:T(8,128)(2,1)S(1)}, u32[]{:S(2)}, u32[]{:S(2)}) collective-permute-start(bf16[64,4096]{1,0:T(8,128)(2,1)S(1)} %get-tuple-element.46), channel_id=1, source_target_pairs={{0,3},{1,0},{2,1},{3,2},{4,7},{5,4},{6,5},{7,6},{8,11},{9,8},{10,9... | collective-permute-start | bytes 1572872 | tf_op jit(solution)/shard_map/ppermute | solution.py:468
  126.6 13.3 %collective-permute-start.19 = (bf16[64,4096]{1,0:T(8,128)(2,1)S(1)}, bf16[64,4096]{1,0:T(8,128)(2,1)S(1)}, u32[]{:S(2)}, u32[]{:S(2)}) collective-permute-start(bf16[64,4096]{1,0:T(8,128)(2,1)S(1)} %get-tuple-element.45), channel_id=1, source_target_pairs={{0,1},{1,2},{2,3},{3,0},{4,5},{5,6},{6,7},{7,4},{8,9},{9,10},{10,1... | collective-permute-start | bytes 1572872 | tf_op jit(solution)/shard_map/ppermute | solution.py:467
  130.4 16.7 %collective-permute-start.18 = (bf16[128,4096]{1,0:T(8,128)(2,1)S(1)}, bf16[128,4096]{1,0:T(8,128)(2,1)S(1)}, u32[]{:S(2)}, u32[]{:S(2)}) collective-permute-start(bf16[128,4096]{1,0:T(8,128)(2,1)S(1)} %convolution_convert_fusion.3), channel_id=1, source_target_pairs={{0,96},{32,0},{64,32},{96,64},{1,97},{33,1},{65,33},{97,65},{2,98}... | collective-permute-start | bytes 3145736 | tf_op jit(solution)/shard_map/ppermute | solution.py:470
  135.6 27.2 %collective-permute-start.22 = (bf16[128,4096]{1,0:T(8,128)(2,1)S(1)}, bf16[128,4096]{1,0:T(8,128)(2,1)S(1)}, u32[]{:S(2)}, u32[]{:S(2)}) collective-permute-start(bf16[128,4096]{1,0:T(8,128)(2,1)S(1)} %add_convert_fusion.1), channel_id=1, source_target_pairs={{0,99},{1,96},{2,97},{3,98},{32,3},{33,0},{34,1},{35,2},{64,35},{6... | collective-permute-start | bytes 3145736 | tf_op jit(solution)/shard_map/ppermute | solution.py:477
  140.0 30.2 %collective-permute-start.20 = (bf16[128,4096]{1,0:T(8,128)(2,1)S(1)}, bf16[128,4096]{1,0:T(8,128)(2,1)S(1)}, u32[]{:S(2)}, u32[]{:S(2)}) collective-permute-start(bf16[128,4096]{1,0:T(8,128)(2,1)S(1)} %add_convert_fusion.2), channel_id=1, source_target_pairs={{0,97},{1,98},{2,99},{3,96},{32,1},{33,2},{34,3},{35,0},{64,33},{6... | collective-permute-start | bytes 3145736 | tf_op jit(solution)/shard_map/ppermute | solution.py:476
where the time goes:
time: 172 us
  waiting for transfers between devices  70.5 us (41%)
  starting transfers between devices  45.6 us (27%)
  Pallas kernels  35.9 us (21%)
  matrix products  9.29 us (5%)
  local copies, waits for them, and re-layouts  5.47 us (3%)
  other arithmetic  3.99 us (2%)
    ppermute x6, waiting for transfers between devices, along_z(): received = send(groups[distance], 'ctx', z_ring(shift))  19.4 us
    ppermute x1, waiting for transfers between devices, per_device(): part_b = send(left, joint, joint_ring(-1))  15.8 us
    pallas_call x1, Pallas kernels, key_call(): pl.pallas_call(key_kernel, grid_spec=pltpu.PrefetchScalarGridSpec(num_sca...  11.8 us
    pallas_call x1, Pallas kernels, forward_call(): pl.pallas_call(forward_kernel, grid_spec=pltpu.PrefetchScalarGridSpec(num...  11 us
    dot_general x4, matrix products, dot_nt(): lax.dot_general(lhs, rhs, (((1,), (1,)), ((), ())), preferred_element_typ...  9.29 us
    ppermute x1, waiting for transfers between devices, per_device(): right_chunk = send(chunk, 'tp', ring(4, -1))  8.71 us
    ppermute x3, starting transfers between devices, per_device(): kv_chunks.append(send(kv_own, 'ctx', z_ring(shift)))  8.7 us
    ppermute x6, starting transfers between devices, along_z(): received = send(groups[distance], 'ctx', z_ring(shift))  7.91 us
  transfers between devices with their start and end apart: 23, of which 15 were waited for; matrix products, arithmetic and copies ran while one was open for 6% of the time, Pallas kernels for 6%

commit v1 on v0

--- a/solution.py
+++ b/solution.py
@@ -168,8 +168,8 @@
 
 
 def grad_kernel(rows_ref, *refs):
-    pieces = refs[:5]
-    weight_ref, out_ref, lhs_ref, acc_ref = refs[5:]
+    pieces = refs[:7]
+    weight_ref, out_ref, lhs_ref, acc_ref = refs[7:]
     step = pl.program_id(0)
     depth = lhs_ref.shape[1]
 
@@ -408,16 +408,18 @@
     own_x, own_z = ctx // 4, ctx % 4
     bf16 = jnp.bfloat16
 
+    chunk = out_grad[0]
+    half_rows = chunk.shape[0] // 2
+    top, low = chunk[:half_rows], chunk[half_rows:]
+    left_top = send(top, "tp", ring(4, 1))
+    right_low = send(low, "tp", ring(4, -1))
+    far_top = send(left_top, "tp", ring(4, 1))
+    far_low = send(right_low, "tp", ring(4, -1))
+    left_low = send(low, "tp", ring(4, 1))
+    right_top = send(top, "tp", ring(4, -1))
+
     kv_own = jnp.concatenate([key_rows[0], value_rows[0]], axis=1)
     kv_pair = send(kv_own, "ctx", X_SWAP)
-
-    chunk = out_grad[0]
-    half_rows = chunk.shape[0] // 2
-    left_chunk = send(chunk, "tp", ring(4, 1))
-    right_chunk = send(chunk, "tp", ring(4, -1))
-    far_top = send(left_chunk[:half_rows], "tp", ring(4, 1))
-    far_low = send(right_chunk[half_rows:], "tp", ring(4, -1))
-
     kv_chunks = [kv_own, kv_pair]
     for shift in (-1, 2, 1):
         kv_chunks.append(send(kv_own, "ctx", z_ring(shift)))
@@ -433,8 +435,8 @@
     saved = forward_call(split, ids, kv_chunks, queries[0])
 
     left, right, far = (tp + 3) % 4, (tp + 1) % 4, (tp + 2) % 4
-    pieces = (chunk, left_chunk, right_chunk, far_top, far_low)
-    places = (2 * tp, 2 * left, 2 * right, 2 * far, 2 * far + 1)
+    pieces = (chunk, left_top, left_low, right_top, right_low, far_top, far_low)
+    places = (2 * tp, 2 * left, 2 * left + 1, 2 * right, 2 * right + 1, 2 * far, 2 * far + 1)
     grad = grad_call(
         (jnp.stack(places) * half_rows).astype(jnp.int32), pieces, output_weight[0]
     )
@@ -452,16 +454,21 @@
     value_sum = along_z(groups)
     query_grad, *groups = key_call(split, ids, grad, saved, queries[0])
     key_sum = along_z(groups)
-    for_pair = jnp.concatenate([key_sum[1], value_sum[1]], axis=1).astype(bf16)
-    own_sum = jnp.concatenate([key_sum[0], value_sum[0]], axis=1)
-    kv_grad = (own_sum + send(for_pair, "ctx", X_SWAP).astype(f32)).astype(bf16)
-
-    stacked = jnp.concatenate([query_grad, kv_grad], axis=1)
+
+    def with_pair(total):
+        received = send(total[1].astype(bf16), "ctx", X_SWAP)
+        return (total[0] + received.astype(f32)).astype(bf16)
+
+    value_grad = with_pair(value_sum)
+    key_grad = with_pair(key_sum)
+
+    stacked = jnp.concatenate([query_grad, key_grad, value_grad], axis=1)
     weights = jnp.concatenate([query_weight[0], key_weight[0], value_weight[0]], axis=1)
 
     def term_of(distance):
         start = ((tp + distance) % 4) * 128
-        return dot_nt(lax.dynamic_slice_in_dim(stacked, start, 128, 0), weights).astype(bf16)
+        rows = lax.dynamic_slice_in_dim(stacked, start, 128, 0)
+        return dot_nt(rows, weights).astype(bf16)
 
     far = term_of(2)
     from_left = send(far[:half_rows], "tp", ring(4, 1))
@@ -476,7 +483,7 @@
     part_a = send(right, joint, joint_ring(1))
     part_b = send(left, joint, joint_ring(-1))
     sent = (own.astype(f32) + part_a.astype(f32) + part_b.astype(f32)).astype(bf16)
-    return (sent[None], kv_grad[None, :, :HD], kv_grad[None, :, HD:])
+    return (sent[None], key_grad[None], value_grad[None])
 
 
 def solution(mesh):

time: 172 us -> 161 us (0.936)
  waiting for transfers between devices: 70.5 us -> 55.8 us
  local copies, waits for them, and re-layouts: 5.47 us -> 12.4 us
  starting transfers between devices: 45.6 us -> 42.7 us
    ppermute x5 -> x8, waiting for transfers between devices: 14.4 us -> 5.04 us  [the longest x2 5.02 us: with_pair(): received = send(total[1].astype(bf16), 'ctx', X_SWAP)]
    ppermute x6, waiting for transfers between devices: 19.4 us -> 11.2 us  [along_z(): received = send(groups[distance], 'ctx', z_ring(shift))]
    unnamed x16 -> x38, local copies, waits for them, and re-layouts: 2.7 us -> 9.75 us
    ppermute x3, waiting for transfers between devices: 0.01 us -> 4.48 us  [per_device(): kv_chunks.append(send(kv_own, 'ctx', z_ring(shift)))]
    ppermute x3, starting transfers between devices: 8.7 us -> 4.46 us  [per_device(): kv_chunks.append(send(kv_own, 'ctx', z_ring(shift)))]
    ppermute x1, starting transfers between devices: 4.26 us -> 6.56 us  [per_device(): part_b = send(left, joint, joint_ring(-1))]
    ppermute x1, waiting for transfers between devices: 2.24 us -> 0.01 us  [per_device(): from_right = send(far[half_rows:], 'tp', ring(4, -1))]
    ppermute x5 -> x8, starting transfers between devices: 9.43 us -> 9.07 us  [the longest x1 1.44 us: per_device(): right_top = send(top, 'tp', ring(4, -1))]
  transfers between devices with their start and end apart: 23 -> 26, of which waited for: 15 -> 9; matrix products, arithmetic and copies ran while one was open for 6% -> 5% of each run, Pallas kernels for 6% -> 14%
where the time goes in v1:
time: 161 us
  waiting for transfers between devices  55.8 us (35%)
  starting transfers between devices  42.7 us (27%)
  Pallas kernels  35.3 us (22%)
  local copies, waits for them, and re-layouts  12.4 us (8%)
  matrix products  9.24 us (6%)
  other arithmetic  4.14 us (3%)
    ppermute x1, waiting for transfers between devices, per_device(): part_b = send(left, joint, joint_ring(-1))  16.7 us
    pallas_call x1, Pallas kernels, key_call(): pl.pallas_call(key_kernel, grid_spec=pltpu.PrefetchScalarGridSpec(num_sca...  11.6 us
    ppermute x6, waiting for transfers between devices, along_z(): received = send(groups[distance], 'ctx', z_ring(shift))  11.2 us
    pallas_call x1, Pallas kernels, forward_call(): pl.pallas_call(forward_kernel, grid_spec=pltpu.PrefetchScalarGridSpec(num...  10.6 us
    unnamed x38, local copies, waits for them, and re-layouts  9.75 us
    dot_general x4, matrix products, dot_nt(): lax.dot_general(lhs, rhs, (((1,), (1,)), ((), ())), preferred_element_typ...  9.24 us
    ppermute x6, starting transfers between devices, along_z(): received = send(groups[distance], 'ctx', z_ring(shift))  7.97 us
    ppermute x1, waiting for transfers between devices, per_device(): part_a = send(right, joint, joint_ring(1))  7.84 us
  transfers between devices with their start and end apart: 26, of which 9 were waited for; matrix products, arithmetic and copies ran while one was open for 5% of the time, Pallas kernels for 14%

profile of v1, /device:TPU:1, one launch (start us, length us, event | category | flops | bytes accessed | tf_op | source)
XLA Modules:
  0.0 160.6 jit_solution(11765601882648050474)
XLA Ops:
  1.7 3.6 %collective-permute-start.6 = (bf16[512,256]{1,0:T(8,128)(2,1)S(1)}, bf16[512,256]{1,0:T(8,128)(2,1)}, u32[]{:S(2)}, u32[]{:S(2)}) collective-permute-start(bf16[512,256]{1,0:T(8,128)(2,1)S(1)} %pad_maximum_fusion.2.refs_0_), channel_id=1, source_target_pairs={{0,16},{4,20},{8,24},{12,28},{16,0},{20,4},{24,8},{28,12},{1,17},{... | collective-permute-start | bytes 786440 | tf_op jit(solution)/shard_map/ppermute | solution.py:422
  5.4 3.8 %collective-permute-start.7 = (bf16[512,256]{1,0:T(8,128)(2,1)S(1)}, bf16[512,256]{1,0:T(8,128)(2,1)S(1)}, u32[]{:S(2)}, u32[]{:S(2)}) collective-permute-start(bf16[512,256]{1,0:T(8,128)(2,1)S(1)} %pad_maximum_fusion.2.refs_0_), channel_id=1, source_target_pairs={{0,12},{4,0},{8,4},{12,8},{16,28},{20,16},{24,20},{28,24},{1,13},{... | collective-permute-start | bytes 786440 | tf_op jit(solution)/shard_map/ppermute | solution.py:425
  9.1 2.3 %slice_bitcast_fusion = (bf16[64,4096]{1,0:T(8,128)(2,1)}, bf16[64,4096]{1,0:T(8,128)(2,1)}) fusion(bf16[1,128,4096]{2,1,0:T(8,128)(2,1)} %param.13), kind=kLoop, calls=%fused_computation.12 | loop fusion | bytes 2097152 | tf_op jit(solution)/shard_map/slice | solution.py:413
  11.4 1.3 collective-permute-start
  12.7 1.4 collective-permute-start.3
  14.8 4.5 %collective-permute-done.7.refs_2_ = bf16[512,256]{1,0:T(8,128)(2,1)S(1)} collective-permute-done((bf16[512,256]{1,0:T(8,128)(2,1)S(1)}, bf16[512,256]{1,0:T(8,128)(2,1)S(1)}, u32[]{:S(2)}, u32[]{:S(2)}) %collective-permute-start.7) | collective-permute-done | bytes 262176 | tf_op jit(solution)/shard_map/ppermute | solution.py:425
  20.0 3.6 %collective-permute-start.8 = (bf16[512,256]{1,0:T(8,128)(2,1)}, bf16[512,256]{1,0:T(8,128)(2,1)S(1)}, u32[]{:S(2)}, u32[]{:S(2)}) collective-permute-start(bf16[512,256]{1,0:T(8,128)(2,1)} %collective-permute-done.6.refs_1_), channel_id=1, source_target_pairs={{0,12},{4,0},{8,4},{12,8},{16,28},{20,16},{24,20},{28,24},{1,13},{... | collective-permute-start | bytes 786440 | tf_op jit(solution)/shard_map/ppermute | solution.py:426
  26.4 1.4 collective-permute-start.2
  28.4 5.4 %collective-permute-done.8.refs_3_ = bf16[512,256]{1,0:T(8,128)(2,1)S(1)} collective-permute-done((bf16[512,256]{1,0:T(8,128)(2,1)}, bf16[512,256]{1,0:T(8,128)(2,1)S(1)}, u32[]{:S(2)}, u32[]{:S(2)}) %collective-permute-start.8) | collective-permute-done | bytes 262176 | tf_op jit(solution)/shard_map/ppermute | solution.py:426
  36.6 1.4 collective-permute-start.5
  45.3 10.6 %attn_forward.1 = (bf16[17,4,256,256]{3,2,1,0:T(8,128)(2,1)S(1)}, f32[2,128,1024]{2,1,0:T(8,128)S(1)}, f32[2,8,1024]{2,1,0:T(8,128)S(1)}, f32[17,1,1024]{2,1,0:T(1,128)S(1)}, bf16[16,256,256]{2,1,0:T(8,128)(2,1)S(1)}) custom-call(s32[1]{0:T(128)S(1)} %bitcast.44, s32[16]{0:T(128)S(1)} %reshape.84.ids_ref, bf16[512,256]{1,0:T(8,128)(2,1)S(1)} %pad_maximum_fusion.2.refs_0_, ...), custom_call_target="tpu_custom_call" | custom-call | flops 2281701376 | bytes 13631488 | tf_op jit(solution)/shard_map/attn_forward/pallas_call | solution.py:130
  56.0 6.9 %attn_grad.1.grad_ref = bf16[512,512]{1,0:T(8,128)(2,1)S(1)} custom-call(s32[7]{0:T(128)S(1)} %broadcast_multiply_fusion.rows_ref, bf16[128,4096]{1,0:T(8,128)(2,1)S(1)} %bitcast.40, bf16[64,4096]{1,0:T(8,128)(2,1)S(1)} %collective-permute-done.refs_1_, bf16[64,4096]{1,0:T(8,128)(2,1)S(1)} %collective-permute-done.1.refs_2_, ...), custom_call_target="tpu_custom_call" | custom-call | flops 2147483648 | bytes 9437184 | tf_op jit(solution)/shard_map/attn_grad/pallas_call | solution.py:194
  62.9 6.2 %attn_value_grad.1 = (bf16[2,512,128]{2,1,0:T(8,128)(2,1)S(1)}, bf16[2,512,128]{2,1,0:T(8,128)(2,1)S(1)}, bf16[2,512,128]{2,1,0:T(8,128)(2,1)S(1)}, bf16[2,512,128]{2,1,0:T(8,128)(2,1)S(1)}) custom-call(s32[1]{0:T(128)S(1)} %bitcast.45, s32[16]{0:T(128)S(1)} %reshape.84.ids_ref, bf16[512,512]{1,0:T(8,128)(2,1)S(1)} %attn_grad.1.grad_ref, ...), custom_call_target="tpu_custom_call" | custom-call | flops 1140850688 | bytes 11534336 | tf_op jit(solution)/shard_map/attn_value_grad/pallas_call | solution.py:260
  69.1 3.5 %collective-permute-start.19 = (bf16[2,512,128]{2,1,0:T(8,128)(2,1)S(1)}, bf16[2,512,128]{2,1,0:T(8,128)(2,1)S(1)}, u32[]{:S(2)}, u32[]{:S(2)}) collective-permute-start(bf16[2,512,128]{2,1,0:T(8,128)(2,1)S(1)} %get-tuple-element.42), channel_id=1, source_target_pairs={{0,12},{4,0},{8,4},{12,8},{16,28},{20,16},{24,20},{28,24},{1,13},{... | collective-permute-start | bytes 786440 | tf_op jit(solution)/shard_map/ppermute | solution.py:449
  73.3 11.6 %attn_key_grad.1 = (bf16[512,512]{1,0:T(8,128)(2,1)S(1)}, bf16[2,512,128]{2,1,0:T(8,128)(2,1)S(1)}, bf16[2,512,128]{2,1,0:T(8,128)(2,1)S(1)}, bf16[2,512,128]{2,1,0:T(8,128)(2,1)S(1)}, bf16[2,512,128]{2,1,0:T(8,128)(2,1)S(1)}) custom-call(s32[1]{0:T(128)S(1)} %bitcast.46, s32[16]{0:T(128)S(1)} %reshape.84.ids_ref, bf16[512,512]{1,0:T(8,128)(2,1)S(1)} %attn_grad.1.grad_ref, ...), custom_call_target="tpu_custom_call" | custom-call | flops 3422552064 | bytes 14680064 | tf_op jit(solution)/shard_map/attn_key_grad/pallas_call | solution.py:359
  84.9 2.1 %collective-permute-start.15 = (bf16[2,512,128]{2,1,0:T(8,128)(2,1)S(1)}, bf16[2,512,128]{2,1,0:T(8,128)(2,1)S(1)}, u32[]{:S(2)}, u32[]{:S(2)}) collective-permute-start(bf16[2,512,128]{2,1,0:T(8,128)(2,1)S(1)} %get-tuple-element.38), channel_id=1, source_target_pairs={{0,12},{4,0},{8,4},{12,8},{16,28},{20,16},{24,20},{28,24},{1,13},{... | collective-permute-start | bytes 786440 | tf_op jit(solution)/shard_map/ppermute | solution.py:449
  87.0 1.7 %collective-permute-start.14 = (bf16[2,512,128]{2,1,0:T(8,128)(2,1)S(1)}, bf16[2,512,128]{2,1,0:T(8,128)(2,1)S(1)}, u32[]{:S(2)}, u32[]{:S(2)}) collective-permute-start(bf16[2,512,128]{2,1,0:T(8,128)(2,1)S(1)} %get-tuple-element.37), channel_id=1, source_target_pairs={{0,8},{4,12},{8,0},{12,4},{16,24},{20,28},{24,16},{28,20},{1,9},{5... | collective-permute-start | bytes 786440 | tf_op jit(solution)/shard_map/ppermute | solution.py:449
  89.2 2.3 %collective-permute-done.15 = bf16[2,512,128]{2,1,0:T(8,128)(2,1)S(1)} collective-permute-done((bf16[2,512,128]{2,1,0:T(8,128)(2,1)S(1)}, bf16[2,512,128]{2,1,0:T(8,128)(2,1)S(1)}, u32[]{:S(2)}, u32[]{:S(2)}) %collective-permute-start.15) | collective-permute-done | bytes 262176 | tf_op jit(solution)/shard_map/ppermute | solution.py:449
  91.5 2.4 %collective-permute-done.14 = bf16[2,512,128]{2,1,0:T(8,128)(2,1)S(1)} collective-permute-done((bf16[2,512,128]{2,1,0:T(8,128)(2,1)S(1)}, bf16[2,512,128]{2,1,0:T(8,128)(2,1)S(1)}, u32[]{:S(2)}, u32[]{:S(2)}) %collective-permute-start.14) | collective-permute-done | bytes 262176 | tf_op jit(solution)/shard_map/ppermute | solution.py:449
  93.8 6.6 %collective-permute-done.13 = bf16[2,512,128]{2,1,0:T(8,128)(2,1)S(1)} collective-permute-done((bf16[2,512,128]{2,1,0:T(8,128)(2,1)S(1)}, bf16[2,512,128]{2,1,0:T(8,128)(2,1)S(1)}, u32[]{:S(2)}, u32[]{:S(2)}) %collective-permute-start.13) | collective-permute-done | bytes 262176 | tf_op jit(solution)/shard_map/ppermute | solution.py:449
  101.2 5.0 %collective-permute-done.16 = bf16[512,128]{1,0:T(8,128)(2,1)S(1)} collective-permute-done((bf16[512,128]{1,0:T(8,128)(2,1)S(1)}, bf16[512,128]{1,0:T(8,128)(2,1)S(1)}, u32[]{:S(2)}, u32[]{:S(2)}) %collective-permute-start.16) | collective-permute-done | bytes 131104 | tf_op jit(solution)/shard_map/ppermute | solution.py:459
  106.3 2.3 %convolution_convert_fusion.2 = bf16[128,4096]{1,0:T(8,128)(2,1)S(1)} fusion(bf16[512,768]{1,0:T(8,128)(2,1)S(1)} %pad_maximum_fusion.1, s32[]{:T(128)S(6)} %select_n.96, bf16[4096,128]{1,0:T(8,128)(2,1)S(1)} %bitcast.55, bf16[4096,128]{1,0:T(8,128)(2,1)S(1)} %bitcast.59, bf16[4096,512]{1,0:T(8,128)(2,1)S(1)} %bitcast.51), kind=kOutput, calls=%fused_computation.3 | convolution fusion | flops 824705024 | bytes 7536644 | tf_op jit(solution)/shard_map/dot_general | solution.py:21
  108.7 2.3 %convolution_convert_fusion = bf16[128,4096]{1,0:T(8,128)(2,1)S(1)} fusion(bf16[512,768]{1,0:T(8,128)(2,1)S(1)} %pad_maximum_fusion.1, s32[]{:T(128)S(6)} %select_n.98, bf16[4096,128]{1,0:T(8,128)(2,1)S(1)} %bitcast.56, bf16[4096,128]{1,0:T(8,128)(2,1)S(1)} %bitcast.60, bf16[4096,512]{1,0:T(8,128)(2,1)S(1)} %bitcast.52), kind=kOutput, calls=%fused_computation.1 | convolution fusion | flops 824705024 | bytes 7536644 | tf_op jit(solution)/shard_map/dot_general | solution.py:21
  111.1 1.5 collective-permute-start.24
  112.6 2.3 %convolution_convert_fusion.1 = bf16[128,4096]{1,0:T(8,128)(2,1)S(1)} fusion(bf16[512,768]{1,0:T(8,128)(2,1)S(1)} %pad_maximum_fusion.1, s32[]{:T(128)S(6)} %select_n.97, bf16[4096,128]{1,0:T(8,128)(2,1)S(1)} %bitcast.57, bf16[4096,128]{1,0:T(8,128)(2,1)S(1)} %bitcast.61, bf16[4096,512]{1,0:T(8,128)(2,1)S(1)} %bitcast.53), kind=kOutput, calls=%fused_computation.2 | convolution fusion | flops 824705024 | bytes 7536644 | tf_op jit(solution)/shard_map/dot_general | solution.py:21
  115.0 2.3 %convolution_convert_fusion.3 = bf16[128,4096]{1,0:T(8,128)(2,1)S(1)} fusion(bf16[512,768]{1,0:T(8,128)(2,1)S(1)} %pad_maximum_fusion.1, s32[]{:T(128)S(6)} %select_n.95, bf16[4096,128]{1,0:T(8,128)(2,1)S(1)} %bitcast.58, bf16[4096,128]{1,0:T(8,128)(2,1)S(1)} %bitcast.62, bf16[4096,512]{1,0:T(8,128)(2,1)S(1)} %bitcast.54), kind=kOutput, calls=%fused_computation.4 | convolution fusion | flops 824705024 | bytes 7536644 | tf_op jit(solution)/shard_map/dot_general | solution.py:21
  117.3 4.2 %collective-permute-start.21 = (bf16[128,4096]{1,0:T(8,128)(2,1)S(1)}, bf16[128,4096]{1,0:T(8,128)(2,1)S(1)}, u32[]{:S(2)}, u32[]{:S(2)}) collective-permute-start(bf16[128,4096]{1,0:T(8,128)(2,1)S(1)} %convolution_convert_fusion.3), channel_id=1, source_target_pairs={{0,96},{32,0},{64,32},{96,64},{1,97},{33,1},{65,33},{97,65},{2,98}... | collective-permute-start | bytes 3145736 | tf_op jit(solution)/shard_map/ppermute | solution.py:477
  121.7 6.6 %collective-permute-start.25 = (bf16[128,4096]{1,0:T(8,128)(2,1)S(1)}, bf16[128,4096]{1,0:T(8,128)(2,1)S(1)}, u32[]{:S(2)}, u32[]{:S(2)}) collective-permute-start(bf16[128,4096]{1,0:T(8,128)(2,1)S(1)} %add_convert_fusion.1), channel_id=1, source_target_pairs={{0,99},{1,96},{2,97},{3,98},{32,3},{33,0},{34,1},{35,2},{64,35},{6... | collective-permute-start | bytes 3145736 | tf_op jit(solution)/shard_map/ppermute | solution.py:484
  129.5 5.1 %collective-permute-done.21 = bf16[128,4096]{1,0:T(8,128)(2,1)S(1)} collective-permute-done((bf16[128,4096]{1,0:T(8,128)(2,1)S(1)}, bf16[128,4096]{1,0:T(8,128)(2,1)S(1)}, u32[]{:S(2)}, u32[]{:S(2)}) %collective-permute-start.21) | collective-permute-done | bytes 1048608 | tf_op jit(solution)/shard_map/ppermute | solution.py:477
  134.5 16.7 %collective-permute-done.25 = bf16[128,4096]{1,0:T(8,128)(2,1)S(1)} collective-permute-done((bf16[128,4096]{1,0:T(8,128)(2,1)S(1)}, bf16[128,4096]{1,0:T(8,128)(2,1)S(1)}, u32[]{:S(2)}, u32[]{:S(2)}) %collective-permute-start.25) | collective-permute-done | bytes 1048608 | tf_op jit(solution)/shard_map/ppermute | solution.py:484
  151.3 7.8 %collective-permute-done.23 = bf16[128,4096]{1,0:T(8,128)(2,1)S(1)} collective-permute-done((bf16[128,4096]{1,0:T(8,128)(2,1)S(1)}, bf16[128,4096]{1,0:T(8,128)(2,1)S(1)}, u32[]{:S(2)}, u32[]{:S(2)}) %collective-permute-start.23) | collective-permute-done | bytes 1048608 | tf_op jit(solution)/shard_map/ppermute | solution.py:483
  159.1 1.4 fusion
  (86 shorter events, 19.4 us)
Async XLA Ops:
  0.6 55.3 %copy-start = (bf16[1,128,4096]{2,1,0:T(8,128)(2,1)S(1)}, bf16[1,128,4096]{2,1,0:T(8,128)(2,1)}, u32[]{:S(2)}) copy-start(bf16[1,128,4096]{2,1,0:T(8,128)(2,1)} %param.13) | copy-start | bytes 3145732
  1.7 12.4 %collective-permute-start.6 = (bf16[512,256]{1,0:T(8,128)(2,1)S(1)}, bf16[512,256]{1,0:T(8,128)(2,1)}, u32[]{:S(2)}, u32[]{:S(2)}) collective-permute-start(bf16[512,256]{1,0:T(8,128)(2,1)S(1)} %pad_maximum_fusion.2.refs_0_), channel_id=1, source_target_pairs={{0,16},{4,20},{8,24},{12,28},{16,0},{20,4},{24,8},{28,12},{1,17},{... | collective-permute-start | bytes 786440 | tf_op jit(solution)/shard_map/ppermute | solution.py:422
  5.4 13.9 %collective-permute-start.7 = (bf16[512,256]{1,0:T(8,128)(2,1)S(1)}, bf16[512,256]{1,0:T(8,128)(2,1)S(1)}, u32[]{:S(2)}, u32[]{:S(2)}) collective-permute-start(bf16[512,256]{1,0:T(8,128)(2,1)S(1)} %pad_maximum_fusion.2.refs_0_), channel_id=1, source_target_pairs={{0,12},{4,0},{8,4},{12,8},{16,28},{20,16},{24,20},{28,24},{1,13},{... | collective-permute-start | bytes 786440 | tf_op jit(solution)/shard_map/ppermute | solution.py:425
  9.1 14.5 %collective-permute-start.9 = (bf16[512,256]{1,0:T(8,128)(2,1)S(1)}, bf16[512,256]{1,0:T(8,128)(2,1)S(1)}, u32[]{:S(2)}, u32[]{:S(2)}) collective-permute-start(bf16[512,256]{1,0:T(8,128)(2,1)S(1)} %pad_maximum_fusion.2.refs_0_), channel_id=1, source_target_pairs={{0,8},{4,12},{8,0},{12,4},{16,24},{20,28},{24,16},{28,20},{1,9},{5... | collective-permute-start | bytes 786440 | tf_op jit(solution)/shard_map/ppermute | solution.py:425
  11.4 15.0 %collective-permute-start = (bf16[64,4096]{1,0:T(8,128)(2,1)}, bf16[64,4096]{1,0:T(8,128)(2,1)S(1)}, u32[]{:S(2)}, u32[]{:S(2)}) collective-permute-start(bf16[64,4096]{1,0:T(8,128)(2,1)} %get-tuple-element.48), channel_id=1, source_target_pairs={{0,1},{1,2},{2,3},{3,0},{4,5},{5,6},{6,7},{7,4},{8,9},{9,10},{10,1... | collective-permute-start | bytes 1572872 | tf_op jit(solution)/shard_map/ppermute | solution.py:414
  12.7 15.2 %collective-permute-start.3 = (bf16[64,4096]{1,0:T(8,128)(2,1)}, bf16[64,4096]{1,0:T(8,128)(2,1)S(1)}, u32[]{:S(2)}, u32[]{:S(2)}) collective-permute-start(bf16[64,4096]{1,0:T(8,128)(2,1)} %get-tuple-element.47), channel_id=1, source_target_pairs={{0,3},{1,0},{2,1},{3,2},{4,7},{5,4},{6,5},{7,6},{8,11},{9,8},{10,9... | collective-permute-start | bytes 1572872 | tf_op jit(solution)/shard_map/ppermute | solution.py:415
  14.1 10.3 %collective-permute-start.11 = (bf16[512,256]{1,0:T(8,128)(2,1)S(1)}, bf16[512,256]{1,0:T(8,128)(2,1)S(1)}, u32[]{:S(2)}, u32[]{:S(2)}) collective-permute-start(bf16[512,256]{1,0:T(8,128)(2,1)S(1)} %pad_maximum_fusion.2.refs_0_), channel_id=1, source_target_pairs={{0,4},{4,8},{8,12},{12,0},{16,20},{20,24},{24,28},{28,16},{1,5},{5... | collective-permute-start | bytes 786440 | tf_op jit(solution)/shard_map/ppermute | solution.py:425
  20.0 13.8 %collective-permute-start.8 = (bf16[512,256]{1,0:T(8,128)(2,1)}, bf16[512,256]{1,0:T(8,128)(2,1)S(1)}, u32[]{:S(2)}, u32[]{:S(2)}) collective-permute-start(bf16[512,256]{1,0:T(8,128)(2,1)} %collective-permute-done.6.refs_1_), channel_id=1, source_target_pairs={{0,12},{4,0},{8,4},{12,8},{16,28},{20,16},{24,20},{28,24},{1,13},{... | collective-permute-start | bytes 786440 | tf_op jit(solution)/shard_map/ppermute | solution.py:426
  24.3 11.5 %collective-permute-start.10 = (bf16[512,256]{1,0:T(8,128)(2,1)}, bf16[512,256]{1,0:T(8,128)(2,1)S(1)}, u32[]{:S(2)}, u32[]{:S(2)}) collective-permute-start(bf16[512,256]{1,0:T(8,128)(2,1)} %collective-permute-done.6.refs_1_), channel_id=1, source_target_pairs={{0,8},{4,12},{8,0},{12,4},{16,24},{20,28},{24,16},{28,20},{1,9},{5... | collective-permute-start | bytes 786440 | tf_op jit(solution)/shard_map/ppermute | solution.py:426
  25.1 30.8 %collective-permute-start.1 = (bf16[64,4096]{1,0:T(8,128)(2,1)}, bf16[64,4096]{1,0:T(8,128)(2,1)S(1)}, u32[]{:S(2)}, u32[]{:S(2)}) collective-permute-start(bf16[64,4096]{1,0:T(8,128)(2,1)} %get-tuple-element.47), channel_id=1, source_target_pairs={{0,1},{1,2},{2,3},{3,0},{4,5},{5,6},{6,7},{7,4},{8,9},{9,10},{10,1... | collective-permute-start | bytes 1572872 | tf_op jit(solution)/shard_map/ppermute | solution.py:418
  26.4 29.5 %collective-permute-start.2 = (bf16[64,4096]{1,0:T(8,128)(2,1)}, bf16[64,4096]{1,0:T(8,128)(2,1)S(1)}, u32[]{:S(2)}, u32[]{:S(2)}) collective-permute-start(bf16[64,4096]{1,0:T(8,128)(2,1)} %get-tuple-element.48), channel_id=1, source_target_pairs={{0,3},{1,0},{2,1},{3,2},{4,7},{5,4},{6,5},{7,6},{8,11},{9,8},{10,9... | collective-permute-start | bytes 1572872 | tf_op jit(solution)/shard_map/ppermute | solution.py:419
  27.9 11.3 %collective-permute-start.12 = (bf16[512,256]{1,0:T(8,128)(2,1)}, bf16[512,256]{1,0:T(8,128)(2,1)}, u32[]{:S(2)}, u32[]{:S(2)}) collective-permute-start(bf16[512,256]{1,0:T(8,128)(2,1)} %collective-permute-done.6.refs_1_), channel_id=1, source_target_pairs={{0,4},{4,8},{8,12},{12,0},{16,20},{20,24},{24,28},{28,16},{1,5},{5... | collective-permute-start | bytes 786440 | tf_op jit(solution)/shard_map/ppermute | solution.py:426
  34.6 21.4 %collective-permute-start.4 = (bf16[64,4096]{1,0:T(8,128)(2,1)S(1)}, bf16[64,4096]{1,0:T(8,128)(2,1)}, u32[]{:S(2)}, u32[]{:S(2)}) collective-permute-start(bf16[64,4096]{1,0:T(8,128)(2,1)S(1)} %collective-permute-done.refs_1_), channel_id=1, source_target_pairs={{0,1},{1,2},{2,3},{3,0},{4,5},{5,6},{6,7},{7,4},{8,9},{9,10},{10,1... | collective-permute-start | bytes 1572872 | tf_op jit(solution)/shard_map/ppermute | solution.py:416
  36.6 19.4 %collective-permute-start.5 = (bf16[64,4096]{1,0:T(8,128)(2,1)S(1)}, bf16[64,4096]{1,0:T(8,128)(2,1)}, u32[]{:S(2)}, u32[]{:S(2)}) collective-permute-start(bf16[64,4096]{1,0:T(8,128)(2,1)S(1)} %collective-permute-done.3.refs_4_), channel_id=1, source_target_pairs={{0,3},{1,0},{2,1},{3,2},{4,7},{5,4},{6,5},{7,6},{8,11},{9,8},{10,9... | collective-permute-start | bytes 1572872 | tf_op jit(solution)/shard_map/ppermute | solution.py:417
  39.1 16.8 %copy-start.1 = (bf16[1,512,4096]{2,1,0:T(8,128)(2,1)S(1)}, bf16[1,512,4096]{2,1,0:T(8,128)(2,1)}, u32[]{:S(2)}) copy-start(bf16[1,512,4096]{2,1,0:T(8,128)(2,1)} %param.17) | copy-start | bytes 12582916
  62.9 10.4 %copy-start.3 = (bf16[1,512,512]{2,1,0:T(8,128)(2,1)S(1)}, bf16[1,512,512]{2,1,0:T(8,128)(2,1)}, u32[]{:S(2)}) copy-start(bf16[1,512,512]{2,1,0:T(8,128)(2,1)} %param.10) | copy-start | bytes 1572868
  69.1 19.6 %collective-permute-start.19 = (bf16[2,512,128]{2,1,0:T(8,128)(2,1)S(1)}, bf16[2,512,128]{2,1,0:T(8,128)(2,1)S(1)}, u32[]{:S(2)}, u32[]{:S(2)}) collective-permute-start(bf16[2,512,128]{2,1,0:T(8,128)(2,1)S(1)} %get-tuple-element.42), channel_id=1, source_target_pairs={{0,12},{4,0},{8,4},{12,8},{16,28},{20,16},{24,20},{28,24},{1,13},{... | collective-permute-start | bytes 786440 | tf_op jit(solution)/shard_map/ppermute | solution.py:449
  72.6 16.1 %collective-permute-start.18 = (bf16[2,512,128]{2,1,0:T(8,128)(2,1)S(1)}, bf16[2,512,128]{2,1,0:T(8,128)(2,1)S(1)}, u32[]{:S(2)}, u32[]{:S(2)}) collective-permute-start(bf16[2,512,128]{2,1,0:T(8,128)(2,1)S(1)} %get-tuple-element.41), channel_id=1, source_target_pairs={{0,8},{4,12},{8,0},{12,4},{16,24},{20,28},{24,16},{28,20},{1,9},{5... | collective-permute-start | bytes 786440 | tf_op jit(solution)/shard_map/ppermute | solution.py:449
  72.6 16.1 %collective-permute-start.17 = (bf16[2,512,128]{2,1,0:T(8,128)(2,1)S(1)}, bf16[2,512,128]{2,1,0:T(8,128)(2,1)S(1)}, u32[]{:S(2)}, u32[]{:S(2)}) collective-permute-start(bf16[2,512,128]{2,1,0:T(8,128)(2,1)S(1)} %get-tuple-element.40), channel_id=1, source_target_pairs={{0,4},{4,8},{8,12},{12,0},{16,20},{20,24},{24,28},{28,16},{1,5},{5... | collective-permute-start | bytes 786440 | tf_op jit(solution)/shard_map/ppermute | solution.py:449
  84.9 21.4 %copy-start.16 = (bf16[1,4096,512]{2,1,0:T(8,128)(2,1)S(1)}, bf16[1,4096,512]{2,1,0:T(8,128)(2,1)}, u32[]{:S(2)}) copy-start(bf16[1,4096,512]{2,1,0:T(8,128)(2,1)} %param.14) | copy-start | bytes 12582916
  84.9 21.4 %copy-start.17 = (bf16[1,4096,128]{2,1,0:T(8,128)(2,1)S(1)}, bf16[1,4096,128]{2,1,0:T(8,128)(2,1)}, u32[]{:S(2)}) copy-start(bf16[1,4096,128]{2,1,0:T(8,128)(2,1)} %param.16) | copy-start | bytes 3145732
  84.9 21.4 %copy-start.18 = (bf16[1,4096,128]{2,1,0:T(8,128)(2,1)S(1)}, bf16[1,4096,128]{2,1,0:T(8,128)(2,1)}, u32[]{:S(2)}) copy-start(bf16[1,4096,128]{2,1,0:T(8,128)(2,1)} %param.15) | copy-start | bytes 3145732
  84.9 6.6 %collective-permute-start.15 = (bf16[2,512,128]{2,1,0:T(8,128)(2,1)S(1)}, bf16[2,512,128]{2,1,0:T(8,128)(2,1)S(1)}, u32[]{:S(2)}, u32[]{:S(2)}) collective-permute-start(bf16[2,512,128]{2,1,0:T(8,128)(2,1)S(1)} %get-tuple-element.38), channel_id=1, source_target_pairs={{0,12},{4,0},{8,4},{12,8},{16,28},{20,16},{24,20},{28,24},{1,13},{... | collective-permute-start | bytes 786440 | tf_op jit(solution)/shard_map/ppermute | solution.py:449
  87.0 6.8 %collective-permute-start.14 = (bf16[2,512,128]{2,1,0:T(8,128)(2,1)S(1)}, bf16[2,512,128]{2,1,0:T(8,128)(2,1)S(1)}, u32[]{:S(2)}, u32[]{:S(2)}) collective-permute-start(bf16[2,512,128]{2,1,0:T(8,128)(2,1)S(1)} %get-tuple-element.37), channel_id=1, source_target_pairs={{0,8},{4,12},{8,0},{12,4},{16,24},{20,28},{24,16},{28,20},{1,9},{5... | collective-permute-start | bytes 786440 | tf_op jit(solution)/shard_map/ppermute | solution.py:449
  88.7 11.7 %collective-permute-start.13 = (bf16[2,512,128]{2,1,0:T(8,128)(2,1)S(1)}, bf16[2,512,128]{2,1,0:T(8,128)(2,1)S(1)}, u32[]{:S(2)}, u32[]{:S(2)}) collective-permute-start(bf16[2,512,128]{2,1,0:T(8,128)(2,1)S(1)} %get-tuple-element.36), channel_id=1, source_target_pairs={{0,4},{4,8},{8,12},{12,0},{16,20},{20,24},{24,28},{28,16},{1,5},{5... | collective-permute-start | bytes 786440 | tf_op jit(solution)/shard_map/ppermute | solution.py:449
  88.9 12.2 %collective-permute-start.20 = (bf16[512,128]{1,0:T(8,128)(2,1)S(1)}, bf16[512,128]{1,0:T(8,128)(2,1)S(1)}, u32[]{:S(2)}, u32[]{:S(2)}) collective-permute-start(bf16[512,128]{1,0:T(8,128)(2,1)S(1)} %fusion.10), channel_id=1, source_target_pairs={{0,16},{4,20},{8,24},{12,28},{16,0},{20,4},{24,8},{28,12},{1,17},{... | collective-permute-start | bytes 393224 | tf_op jit(solution)/shard_map/ppermute | solution.py:459
  100.6 5.6 %collective-permute-start.16 = (bf16[512,128]{1,0:T(8,128)(2,1)S(1)}, bf16[512,128]{1,0:T(8,128)(2,1)S(1)}, u32[]{:S(2)}, u32[]{:S(2)}) collective-permute-start(bf16[512,128]{1,0:T(8,128)(2,1)S(1)} %fusion.9), channel_id=1, source_target_pairs={{0,16},{4,20},{8,24},{12,28},{16,0},{20,4},{24,8},{28,12},{1,17},{... | collective-permute-start | bytes 393224 | tf_op jit(solution)/shard_map/ppermute | solution.py:459
  111.1 10.4 %collective-permute-start.24 = (bf16[64,4096]{1,0:T(8,128)(2,1)S(1)}, bf16[64,4096]{1,0:T(8,128)(2,1)S(1)}, u32[]{:S(2)}, u32[]{:S(2)}) collective-permute-start(bf16[64,4096]{1,0:T(8,128)(2,1)S(1)} %get-tuple-element.46), channel_id=1, source_target_pairs={{0,3},{1,0},{2,1},{3,2},{4,7},{5,4},{6,5},{7,6},{8,11},{9,8},{10,9... | collective-permute-start | bytes 1572872 | tf_op jit(solution)/shard_map/ppermute | solution.py:475
  114.9 13.4 %collective-permute-start.22 = (bf16[64,4096]{1,0:T(8,128)(2,1)S(1)}, bf16[64,4096]{1,0:T(8,128)(2,1)S(1)}, u32[]{:S(2)}, u32[]{:S(2)}) collective-permute-start(bf16[64,4096]{1,0:T(8,128)(2,1)S(1)} %get-tuple-element.45), channel_id=1, source_target_pairs={{0,1},{1,2},{2,3},{3,0},{4,5},{5,6},{6,7},{7,4},{8,9},{9,10},{10,1... | collective-permute-start | bytes 1572872 | tf_op jit(solution)/shard_map/ppermute | solution.py:474
  117.3 17.2 %collective-permute-start.21 = (bf16[128,4096]{1,0:T(8,128)(2,1)S(1)}, bf16[128,4096]{1,0:T(8,128)(2,1)S(1)}, u32[]{:S(2)}, u32[]{:S(2)}) collective-permute-start(bf16[128,4096]{1,0:T(8,128)(2,1)S(1)} %convolution_convert_fusion.3), channel_id=1, source_target_pairs={{0,96},{32,0},{64,32},{96,64},{1,97},{33,1},{65,33},{97,65},{2,98}... | collective-permute-start | bytes 3145736 | tf_op jit(solution)/shard_map/ppermute | solution.py:477
  121.7 29.5 %collective-permute-start.25 = (bf16[128,4096]{1,0:T(8,128)(2,1)S(1)}, bf16[128,4096]{1,0:T(8,128)(2,1)S(1)}, u32[]{:S(2)}, u32[]{:S(2)}) collective-permute-start(bf16[128,4096]{1,0:T(8,128)(2,1)S(1)} %add_convert_fusion.1), channel_id=1, source_target_pairs={{0,99},{1,96},{2,97},{3,98},{32,3},{33,0},{34,1},{35,2},{64,35},{6... | collective-permute-start | bytes 3145736 | tf_op jit(solution)/shard_map/ppermute | solution.py:484
  128.4 30.7 %collective-permute-start.23 = (bf16[128,4096]{1,0:T(8,128)(2,1)S(1)}, bf16[128,4096]{1,0:T(8,128)(2,1)S(1)}, u32[]{:S(2)}, u32[]{:S(2)}) collective-permute-start(bf16[128,4096]{1,0:T(8,128)(2,1)S(1)} %add_convert_fusion.2), channel_id=1, source_target_pairs={{0,97},{1,98},{2,99},{3,96},{32,1},{33,2},{34,3},{35,0},{64,33},{6... | collective-permute-start | bytes 3145736 | tf_op jit(solution)/shard_map/ppermute | solution.py:483
  (13 other events, 19.7 us)

commit v2 on v1

--- a/solution.py
+++ b/solution.py
@@ -420,10 +420,20 @@
 
     kv_own = jnp.concatenate([key_rows[0], value_rows[0]], axis=1)
     kv_pair = send(kv_own, "ctx", X_SWAP)
+    along, crossed = {}, {}
+    for distance, shift in ((2, 2), (1, -1), (3, 1)):
+        along[distance] = send(kv_own, "ctx", z_ring(shift))
+    for distance, shift in ((1, -1), (3, 1)):
+        crossed[distance] = send(kv_pair, "ctx", z_ring(shift))
+    crossed[2] = send(along[2], "ctx", X_SWAP)
     kv_chunks = [kv_own, kv_pair]
-    for shift in (-1, 2, 1):
-        kv_chunks.append(send(kv_own, "ctx", z_ring(shift)))
-        kv_chunks.append(send(kv_pair, "ctx", z_ring(shift)))
+    for distance in (1, 2, 3):
+        kv_chunks += [along[distance], crossed[distance]]
+
+    joint = ("section", "tp")
+    kv_weights = jnp.concatenate([key_weight[0], value_weight[0]], axis=1)
+    own_weights = send(kv_weights, "section", ring(4, -1))
+    far_weights = send(kv_weights, joint, joint_ring(2))
 
     index = jnp.arange(8, dtype=jnp.int32)
     source = ((own_x + index % 2) % 2) * 4 + (own_z + index // 2) % 4
@@ -459,30 +469,35 @@
         received = send(total[1].astype(bf16), "ctx", X_SWAP)
         return (total[0] + received.astype(f32)).astype(bf16)
 
+    def chunk_of(array, distance):
+        return lax.dynamic_slice_in_dim(array, ((tp + distance) % 4) * 128, 128, 0)
+
+    def query_term(distance):
+        return dot_nt(chunk_of(query_grad, distance), query_weight[0])
+
+    far_term = query_term(2).astype(bf16)
+    from_left = send(far_term[:half_rows], "tp", ring(4, 1))
+    from_right = send(far_term[half_rows:], "tp", ring(4, -1))
+    own_term = query_term(0).astype(bf16)
+    own = send(own_term, "section", ring(4, -1))
+    right, left = lax.optimization_barrier((query_term(1), query_term(3)))
+
     value_grad = with_pair(value_sum)
     key_grad = with_pair(key_sum)
 
-    stacked = jnp.concatenate([query_grad, key_grad, value_grad], axis=1)
-    weights = jnp.concatenate([query_weight[0], key_weight[0], value_weight[0]], axis=1)
-
-    def term_of(distance):
-        start = ((tp + distance) % 4) * 128
-        rows = lax.dynamic_slice_in_dim(stacked, start, 128, 0)
-        return dot_nt(rows, weights).astype(bf16)
-
-    far = term_of(2)
-    from_left = send(far[:half_rows], "tp", ring(4, 1))
-    from_right = send(far[half_rows:], "tp", ring(4, -1))
-    own_term = term_of(0)
-    own = send(own_term, "section", ring(4, -1))
-    right, left = lax.optimization_barrier((term_of(1), term_of(3)))
+    kv_grad = jnp.concatenate([key_grad, value_grad], axis=1)
     empty = jnp.zeros_like(from_left, dtype=f32)
-    right = (right.astype(f32) + jnp.concatenate([from_left.astype(f32), empty])).astype(bf16)
-    left = (left.astype(f32) + jnp.concatenate([empty, from_right.astype(f32)])).astype(bf16)
-    joint = ("section", "tp")
+    right = right + dot_nt(chunk_of(kv_grad, 1), kv_weights)
+    right = (right + jnp.concatenate([from_left.astype(f32), empty])).astype(bf16)
+    left = left + dot_nt(chunk_of(kv_grad, 3), kv_weights)
+    left = (left + jnp.concatenate([empty, from_right.astype(f32)])).astype(bf16)
     part_a = send(right, joint, joint_ring(1))
     part_b = send(left, joint, joint_ring(-1))
-    sent = (own.astype(f32) + part_a.astype(f32) + part_b.astype(f32)).astype(bf16)
+    far_rows = send(chunk_of(kv_grad, 2), joint, joint_ring(2))
+    own_rows = send(chunk_of(kv_grad, 0), "section", ring(4, -1))
+    rest = own.astype(f32) + dot_nt(own_rows, own_weights) + dot_nt(far_rows, far_weights)
+    rest = lax.optimization_barrier(rest)
+    sent = (rest + part_a.astype(f32) + part_b.astype(f32)).astype(bf16)
     return (sent[None], key_grad[None], value_grad[None])
 
 

time: 161 us -> 176 us (1.093); the launches traced: 161 us -> 173 us
  starting transfers between devices: 42.7 us -> 60.2 us
  waiting for transfers between devices: 55.8 us -> 49.6 us
  matrix products: 9.24 us -> 12.5 us
  local copies, waits for them, and re-layouts: 12.4 us -> 9.33 us
    ppermute x1, waiting for transfers between devices: 16.7 us -> 0.01 us  [per_device(): part_b = send(left, joint, joint_ring(-1))]
    ppermute x8 -> x12, starting transfers between devices: 10.2 us -> 26 us  [the longest x1 9.3 us: per_device(): own_rows = send(chunk_of(kv_grad, 0), 'section', ring(4, -1))]
    ppermute x8 -> x12, waiting for transfers between devices: 9.91 us -> 24.2 us  [the longest x1 19.6 us: per_device(): far_rows = send(chunk_of(kv_grad, 2), joint, joint_ring(2))]
    ppermute x1, waiting for transfers between devices: 7.84 us -> 0.01 us  [per_device(): part_a = send(right, joint, joint_ring(1))]
    ppermute x6, waiting for transfers between devices: 11.2 us -> 16.8 us  [along_z(): received = send(groups[distance], 'ctx', z_ring(shift))]
    ppermute x1, waiting for transfers between devices: 5.07 us -> 0.01 us  [per_device(): own = send(own_term, 'section', ring(4, -1))]
    ppermute x2, starting transfers between devices: 0.85 us -> 4.68 us  [with_pair(): received = send(total[1].astype(bf16), 'ctx', X_SWAP)]
    ppermute x2, waiting for transfers between devices: 5.02 us -> 8.57 us  [with_pair(): received = send(total[1].astype(bf16), 'ctx', X_SWAP)]
  transfers between devices with their start and end apart: 26 -> 30, of which waited for: 9 -> 11; matrix products, arithmetic and copies ran while one was open for 5% -> 10% of each run, Pallas kernels for 14% -> 21%
where the time goes in v2:
time: 176 us; the launch traced here: 173 us
  starting transfers between devices  60.2 us (34%)
  waiting for transfers between devices  49.6 us (28%)
  Pallas kernels  35.5 us (20%)
  matrix products  12.5 us (7%)
  local copies, waits for them, and re-layouts  9.33 us (5%)
  other arithmetic  4.64 us (3%)
    ppermute x1, waiting for transfers between devices, per_device(): far_rows = send(chunk_of(kv_grad, 2), joint, joint_ring(2))  19.6 us
    ppermute x6, waiting for transfers between devices, along_z(): received = send(groups[distance], 'ctx', z_ring(shift))  16.8 us
    dot_general x8, matrix products, dot_nt(): lax.dot_general(lhs, rhs, (((1,), (1,)), ((), ())), preferred_element_typ...  12.5 us
    pallas_call x1, Pallas kernels, key_call(): pl.pallas_call(key_kernel, grid_spec=pltpu.PrefetchScalarGridSpec(num_sca...  11.6 us
    pallas_call x1, Pallas kernels, forward_call(): pl.pallas_call(forward_kernel, grid_spec=pltpu.PrefetchScalarGridSpec(num...  11 us
    ppermute x1, starting transfers between devices, per_device(): own_rows = send(chunk_of(kv_grad, 0), 'section', ring(4, -1))  9.3 us
    ppermute x2, waiting for transfers between devices, with_pair(): received = send(total[1].astype(bf16), 'ctx', X_SWAP)  8.57 us
    ppermute x1, starting transfers between devices, per_device(): part_b = send(left, joint, joint_ring(-1))  8.1 us
  transfers between devices with their start and end apart: 30, of which 11 were waited for; matrix products, arithmetic and copies ran while one was open for 10% of the time, Pallas kernels for 21%

profile of v2, /device:TPU:1, one launch (start us, length us, event | category | flops | bytes accessed | tf_op | source)
XLA Modules:
  0.0 172.8 jit_solution(15815520255280014590)
XLA Ops:
  1.8 3.6 %collective-permute-start.6 = (bf16[512,256]{1,0:T(8,128)(2,1)S(1)}, bf16[512,256]{1,0:T(8,128)(2,1)}, u32[]{:S(2)}, u32[]{:S(2)}) collective-permute-start(bf16[512,256]{1,0:T(8,128)(2,1)S(1)} %pad_maximum_fusion.1.refs_0_), channel_id=1, source_target_pairs={{0,16},{4,20},{8,24},{12,28},{16,0},{20,4},{24,8},{28,12},{1,17},{... | collective-permute-start | bytes 786440 | tf_op jit(solution)/shard_map/ppermute | solution.py:422
  5.4 3.8 %collective-permute-start.7 = (bf16[512,256]{1,0:T(8,128)(2,1)S(1)}, bf16[512,256]{1,0:T(8,128)(2,1)S(1)}, u32[]{:S(2)}, u32[]{:S(2)}) collective-permute-start(bf16[512,256]{1,0:T(8,128)(2,1)S(1)} %pad_maximum_fusion.1.refs_0_), channel_id=1, source_target_pairs={{0,12},{4,0},{8,4},{12,8},{16,28},{20,16},{24,20},{28,24},{1,13},{... | collective-permute-start | bytes 786440 | tf_op jit(solution)/shard_map/ppermute | solution.py:425
  9.2 2.3 %slice_bitcast_fusion = (bf16[64,4096]{1,0:T(8,128)(2,1)}, bf16[64,4096]{1,0:T(8,128)(2,1)}) fusion(bf16[1,128,4096]{2,1,0:T(8,128)(2,1)} %param.13), kind=kLoop, calls=%fused_computation.18 | loop fusion | bytes 2097152 | tf_op jit(solution)/shard_map/slice | solution.py:413
  14.2 1.6 pad_maximum_fusion
  16.5 2.9 %collective-permute-done.7.refs_2_ = bf16[512,256]{1,0:T(8,128)(2,1)S(1)} collective-permute-done((bf16[512,256]{1,0:T(8,128)(2,1)S(1)}, bf16[512,256]{1,0:T(8,128)(2,1)S(1)}, u32[]{:S(2)}, u32[]{:S(2)}) %collective-permute-start.7) | collective-permute-done | bytes 262176 | tf_op jit(solution)/shard_map/ppermute | solution.py:425
  20.1 3.6 %collective-permute-start.8 = (bf16[512,256]{1,0:T(8,128)(2,1)}, bf16[512,256]{1,0:T(8,128)(2,1)S(1)}, u32[]{:S(2)}, u32[]{:S(2)}) collective-permute-start(bf16[512,256]{1,0:T(8,128)(2,1)} %collective-permute-done.6.refs_1_), channel_id=1, source_target_pairs={{0,12},{4,0},{8,4},{12,8},{16,28},{20,16},{24,20},{28,24},{1,13},{... | collective-permute-start | bytes 786440 | tf_op jit(solution)/shard_map/ppermute | solution.py:427
  31.9 2.7 %collective-permute-start.5 = (bf16[64,4096]{1,0:T(8,128)(2,1)S(1)}, bf16[64,4096]{1,0:T(8,128)(2,1)}, u32[]{:S(2)}, u32[]{:S(2)}) collective-permute-start(bf16[64,4096]{1,0:T(8,128)(2,1)S(1)} %collective-permute-done.3.refs_4_), channel_id=1, source_target_pairs={{0,3},{1,0},{2,1},{3,2},{4,7},{5,4},{6,5},{7,6},{8,11},{9,8},{10,9... | collective-permute-start | bytes 1572872 | tf_op jit(solution)/shard_map/ppermute | solution.py:417
  35.1 3.3 %collective-permute-start.23 = (bf16[4096,256]{1,0:T(8,128)(2,1)}, bf16[4096,256]{1,0:T(8,128)(2,1)}, u32[]{:S(2)}, u32[]{:S(2)}) collective-permute-start(bf16[4096,256]{1,0:T(8,128)(2,1)} %pad_maximum_fusion), channel_id=1, source_target_pairs={{0,96},{32,0},{64,32},{96,64},{1,97},{33,1},{65,33},{97,65},{2,98}... | collective-permute-start | bytes 6291464 | tf_op jit(solution)/shard_map/ppermute | solution.py:435
  42.2 11.0 %attn_forward.1 = (bf16[17,4,256,256]{3,2,1,0:T(8,128)(2,1)S(1)}, f32[2,128,1024]{2,1,0:T(8,128)S(1)}, f32[2,8,1024]{2,1,0:T(8,128)S(1)}, f32[17,1,1024]{2,1,0:T(1,128)S(1)}, bf16[16,256,256]{2,1,0:T(8,128)(2,1)S(1)}) custom-call(s32[1]{0:T(128)S(1)} %bitcast.56, s32[16]{0:T(128)S(1)} %reshape.84.ids_ref, bf16[512,256]{1,0:T(8,128)(2,1)S(1)} %pad_maximum_fusion.1.refs_0_, ...), custom_call_target="tpu_custom_call" | custom-call | flops 2281701376 | bytes 13631488 | tf_op jit(solution)/shard_map/attn_forward/pallas_call | solution.py:130
  53.2 1.7 collective-permute-start.25
  54.9 6.7 %attn_grad.1.grad_ref = bf16[512,512]{1,0:T(8,128)(2,1)S(1)} custom-call(s32[7]{0:T(128)S(1)} %broadcast_multiply_fusion.rows_ref, bf16[128,4096]{1,0:T(8,128)(2,1)S(1)} %bitcast.52, bf16[64,4096]{1,0:T(8,128)(2,1)S(1)} %collective-permute-done.refs_1_, bf16[64,4096]{1,0:T(8,128)(2,1)S(1)} %collective-permute-done.1.refs_2_, ...), custom_call_target="tpu_custom_call" | custom-call | flops 2147483648 | bytes 9437184 | tf_op jit(solution)/shard_map/attn_grad/pallas_call | solution.py:194
  61.7 6.2 %attn_value_grad.1 = (bf16[2,512,128]{2,1,0:T(8,128)(2,1)S(1)}, bf16[2,512,128]{2,1,0:T(8,128)(2,1)S(1)}, bf16[2,512,128]{2,1,0:T(8,128)(2,1)S(1)}, bf16[2,512,128]{2,1,0:T(8,128)(2,1)S(1)}) custom-call(s32[1]{0:T(128)S(1)} %bitcast.57, s32[16]{0:T(128)S(1)} %reshape.84.ids_ref, bf16[512,512]{1,0:T(8,128)(2,1)S(1)} %attn_grad.1.grad_ref, ...), custom_call_target="tpu_custom_call" | custom-call | flops 1140850688 | bytes 11534336 | tf_op jit(solution)/shard_map/attn_value_grad/pallas_call | solution.py:260
  67.8 11.6 %attn_key_grad.1 = (bf16[512,512]{1,0:T(8,128)(2,1)S(1)}, bf16[2,512,128]{2,1,0:T(8,128)(2,1)S(1)}, bf16[2,512,128]{2,1,0:T(8,128)(2,1)S(1)}, bf16[2,512,128]{2,1,0:T(8,128)(2,1)S(1)}, bf16[2,512,128]{2,1,0:T(8,128)(2,1)S(1)}) custom-call(s32[1]{0:T(128)S(1)} %bitcast.58, s32[16]{0:T(128)S(1)} %reshape.84.ids_ref, bf16[512,512]{1,0:T(8,128)(2,1)S(1)} %attn_grad.1.grad_ref, ...), custom_call_target="tpu_custom_call" | custom-call | flops 3422552064 | bytes 14680064 | tf_op jit(solution)/shard_map/attn_key_grad/pallas_call | solution.py:359
  79.5 1.5 convolution_convert_fusion
  82.5 1.5 fusion.1
  85.8 1.5 convolution_convert_fusion.1
  87.2 3.4 %collective-permute-done.16 = bf16[2,512,128]{2,1,0:T(8,128)(2,1)S(1)} collective-permute-done((bf16[2,512,128]{2,1,0:T(8,128)(2,1)S(1)}, bf16[2,512,128]{2,1,0:T(8,128)(2,1)S(1)}, u32[]{:S(2)}, u32[]{:S(2)}) %collective-permute-start.16) | collective-permute-done | bytes 262176 | tf_op jit(solution)/shard_map/ppermute | solution.py:459
  90.6 3.6 %collective-permute-start.20 = (bf16[2,512,128]{2,1,0:T(8,128)(2,1)S(1)}, bf16[2,512,128]{2,1,0:T(8,128)(2,1)S(1)}, u32[]{:S(2)}, u32[]{:S(2)}) collective-permute-start(bf16[2,512,128]{2,1,0:T(8,128)(2,1)S(1)} %get-tuple-element.42), channel_id=1, source_target_pairs={{0,12},{4,0},{8,4},{12,8},{16,28},{20,16},{24,20},{28,24},{1,13},{... | collective-permute-start | bytes 786440 | tf_op jit(solution)/shard_map/ppermute | solution.py:459
  94.2 7.3 %collective-permute-done.14 = bf16[2,512,128]{2,1,0:T(8,128)(2,1)S(1)} collective-permute-done((bf16[2,512,128]{2,1,0:T(8,128)(2,1)S(1)}, bf16[2,512,128]{2,1,0:T(8,128)(2,1)S(1)}, u32[]{:S(2)}, u32[]{:S(2)}) %collective-permute-start.14) | collective-permute-done | bytes 262176 | tf_op jit(solution)/shard_map/ppermute | solution.py:459
  102.6 2.1 %collective-permute-done.19 = bf16[2,512,128]{2,1,0:T(8,128)(2,1)S(1)} collective-permute-done((bf16[2,512,128]{2,1,0:T(8,128)(2,1)S(1)}, bf16[2,512,128]{2,1,0:T(8,128)(2,1)S(1)}, u32[]{:S(2)}, u32[]{:S(2)}) %collective-permute-start.19) | collective-permute-done | bytes 262176 | tf_op jit(solution)/shard_map/ppermute | solution.py:459
  104.8 2.9 %collective-permute-start.13 = (bf16[128,4096]{1,0:T(8,128)(2,1)S(1)}, bf16[128,4096]{1,0:T(8,128)(2,1)S(1)}, u32[]{:S(2)}, u32[]{:S(2)}) collective-permute-start(bf16[128,4096]{1,0:T(8,128)(2,1)S(1)} %convolution_convert_fusion.1), channel_id=1, source_target_pairs={{0,96},{32,0},{64,32},{96,64},{1,97},{33,1},{65,33},{97,65},{2,98}... | collective-permute-start | bytes 3145736 | tf_op jit(solution)/shard_map/ppermute | solution.py:482
  107.7 3.8 %collective-permute-done.18 = bf16[2,512,128]{2,1,0:T(8,128)(2,1)S(1)} collective-permute-done((bf16[2,512,128]{2,1,0:T(8,128)(2,1)S(1)}, bf16[2,512,128]{2,1,0:T(8,128)(2,1)S(1)}, u32[]{:S(2)}, u32[]{:S(2)}) %collective-permute-start.18) | collective-permute-done | bytes 262176 | tf_op jit(solution)/shard_map/ppermute | solution.py:459
  111.5 2.3 %collective-permute-start.17 = (bf16[512,128]{1,0:T(8,128)(2,1)S(1)}, bf16[512,128]{1,0:T(8,128)(2,1)S(1)}, u32[]{:S(2)}, u32[]{:S(2)}) collective-permute-start(bf16[512,128]{1,0:T(8,128)(2,1)S(1)} %fusion.11), channel_id=1, source_target_pairs={{0,16},{4,20},{8,24},{12,28},{16,0},{20,4},{24,8},{28,12},{1,17},{... | collective-permute-start | bytes 393224 | tf_op jit(solution)/shard_map/ppermute | solution.py:469
  114.0 4.2 %collective-permute-done.17 = bf16[512,128]{1,0:T(8,128)(2,1)S(1)} collective-permute-done((bf16[512,128]{1,0:T(8,128)(2,1)S(1)}, bf16[512,128]{1,0:T(8,128)(2,1)S(1)}, u32[]{:S(2)}, u32[]{:S(2)}) %collective-permute-start.17) | collective-permute-done | bytes 131104 | tf_op jit(solution)/shard_map/ppermute | solution.py:469
  118.2 2.3 %collective-permute-start.21 = (bf16[512,128]{1,0:T(8,128)(2,1)S(1)}, bf16[512,128]{1,0:T(8,128)(2,1)S(1)}, u32[]{:S(2)}, u32[]{:S(2)}) collective-permute-start(bf16[512,128]{1,0:T(8,128)(2,1)S(1)} %fusion.12), channel_id=1, source_target_pairs={{0,16},{4,20},{8,24},{12,28},{16,0},{20,4},{24,8},{28,12},{1,17},{... | collective-permute-start | bytes 393224 | tf_op jit(solution)/shard_map/ppermute | solution.py:469
  120.6 4.3 %collective-permute-done.21 = bf16[512,128]{1,0:T(8,128)(2,1)S(1)} collective-permute-done((bf16[512,128]{1,0:T(8,128)(2,1)S(1)}, bf16[512,128]{1,0:T(8,128)(2,1)S(1)}, u32[]{:S(2)}, u32[]{:S(2)}) %collective-permute-start.21) | collective-permute-done | bytes 131104 | tf_op jit(solution)/shard_map/ppermute | solution.py:469
  125.3 9.3 %collective-permute-start.22 = (bf16[128,256]{1,0:T(8,128)(2,1)S(1)}, bf16[128,256]{1,0:T(8,128)(2,1)S(1)}, u32[]{:S(2)}, u32[]{:S(2)}) collective-permute-start(bf16[128,256]{1,0:T(8,128)(2,1)S(1)} %get-tuple-element.49), channel_id=1, source_target_pairs={{0,96},{32,0},{64,32},{96,64},{1,97},{33,1},{65,33},{97,65},{2,98}... | collective-permute-start | bytes 196616 | tf_op jit(solution)/shard_map/ppermute | solution.py:497
  135.5 8.1 %collective-permute-start.29 = (bf16[128,4096]{1,0:T(8,128)(2,1)S(1)}, bf16[128,4096]{1,0:T(8,128)(2,1)S(1)}, u32[]{:S(2)}, u32[]{:S(2)}) collective-permute-start(bf16[128,4096]{1,0:T(8,128)(2,1)S(1)} %add_convert_fusion.1), channel_id=1, source_target_pairs={{0,99},{1,96},{2,97},{3,98},{32,3},{33,0},{34,1},{35,2},{64,35},{6... | collective-permute-start | bytes 3145736 | tf_op jit(solution)/shard_map/ppermute | solution.py:495
  144.6 2.3 %collective-permute-start.24 = (bf16[128,256]{1,0:T(8,128)(2,1)S(1)}, bf16[128,256]{1,0:T(8,128)(2,1)S(1)}, u32[]{:S(2)}, u32[]{:S(2)}) collective-permute-start(bf16[128,256]{1,0:T(8,128)(2,1)S(1)} %get-tuple-element.50), channel_id=1, source_target_pairs={{0,98},{1,99},{2,96},{3,97},{32,2},{33,3},{34,0},{35,1},{64,34},{6... | collective-permute-start | bytes 196616 | tf_op jit(solution)/shard_map/ppermute | solution.py:496
  146.9 2.4 %fusion.42 = f32[128,4096]{1,0:T(8,128)S(1)} fusion(bf16[128,256]{1,0:T(8,128)(2,1)S(1)} %collective-permute-done.22, bf16[4096,256]{1,0:T(8,128)(2,1)} %collective-permute-done.23), kind=kOutput, calls=%fused_computation.75 | convolution fusion | flops 268435456 | bytes 4259840 | tf_op jit(solution)/shard_map/dot_general | solution.py:21
  149.3 19.6 %collective-permute-done.24 = bf16[128,256]{1,0:T(8,128)(2,1)S(1)} collective-permute-done((bf16[128,256]{1,0:T(8,128)(2,1)S(1)}, bf16[128,256]{1,0:T(8,128)(2,1)S(1)}, u32[]{:S(2)}, u32[]{:S(2)}) %collective-permute-start.24) | collective-permute-done | bytes 65568 | tf_op jit(solution)/shard_map/ppermute | solution.py:496
  169.0 2.5 %add_add_fusion = f32[128,4096]{1,0:T(8,128)S(1)} fusion(f32[128,4096]{1,0:T(8,128)S(1)} %fusion.42, bf16[128,4096]{1,0:T(8,128)(2,1)S(1)} %collective-permute-done.13, bf16[128,256]{1,0:T(8,128)(2,1)S(1)} %collective-permute-done.24, bf16[4096,256]{1,0:T(8,128)(2,1)} %collective-permute-done.25), kind=kOutput, calls=%fused_computation.14 | convolution fusion | flops 270008320 | bytes 7405568 | tf_op jit(solution)/shard_map/dot_general | solution.py:21
  (97 shorter events, 25.8 us)
Async XLA Ops:
  1.8 14.0 %collective-permute-start.6 = (bf16[512,256]{1,0:T(8,128)(2,1)S(1)}, bf16[512,256]{1,0:T(8,128)(2,1)}, u32[]{:S(2)}, u32[]{:S(2)}) collective-permute-start(bf16[512,256]{1,0:T(8,128)(2,1)S(1)} %pad_maximum_fusion.1.refs_0_), channel_id=1, source_target_pairs={{0,16},{4,20},{8,24},{12,28},{16,0},{20,4},{24,8},{28,12},{1,17},{... | collective-permute-start | bytes 786440 | tf_op jit(solution)/shard_map/ppermute | solution.py:422
  5.4 13.9 %collective-permute-start.7 = (bf16[512,256]{1,0:T(8,128)(2,1)S(1)}, bf16[512,256]{1,0:T(8,128)(2,1)S(1)}, u32[]{:S(2)}, u32[]{:S(2)}) collective-permute-start(bf16[512,256]{1,0:T(8,128)(2,1)S(1)} %pad_maximum_fusion.1.refs_0_), channel_id=1, source_target_pairs={{0,12},{4,0},{8,4},{12,8},{16,28},{20,16},{24,20},{28,24},{1,13},{... | collective-permute-start | bytes 786440 | tf_op jit(solution)/shard_map/ppermute | solution.py:425
  9.2 14.4 %collective-permute-start.9 = (bf16[512,256]{1,0:T(8,128)(2,1)S(1)}, bf16[512,256]{1,0:T(8,128)(2,1)}, u32[]{:S(2)}, u32[]{:S(2)}) collective-permute-start(bf16[512,256]{1,0:T(8,128)(2,1)S(1)} %pad_maximum_fusion.1.refs_0_), channel_id=1, source_target_pairs={{0,8},{4,12},{8,0},{12,4},{16,24},{20,28},{24,16},{28,20},{1,9},{5... | collective-permute-start | bytes 786440 | tf_op jit(solution)/shard_map/ppermute | solution.py:425
  11.5 14.5 %collective-permute-start = (bf16[64,4096]{1,0:T(8,128)(2,1)}, bf16[64,4096]{1,0:T(8,128)(2,1)S(1)}, u32[]{:S(2)}, u32[]{:S(2)}) collective-permute-start(bf16[64,4096]{1,0:T(8,128)(2,1)} %get-tuple-element.48), channel_id=1, source_target_pairs={{0,1},{1,2},{2,3},{3,0},{4,5},{5,6},{6,7},{7,4},{8,9},{9,10},{10,1... | collective-permute-start | bytes 1572872 | tf_op jit(solution)/shard_map/ppermute | solution.py:414
  12.8 14.7 %collective-permute-start.3 = (bf16[64,4096]{1,0:T(8,128)(2,1)}, bf16[64,4096]{1,0:T(8,128)(2,1)S(1)}, u32[]{:S(2)}, u32[]{:S(2)}) collective-permute-start(bf16[64,4096]{1,0:T(8,128)(2,1)} %get-tuple-element.47), channel_id=1, source_target_pairs={{0,3},{1,0},{2,1},{3,2},{4,7},{5,4},{6,5},{7,6},{8,11},{9,8},{10,9... | collective-permute-start | bytes 1572872 | tf_op jit(solution)/shard_map/ppermute | solution.py:415
  15.8 8.2 %collective-permute-start.11 = (bf16[512,256]{1,0:T(8,128)(2,1)S(1)}, bf16[512,256]{1,0:T(8,128)(2,1)S(1)}, u32[]{:S(2)}, u32[]{:S(2)}) collective-permute-start(bf16[512,256]{1,0:T(8,128)(2,1)S(1)} %pad_maximum_fusion.1.refs_0_), channel_id=1, source_target_pairs={{0,4},{4,8},{8,12},{12,0},{16,20},{20,24},{24,28},{28,16},{1,5},{5... | collective-permute-start | bytes 786440 | tf_op jit(solution)/shard_map/ppermute | solution.py:425
  20.1 7.7 %collective-permute-start.8 = (bf16[512,256]{1,0:T(8,128)(2,1)}, bf16[512,256]{1,0:T(8,128)(2,1)S(1)}, u32[]{:S(2)}, u32[]{:S(2)}) collective-permute-start(bf16[512,256]{1,0:T(8,128)(2,1)} %collective-permute-done.6.refs_1_), channel_id=1, source_target_pairs={{0,12},{4,0},{8,4},{12,8},{16,28},{20,16},{24,20},{28,24},{1,13},{... | collective-permute-start | bytes 786440 | tf_op jit(solution)/shard_map/ppermute | solution.py:427
  23.6 7.5 %collective-permute-start.10 = (bf16[512,256]{1,0:T(8,128)(2,1)}, bf16[512,256]{1,0:T(8,128)(2,1)S(1)}, u32[]{:S(2)}, u32[]{:S(2)}) collective-permute-start(bf16[512,256]{1,0:T(8,128)(2,1)} %collective-permute-done.9.refs_4_), channel_id=1, source_target_pairs={{0,16},{4,20},{8,24},{12,28},{16,0},{20,4},{24,8},{28,12},{1,17},{... | collective-permute-start | bytes 786440 | tf_op jit(solution)/shard_map/ppermute | solution.py:428
  24.7 28.5 %collective-permute-start.1 = (bf16[64,4096]{1,0:T(8,128)(2,1)}, bf16[64,4096]{1,0:T(8,128)(2,1)S(1)}, u32[]{:S(2)}, u32[]{:S(2)}) collective-permute-start(bf16[64,4096]{1,0:T(8,128)(2,1)} %get-tuple-element.47), channel_id=1, source_target_pairs={{0,1},{1,2},{2,3},{3,0},{4,5},{5,6},{6,7},{7,4},{8,9},{9,10},{10,1... | collective-permute-start | bytes 1572872 | tf_op jit(solution)/shard_map/ppermute | solution.py:418
  26.0 28.9 %collective-permute-start.2 = (bf16[64,4096]{1,0:T(8,128)(2,1)}, bf16[64,4096]{1,0:T(8,128)(2,1)S(1)}, u32[]{:S(2)}, u32[]{:S(2)}) collective-permute-start(bf16[64,4096]{1,0:T(8,128)(2,1)} %get-tuple-element.48), channel_id=1, source_target_pairs={{0,3},{1,0},{2,1},{3,2},{4,7},{5,4},{6,5},{7,6},{8,11},{9,8},{10,9... | collective-permute-start | bytes 1572872 | tf_op jit(solution)/shard_map/ppermute | solution.py:419
  27.4 7.6 %collective-permute-start.12 = (bf16[512,256]{1,0:T(8,128)(2,1)}, bf16[512,256]{1,0:T(8,128)(2,1)}, u32[]{:S(2)}, u32[]{:S(2)}) collective-permute-start(bf16[512,256]{1,0:T(8,128)(2,1)} %collective-permute-done.6.refs_1_), channel_id=1, source_target_pairs={{0,4},{4,8},{8,12},{12,0},{16,20},{20,24},{24,28},{28,16},{1,5},{5... | collective-permute-start | bytes 786440 | tf_op jit(solution)/shard_map/ppermute | solution.py:427
  28.5 26.4 %collective-permute-start.4 = (bf16[64,4096]{1,0:T(8,128)(2,1)S(1)}, bf16[64,4096]{1,0:T(8,128)(2,1)S(1)}, u32[]{:S(2)}, u32[]{:S(2)}) collective-permute-start(bf16[64,4096]{1,0:T(8,128)(2,1)S(1)} %collective-permute-done.refs_1_), channel_id=1, source_target_pairs={{0,1},{1,2},{2,3},{3,0},{4,5},{5,6},{6,7},{7,4},{8,9},{9,10},{10,1... | collective-permute-start | bytes 1572872 | tf_op jit(solution)/shard_map/ppermute | solution.py:416
  31.9 23.0 %collective-permute-start.5 = (bf16[64,4096]{1,0:T(8,128)(2,1)S(1)}, bf16[64,4096]{1,0:T(8,128)(2,1)}, u32[]{:S(2)}, u32[]{:S(2)}) collective-permute-start(bf16[64,4096]{1,0:T(8,128)(2,1)S(1)} %collective-permute-done.3.refs_4_), channel_id=1, source_target_pairs={{0,3},{1,0},{2,1},{3,2},{4,7},{5,4},{6,5},{7,6},{8,11},{9,8},{10,9... | collective-permute-start | bytes 1572872 | tf_op jit(solution)/shard_map/ppermute | solution.py:417
  35.1 109.5 %collective-permute-start.23 = (bf16[4096,256]{1,0:T(8,128)(2,1)}, bf16[4096,256]{1,0:T(8,128)(2,1)}, u32[]{:S(2)}, u32[]{:S(2)}) collective-permute-start(bf16[4096,256]{1,0:T(8,128)(2,1)} %pad_maximum_fusion), channel_id=1, source_target_pairs={{0,96},{32,0},{64,32},{96,64},{1,97},{33,1},{65,33},{97,65},{2,98}... | collective-permute-start | bytes 6291464 | tf_op jit(solution)/shard_map/ppermute | solution.py:435
  53.2 115.8 %collective-permute-start.25 = (bf16[4096,256]{1,0:T(8,128)(2,1)}, bf16[4096,256]{1,0:T(8,128)(2,1)}, u32[]{:S(2)}, u32[]{:S(2)}) collective-permute-start(bf16[4096,256]{1,0:T(8,128)(2,1)} %pad_maximum_fusion), channel_id=1, source_target_pairs={{0,98},{1,99},{2,96},{3,97},{32,2},{33,3},{34,0},{35,1},{64,34},{6... | collective-permute-start | bytes 6291464 | tf_op jit(solution)/shard_map/ppermute | solution.py:436
  84.0 6.6 %collective-permute-start.16 = (bf16[2,512,128]{2,1,0:T(8,128)(2,1)S(1)}, bf16[2,512,128]{2,1,0:T(8,128)(2,1)S(1)}, u32[]{:S(2)}, u32[]{:S(2)}) collective-permute-start(bf16[2,512,128]{2,1,0:T(8,128)(2,1)S(1)} %get-tuple-element.38), channel_id=1, source_target_pairs={{0,12},{4,0},{8,4},{12,8},{16,28},{20,16},{24,20},{28,24},{1,13},{... | collective-permute-start | bytes 786440 | tf_op jit(solution)/shard_map/ppermute | solution.py:459
  84.9 9.2 %collective-permute-start.15 = (bf16[2,512,128]{2,1,0:T(8,128)(2,1)S(1)}, bf16[2,512,128]{2,1,0:T(8,128)(2,1)S(1)}, u32[]{:S(2)}, u32[]{:S(2)}) collective-permute-start(bf16[2,512,128]{2,1,0:T(8,128)(2,1)S(1)} %get-tuple-element.37), channel_id=1, source_target_pairs={{0,8},{4,12},{8,0},{12,4},{16,24},{20,28},{24,16},{28,20},{1,9},{5... | collective-permute-start | bytes 786440 | tf_op jit(solution)/shard_map/ppermute | solution.py:459
  85.0 16.5 %collective-permute-start.14 = (bf16[2,512,128]{2,1,0:T(8,128)(2,1)S(1)}, bf16[2,512,128]{2,1,0:T(8,128)(2,1)S(1)}, u32[]{:S(2)}, u32[]{:S(2)}) collective-permute-start(bf16[2,512,128]{2,1,0:T(8,128)(2,1)S(1)} %get-tuple-element.36), channel_id=1, source_target_pairs={{0,4},{4,8},{8,12},{12,0},{16,20},{20,24},{24,28},{28,16},{1,5},{5... | collective-permute-start | bytes 786440 | tf_op jit(solution)/shard_map/ppermute | solution.py:459
  90.6 11.2 %collective-permute-start.20 = (bf16[2,512,128]{2,1,0:T(8,128)(2,1)S(1)}, bf16[2,512,128]{2,1,0:T(8,128)(2,1)S(1)}, u32[]{:S(2)}, u32[]{:S(2)}) collective-permute-start(bf16[2,512,128]{2,1,0:T(8,128)(2,1)S(1)} %get-tuple-element.42), channel_id=1, source_target_pairs={{0,12},{4,0},{8,4},{12,8},{16,28},{20,16},{24,20},{28,24},{1,13},{... | collective-permute-start | bytes 786440 | tf_op jit(solution)/shard_map/ppermute | solution.py:459
  94.2 10.6 %collective-permute-start.19 = (bf16[2,512,128]{2,1,0:T(8,128)(2,1)S(1)}, bf16[2,512,128]{2,1,0:T(8,128)(2,1)S(1)}, u32[]{:S(2)}, u32[]{:S(2)}) collective-permute-start(bf16[2,512,128]{2,1,0:T(8,128)(2,1)S(1)} %get-tuple-element.41), channel_id=1, source_target_pairs={{0,8},{4,12},{8,0},{12,4},{16,24},{20,28},{24,16},{28,20},{1,9},{5... | collective-permute-start | bytes 786440 | tf_op jit(solution)/shard_map/ppermute | solution.py:459
  101.5 10.0 %collective-permute-start.18 = (bf16[2,512,128]{2,1,0:T(8,128)(2,1)S(1)}, bf16[2,512,128]{2,1,0:T(8,128)(2,1)S(1)}, u32[]{:S(2)}, u32[]{:S(2)}) collective-permute-start(bf16[2,512,128]{2,1,0:T(8,128)(2,1)S(1)} %get-tuple-element.40), channel_id=1, source_target_pairs={{0,4},{4,8},{8,12},{12,0},{16,20},{20,24},{24,28},{28,16},{1,5},{5... | collective-permute-start | bytes 786440 | tf_op jit(solution)/shard_map/ppermute | solution.py:459
  101.6 33.0 %copy-start.13 = (bf16[1,4096,128]{2,1,0:T(8,128)(2,1)S(1)}, bf16[1,4096,128]{2,1,0:T(8,128)(2,1)}, u32[]{:S(2)}) copy-start(bf16[1,4096,128]{2,1,0:T(8,128)(2,1)} %param.16) | copy-start | bytes 3145732
  101.6 33.0 %copy-start.15 = (bf16[1,4096,128]{2,1,0:T(8,128)(2,1)S(1)}, bf16[1,4096,128]{2,1,0:T(8,128)(2,1)}, u32[]{:S(2)}) copy-start(bf16[1,4096,128]{2,1,0:T(8,128)(2,1)} %param.15) | copy-start | bytes 3145732
  101.8 23.5 %collective-permute-start.28 = (bf16[64,4096]{1,0:T(8,128)(2,1)S(1)}, bf16[64,4096]{1,0:T(8,128)(2,1)S(1)}, u32[]{:S(2)}, u32[]{:S(2)}) collective-permute-start(bf16[64,4096]{1,0:T(8,128)(2,1)S(1)} %get-tuple-element.46), channel_id=1, source_target_pairs={{0,3},{1,0},{2,1},{3,2},{4,7},{5,4},{6,5},{7,6},{8,11},{9,8},{10,9... | collective-permute-start | bytes 1572872 | tf_op jit(solution)/shard_map/ppermute | solution.py:480
  104.8 64.2 %collective-permute-start.13 = (bf16[128,4096]{1,0:T(8,128)(2,1)S(1)}, bf16[128,4096]{1,0:T(8,128)(2,1)S(1)}, u32[]{:S(2)}, u32[]{:S(2)}) collective-permute-start(bf16[128,4096]{1,0:T(8,128)(2,1)S(1)} %convolution_convert_fusion.1), channel_id=1, source_target_pairs={{0,96},{32,0},{64,32},{96,64},{1,97},{33,1},{65,33},{97,65},{2,98}... | collective-permute-start | bytes 3145736 | tf_op jit(solution)/shard_map/ppermute | solution.py:482
  111.5 6.7 %collective-permute-start.17 = (bf16[512,128]{1,0:T(8,128)(2,1)S(1)}, bf16[512,128]{1,0:T(8,128)(2,1)S(1)}, u32[]{:S(2)}, u32[]{:S(2)}) collective-permute-start(bf16[512,128]{1,0:T(8,128)(2,1)S(1)} %fusion.11), channel_id=1, source_target_pairs={{0,16},{4,20},{8,24},{12,28},{16,0},{20,4},{24,8},{28,12},{1,17},{... | collective-permute-start | bytes 393224 | tf_op jit(solution)/shard_map/ppermute | solution.py:469
  118.2 6.7 %collective-permute-start.21 = (bf16[512,128]{1,0:T(8,128)(2,1)S(1)}, bf16[512,128]{1,0:T(8,128)(2,1)S(1)}, u32[]{:S(2)}, u32[]{:S(2)}) collective-permute-start(bf16[512,128]{1,0:T(8,128)(2,1)S(1)} %fusion.12), channel_id=1, source_target_pairs={{0,16},{4,20},{8,24},{12,28},{16,0},{20,4},{24,8},{28,12},{1,17},{... | collective-permute-start | bytes 393224 | tf_op jit(solution)/shard_map/ppermute | solution.py:469
  124.9 10.6 %collective-permute-start.26 = (bf16[64,4096]{1,0:T(8,128)(2,1)S(1)}, bf16[64,4096]{1,0:T(8,128)(2,1)S(1)}, u32[]{:S(2)}, u32[]{:S(2)}) collective-permute-start(bf16[64,4096]{1,0:T(8,128)(2,1)S(1)} %get-tuple-element.45), channel_id=1, source_target_pairs={{0,1},{1,2},{2,3},{3,0},{4,5},{5,6},{6,7},{7,4},{8,9},{9,10},{10,1... | collective-permute-start | bytes 1572872 | tf_op jit(solution)/shard_map/ppermute | solution.py:479
  125.3 19.2 %collective-permute-start.22 = (bf16[128,256]{1,0:T(8,128)(2,1)S(1)}, bf16[128,256]{1,0:T(8,128)(2,1)S(1)}, u32[]{:S(2)}, u32[]{:S(2)}) collective-permute-start(bf16[128,256]{1,0:T(8,128)(2,1)S(1)} %get-tuple-element.49), channel_id=1, source_target_pairs={{0,96},{32,0},{64,32},{96,64},{1,97},{33,1},{65,33},{97,65},{2,98}... | collective-permute-start | bytes 196616 | tf_op jit(solution)/shard_map/ppermute | solution.py:497
  135.5 35.9 %collective-permute-start.29 = (bf16[128,4096]{1,0:T(8,128)(2,1)S(1)}, bf16[128,4096]{1,0:T(8,128)(2,1)S(1)}, u32[]{:S(2)}, u32[]{:S(2)}) collective-permute-start(bf16[128,4096]{1,0:T(8,128)(2,1)S(1)} %add_convert_fusion.1), channel_id=1, source_target_pairs={{0,99},{1,96},{2,97},{3,98},{32,3},{33,0},{34,1},{35,2},{64,35},{6... | collective-permute-start | bytes 3145736 | tf_op jit(solution)/shard_map/ppermute | solution.py:495
  144.5 27.0 %collective-permute-start.27 = (bf16[128,4096]{1,0:T(8,128)(2,1)S(1)}, bf16[128,4096]{1,0:T(8,128)(2,1)S(1)}, u32[]{:S(2)}, u32[]{:S(2)}) collective-permute-start(bf16[128,4096]{1,0:T(8,128)(2,1)S(1)} %add_convert_fusion.2), channel_id=1, source_target_pairs={{0,97},{1,98},{2,99},{3,96},{32,1},{33,2},{34,3},{35,0},{64,33},{6... | collective-permute-start | bytes 3145736 | tf_op jit(solution)/shard_map/ppermute | solution.py:494
  144.6 24.4 %collective-permute-start.24 = (bf16[128,256]{1,0:T(8,128)(2,1)S(1)}, bf16[128,256]{1,0:T(8,128)(2,1)S(1)}, u32[]{:S(2)}, u32[]{:S(2)}) collective-permute-start(bf16[128,256]{1,0:T(8,128)(2,1)S(1)} %get-tuple-element.50), channel_id=1, source_target_pairs={{0,98},{1,99},{2,96},{3,97},{32,2},{33,3},{34,0},{35,1},{64,34},{6... | collective-permute-start | bytes 196616 | tf_op jit(solution)/shard_map/ppermute | solution.py:496
  (17 other events, 156.8 us)

commit v3 on v1

--- a/solution.py
+++ b/solution.py
@@ -14,6 +14,7 @@
 NEG_LARGE = -1e30
 
 VMEM_WHOLE = pl.BlockSpec(memory_space=pltpu.VMEM)
+TP, CTX, SECTION = "tp", "ctx", "section"
 PARAMS = pltpu.CompilerParams(vmem_limit_bytes=36 << 20)
 
 
@@ -163,7 +164,6 @@
             bytes_accessed=13 << 20,
             transcendentals=STEPS * wide * BLK,
         ),
-        name="attn_forward",
     )(split, ids, *kv_chunks, queries)
 
 
@@ -387,7 +387,6 @@
         cost_estimate=pl.CostEstimate(
             flops=2 * 3 * STEPS * wide * BLK * HD, bytes_accessed=14 << 20, transcendentals=0
         ),
-        name="attn_key_grad",
     )(split, ids, grad, queries, probs, kv_sorted, kv_sorted, outs, stats, hist)
 
 
@@ -403,27 +402,32 @@
     output_weight,
 ):
     send = lax.ppermute
-    tp = lax.axis_index("tp")
-    ctx = lax.axis_index("ctx")
+    tp = lax.axis_index(TP)
+    ctx = lax.axis_index(CTX)
     own_x, own_z = ctx // 4, ctx % 4
     bf16 = jnp.bfloat16
 
     chunk = out_grad[0]
     half_rows = chunk.shape[0] // 2
     top, low = chunk[:half_rows], chunk[half_rows:]
-    left_top = send(top, "tp", ring(4, 1))
-    right_low = send(low, "tp", ring(4, -1))
-    far_top = send(left_top, "tp", ring(4, 1))
-    far_low = send(right_low, "tp", ring(4, -1))
-    left_low = send(low, "tp", ring(4, 1))
-    right_top = send(top, "tp", ring(4, -1))
+    left_top = send(top, TP, ring(4, 1))
+    right_low = send(low, TP, ring(4, -1))
+    far_top = send(left_top, TP, ring(4, 1))
+    far_low = send(right_low, TP, ring(4, -1))
+    left_low = send(low, TP, ring(4, 1))
+    right_top = send(top, TP, ring(4, -1))
 
     kv_own = jnp.concatenate([key_rows[0], value_rows[0]], axis=1)
-    kv_pair = send(kv_own, "ctx", X_SWAP)
+    kv_pair = send(kv_own, CTX, X_SWAP)
+    along, crossed = {}, {}
+    for distance, shift in ((2, 2), (1, -1), (3, 1)):
+        along[distance] = send(kv_own, CTX, z_ring(shift))
+    for distance, shift in ((1, -1), (3, 1)):
+        crossed[distance] = send(kv_pair, CTX, z_ring(shift))
+    crossed[2] = send(along[2], CTX, X_SWAP)
     kv_chunks = [kv_own, kv_pair]
-    for shift in (-1, 2, 1):
-        kv_chunks.append(send(kv_own, "ctx", z_ring(shift)))
-        kv_chunks.append(send(kv_pair, "ctx", z_ring(shift)))
+    for distance in (1, 2, 3):
+        kv_chunks += [along[distance], crossed[distance]]
 
     index = jnp.arange(8, dtype=jnp.int32)
     source = ((own_x + index % 2) % 2) * 4 + (own_z + index // 2) % 4
@@ -446,7 +450,7 @@
     def along_z(groups):
         total = groups[0].astype(f32)
         for distance, shift in ((1, 1), (2, 2), (3, -1)):
-            received = send(groups[distance], "ctx", z_ring(shift))
+            received = send(groups[distance], CTX, z_ring(shift))
             total = total + received.astype(f32)
         return total
 
@@ -456,7 +460,7 @@
     key_sum = along_z(groups)
 
     def with_pair(total):
-        received = send(total[1].astype(bf16), "ctx", X_SWAP)
+        received = send(total[1].astype(bf16), CTX, X_SWAP)
         return (total[0] + received.astype(f32)).astype(bf16)
 
     value_grad = with_pair(value_sum)
@@ -471,15 +475,15 @@
         return dot_nt(rows, weights).astype(bf16)
 
     far = term_of(2)
-    from_left = send(far[:half_rows], "tp", ring(4, 1))
-    from_right = send(far[half_rows:], "tp", ring(4, -1))
+    from_left = send(far[:half_rows], TP, ring(4, 1))
+    from_right = send(far[half_rows:], TP, ring(4, -1))
     own_term = term_of(0)
-    own = send(own_term, "section", ring(4, -1))
+    own = send(own_term, SECTION, ring(4, -1))
     right, left = lax.optimization_barrier((term_of(1), term_of(3)))
     empty = jnp.zeros_like(from_left, dtype=f32)
     right = (right.astype(f32) + jnp.concatenate([from_left.astype(f32), empty])).astype(bf16)
     left = (left.astype(f32) + jnp.concatenate([empty, from_right.astype(f32)])).astype(bf16)
-    joint = ("section", "tp")
+    joint = (SECTION, TP)
     part_a = send(right, joint, joint_ring(1))
     part_b = send(left, joint, joint_ring(-1))
     sent = (own.astype(f32) + part_a.astype(f32) + part_b.astype(f32)).astype(bf16)
@@ -489,14 +493,14 @@
 def solution(mesh):
     placed = (
         P(),
-        P("section", "ctx", "tp"),
-        P("section", "ctx", "tp"),
-        P("section", "ctx", "tp"),
-        P("section", ("ctx", "tp"), None),
-        P("section", None, "tp"),
-        P("section", None, "tp"),
-        P("section", None, "tp"),
-        P("section", "tp", None),
+        P(SECTION, CTX, TP),
+        P(SECTION, CTX, TP),
+        P(SECTION, CTX, TP),
+        P(SECTION, (CTX, TP), None),
+        P(SECTION, None, TP),
+        P(SECTION, None, TP),
+        P(SECTION, None, TP),
+        P(SECTION, TP, None),
     )
 
     return jax.shard_map(
@@ -504,9 +508,9 @@
         mesh=mesh,
         in_specs=placed,
         out_specs=(
-            P("section", ("ctx", "tp"), None),
-            P("section", "ctx", "tp"),
-            P("section", "ctx", "tp"),
+            P(SECTION, (CTX, TP), None),
+            P(SECTION, CTX, TP),
+            P(SECTION, CTX, TP),
         ),
         check_vma=False,
     )

time: 161 us -> 154 us (0.957)
  waiting for transfers between devices: 55.8 us -> 50.8 us
  local copies, waits for them, and re-layouts: 12.4 us -> 10.5 us
    ppermute x24, waiting for transfers between devices: 31.3 us -> 26.7 us  [the longest x6 9.42 us: along_z(): received = send(groups[distance], CTX, z_ring(shift))]
    ppermute x1, waiting for transfers between devices: 16.7 us -> 14.7 us  [per_device(): part_b = send(left, joint, joint_ring(-1))]
    ppermute x1, starting transfers between devices: 6.56 us -> 4.52 us  [per_device(): part_b = send(left, joint, joint_ring(-1))]
    unnamed x38 -> x36, local copies, waits for them, and re-layouts: 9.75 us -> 8.1 us
  transfers between devices with their start and end apart: 26 -> 26, of which waited for: 9 -> 10; matrix products, arithmetic and copies ran while one was open for 5% -> 6% of each run, Pallas kernels for 14% -> 15%
where the time goes in v3:
time: 154 us
  waiting for transfers between devices  50.8 us (33%)
  starting transfers between devices  42.3 us (27%)
  Pallas kernels  35.7 us (23%)
  local copies, waits for them, and re-layouts  10.5 us (7%)
  matrix products  9.33 us (6%)
  other arithmetic  4.16 us (3%)
    ppermute x1, waiting for transfers between devices, per_device(): part_b = send(left, joint, joint_ring(-1))  14.7 us
    pallas_call x1, Pallas kernels, key_call(): pl.pallas_call(key_kernel, grid_spec=pltpu.PrefetchScalarGridSpec(num_sca...  11.8 us
    pallas_call x1, Pallas kernels, forward_call(): pl.pallas_call(forward_kernel, grid_spec=pltpu.PrefetchScalarGridSpec(num...  10.7 us
    ppermute x6, waiting for transfers between devices, along_z(): received = send(groups[distance], CTX, z_ring(shift))  9.42 us
    ppermute x1, waiting for transfers between devices, per_device(): part_a = send(right, joint, joint_ring(1))  9.41 us
    dot_general x4, matrix products, dot_nt(): lax.dot_general(lhs, rhs, (((1,), (1,)), ((), ())), preferred_element_typ...  9.33 us
    unnamed x36, local copies, waits for them, and re-layouts  8.1 us
    pallas_call x1, Pallas kernels, grad_call(): pl.pallas_call(grad_kernel, grid_spec=pltpu.PrefetchScalarGridSpec(num_sc...  6.93 us
  transfers between devices with their start and end apart: 26, of which 10 were waited for; matrix products, arithmetic and copies ran while one was open for 6% of the time, Pallas kernels for 15%

profile of v3, /device:TPU:1, one launch (start us, length us, event | category | flops | bytes accessed | tf_op | source)
XLA Modules:
  0.0 153.8 jit_solution(18239591591626915631)
XLA Ops:
  1.7 3.6 %collective-permute-start.6 = (bf16[512,256]{1,0:T(8,128)(2,1)S(1)}, bf16[512,256]{1,0:T(8,128)(2,1)}, u32[]{:S(2)}, u32[]{:S(2)}) collective-permute-start(bf16[512,256]{1,0:T(8,128)(2,1)S(1)} %pad_maximum_fusion.2.refs_0_), channel_id=1, source_target_pairs={{0,16},{4,20},{8,24},{12,28},{16,0},{20,4},{24,8},{28,12},{1,17},{... | collective-permute-start | bytes 786440 | tf_op jit(solution)/shard_map/ppermute | solution.py:421
  5.4 3.8 %collective-permute-start.7 = (bf16[512,256]{1,0:T(8,128)(2,1)S(1)}, bf16[512,256]{1,0:T(8,128)(2,1)S(1)}, u32[]{:S(2)}, u32[]{:S(2)}) collective-permute-start(bf16[512,256]{1,0:T(8,128)(2,1)S(1)} %pad_maximum_fusion.2.refs_0_), channel_id=1, source_target_pairs={{0,12},{4,0},{8,4},{12,8},{16,28},{20,16},{24,20},{28,24},{1,13},{... | collective-permute-start | bytes 786440 | tf_op jit(solution)/shard_map/ppermute | solution.py:424
  9.1 2.1 %slice_bitcast_fusion = (bf16[64,4096]{1,0:T(8,128)(2,1)}, bf16[64,4096]{1,0:T(8,128)(2,1)S(1)}) fusion(bf16[1,128,4096]{2,1,0:T(8,128)(2,1)} %param.13), kind=kLoop, calls=%fused_computation.12 | loop fusion | bytes 2097152 | tf_op jit(solution)/shard_map/slice | solution.py:412
  11.2 1.3 collective-permute-start
  12.5 1.4 collective-permute-start.3
  14.7 4.7 %collective-permute-done.7.refs_2_ = bf16[512,256]{1,0:T(8,128)(2,1)S(1)} collective-permute-done((bf16[512,256]{1,0:T(8,128)(2,1)S(1)}, bf16[512,256]{1,0:T(8,128)(2,1)S(1)}, u32[]{:S(2)}, u32[]{:S(2)}) %collective-permute-start.7) | collective-permute-done | bytes 262176 | tf_op jit(solution)/shard_map/ppermute | solution.py:424
  20.0 3.6 %collective-permute-start.8 = (bf16[512,256]{1,0:T(8,128)(2,1)}, bf16[512,256]{1,0:T(8,128)(2,1)S(1)}, u32[]{:S(2)}, u32[]{:S(2)}) collective-permute-start(bf16[512,256]{1,0:T(8,128)(2,1)} %collective-permute-done.6.refs_1_), channel_id=1, source_target_pairs={{0,12},{4,0},{8,4},{12,8},{16,28},{20,16},{24,20},{28,24},{1,13},{... | collective-permute-start | bytes 786440 | tf_op jit(solution)/shard_map/ppermute | solution.py:426
  24.6 1.3 collective-permute-start.1
  26.0 1.5 collective-permute-start.2
  29.8 1.3 collective-permute-done.10.refs_5_
  31.8 2.7 %collective-permute-start.5 = (bf16[64,4096]{1,0:T(8,128)(2,1)S(1)}, bf16[64,4096]{1,0:T(8,128)(2,1)}, u32[]{:S(2)}, u32[]{:S(2)}) collective-permute-start(bf16[64,4096]{1,0:T(8,128)(2,1)S(1)} %collective-permute-done.3.refs_4_), channel_id=1, source_target_pairs={{0,3},{1,0},{2,1},{3,2},{4,7},{5,4},{6,5},{7,6},{8,11},{9,8},{10,9... | collective-permute-start | bytes 1572872 | tf_op jit(solution)/shard_map/ppermute | solution.py:416
  40.9 10.7 %shard_map.112 = (bf16[17,4,256,256]{3,2,1,0:T(8,128)(2,1)S(1)}, f32[2,128,1024]{2,1,0:T(8,128)S(1)}, f32[2,8,1024]{2,1,0:T(8,128)S(1)}, f32[17,1,1024]{2,1,0:T(1,128)S(1)}, bf16[16,256,256]{2,1,0:T(8,128)(2,1)S(1)}) custom-call(s32[1]{0:T(128)S(1)} %bitcast.44, s32[16]{0:T(128)S(1)} %reshape.84.ids_ref, bf16[512,256]{1,0:T(8,128)(2,1)S(1)} %pad_maximum_fusion.2.refs_0_, ...), custom_call_target="tpu_custom_call" | custom-call | flops 2281701376 | bytes 13631488 | tf_op jit(solution)/shard_map/pallas_call | solution.py:131
  51.7 6.9 %attn_grad.1.grad_ref = bf16[512,512]{1,0:T(8,128)(2,1)S(1)} custom-call(s32[7]{0:T(128)S(1)} %broadcast_multiply_fusion.rows_ref, bf16[128,4096]{1,0:T(8,128)(2,1)S(1)} %bitcast.40, bf16[64,4096]{1,0:T(8,128)(2,1)S(1)} %collective-permute-done.refs_1_, bf16[64,4096]{1,0:T(8,128)(2,1)S(1)} %collective-permute-done.1.refs_2_, ...), custom_call_target="tpu_custom_call" | custom-call | flops 2147483648 | bytes 9437184 | tf_op jit(solution)/shard_map/attn_grad/pallas_call | solution.py:194
  58.6 6.2 %attn_value_grad.1 = (bf16[2,512,128]{2,1,0:T(8,128)(2,1)S(1)}, bf16[2,512,128]{2,1,0:T(8,128)(2,1)S(1)}, bf16[2,512,128]{2,1,0:T(8,128)(2,1)S(1)}, bf16[2,512,128]{2,1,0:T(8,128)(2,1)S(1)}) custom-call(s32[1]{0:T(128)S(1)} %bitcast.45, s32[16]{0:T(128)S(1)} %reshape.84.ids_ref, bf16[512,512]{1,0:T(8,128)(2,1)S(1)} %attn_grad.1.grad_ref, ...), custom_call_target="tpu_custom_call" | custom-call | flops 1140850688 | bytes 11534336 | tf_op jit(solution)/shard_map/attn_value_grad/pallas_call | solution.py:260
  66.4 11.8 %shard_map.113 = (bf16[512,512]{1,0:T(8,128)(2,1)S(1)}, bf16[2,512,128]{2,1,0:T(8,128)(2,1)S(1)}, bf16[2,512,128]{2,1,0:T(8,128)(2,1)S(1)}, bf16[2,512,128]{2,1,0:T(8,128)(2,1)S(1)}, bf16[2,512,128]{2,1,0:T(8,128)(2,1)S(1)}) custom-call(s32[1]{0:T(128)S(1)} %bitcast.46, s32[16]{0:T(128)S(1)} %reshape.84.ids_ref, bf16[512,512]{1,0:T(8,128)(2,1)S(1)} %attn_grad.1.grad_ref, ...), custom_call_target="tpu_custom_call" | custom-call | flops 3422552064 | bytes 14680064 | tf_op jit(solution)/shard_map/pallas_call | solution.py:359
  78.3 2.5 %collective-permute-start.15 = (bf16[2,512,128]{2,1,0:T(8,128)(2,1)S(1)}, bf16[2,512,128]{2,1,0:T(8,128)(2,1)S(1)}, u32[]{:S(2)}, u32[]{:S(2)}) collective-permute-start(bf16[2,512,128]{2,1,0:T(8,128)(2,1)S(1)} %get-tuple-element.38), channel_id=1, source_target_pairs={{0,12},{4,0},{8,4},{12,8},{16,28},{20,16},{24,20},{28,24},{1,13},{... | collective-permute-start | bytes 786440 | tf_op jit(solution)/shard_map/ppermute | solution.py:453
  84.1 1.8 %collective-permute-done.15 = bf16[2,512,128]{2,1,0:T(8,128)(2,1)S(1)} collective-permute-done((bf16[2,512,128]{2,1,0:T(8,128)(2,1)S(1)}, bf16[2,512,128]{2,1,0:T(8,128)(2,1)S(1)}, u32[]{:S(2)}, u32[]{:S(2)}) %collective-permute-start.15) | collective-permute-done | bytes 262176 | tf_op jit(solution)/shard_map/ppermute | solution.py:453
  85.9 1.6 %collective-permute-done.14 = bf16[2,512,128]{2,1,0:T(8,128)(2,1)S(1)} collective-permute-done((bf16[2,512,128]{2,1,0:T(8,128)(2,1)S(1)}, bf16[2,512,128]{2,1,0:T(8,128)(2,1)S(1)}, u32[]{:S(2)}, u32[]{:S(2)}) %collective-permute-start.14) | collective-permute-done | bytes 262176 | tf_op jit(solution)/shard_map/ppermute | solution.py:453
  87.5 6.0 %collective-permute-done.13 = bf16[2,512,128]{2,1,0:T(8,128)(2,1)S(1)} collective-permute-done((bf16[2,512,128]{2,1,0:T(8,128)(2,1)S(1)}, bf16[2,512,128]{2,1,0:T(8,128)(2,1)S(1)}, u32[]{:S(2)}, u32[]{:S(2)}) %collective-permute-start.13) | collective-permute-done | bytes 262176 | tf_op jit(solution)/shard_map/ppermute | solution.py:453
  94.0 5.2 %collective-permute-done.16 = bf16[512,128]{1,0:T(8,128)(2,1)S(1)} collective-permute-done((bf16[512,128]{1,0:T(8,128)(2,1)S(1)}, bf16[512,128]{1,0:T(8,128)(2,1)S(1)}, u32[]{:S(2)}, u32[]{:S(2)}) %collective-permute-start.16) | collective-permute-done | bytes 131104 | tf_op jit(solution)/shard_map/ppermute | solution.py:463
  99.4 2.3 %convolution_convert_fusion.2 = bf16[128,4096]{1,0:T(8,128)(2,1)S(1)} fusion(bf16[512,768]{1,0:T(8,128)(2,1)S(1)} %pad_maximum_fusion.1, s32[]{:T(128)S(6)} %select_n.96, bf16[4096,128]{1,0:T(8,128)(2,1)S(1)} %bitcast.55, bf16[4096,128]{1,0:T(8,128)(2,1)S(1)} %bitcast.59, bf16[4096,512]{1,0:T(8,128)(2,1)S(1)} %bitcast.51), kind=kOutput, calls=%fused_computation.3 | convolution fusion | flops 824705024 | bytes 7536644 | tf_op jit(solution)/shard_map/dot_general | solution.py:22
  101.8 2.3 %convolution_convert_fusion = bf16[128,4096]{1,0:T(8,128)(2,1)S(1)} fusion(bf16[512,768]{1,0:T(8,128)(2,1)S(1)} %pad_maximum_fusion.1, s32[]{:T(128)S(6)} %select_n.98, bf16[4096,128]{1,0:T(8,128)(2,1)S(1)} %bitcast.56, bf16[4096,128]{1,0:T(8,128)(2,1)S(1)} %bitcast.60, bf16[4096,512]{1,0:T(8,128)(2,1)S(1)} %bitcast.52), kind=kOutput, calls=%fused_computation.1 | convolution fusion | flops 824705024 | bytes 7536644 | tf_op jit(solution)/shard_map/dot_general | solution.py:22
  104.3 2.3 %convolution_convert_fusion.1 = bf16[128,4096]{1,0:T(8,128)(2,1)S(1)} fusion(bf16[512,768]{1,0:T(8,128)(2,1)S(1)} %pad_maximum_fusion.1, s32[]{:T(128)S(6)} %select_n.97, bf16[4096,128]{1,0:T(8,128)(2,1)S(1)} %bitcast.57, bf16[4096,128]{1,0:T(8,128)(2,1)S(1)} %bitcast.61, bf16[4096,512]{1,0:T(8,128)(2,1)S(1)} %bitcast.53), kind=kOutput, calls=%fused_computation.2 | convolution fusion | flops 824705024 | bytes 7536644 | tf_op jit(solution)/shard_map/dot_general | solution.py:22
  106.7 1.5 collective-permute-start.22
  108.2 2.3 %convolution_convert_fusion.3 = bf16[128,4096]{1,0:T(8,128)(2,1)S(1)} fusion(bf16[512,768]{1,0:T(8,128)(2,1)S(1)} %pad_maximum_fusion.1, s32[]{:T(128)S(6)} %select_n.95, bf16[4096,128]{1,0:T(8,128)(2,1)S(1)} %bitcast.58, bf16[4096,128]{1,0:T(8,128)(2,1)S(1)} %bitcast.62, bf16[4096,512]{1,0:T(8,128)(2,1)S(1)} %bitcast.54), kind=kOutput, calls=%fused_computation.4 | convolution fusion | flops 824705024 | bytes 7536644 | tf_op jit(solution)/shard_map/dot_general | solution.py:22
  110.5 4.8 %collective-permute-start.21 = (bf16[128,4096]{1,0:T(8,128)(2,1)S(1)}, bf16[128,4096]{1,0:T(8,128)(2,1)S(1)}, u32[]{:S(2)}, u32[]{:S(2)}) collective-permute-start(bf16[128,4096]{1,0:T(8,128)(2,1)S(1)} %convolution_convert_fusion.3), channel_id=1, source_target_pairs={{0,96},{32,0},{64,32},{96,64},{1,97},{33,1},{65,33},{97,65},{2,98}... | collective-permute-start | bytes 3145736 | tf_op jit(solution)/shard_map/ppermute | solution.py:481
  115.5 4.5 %collective-permute-start.25 = (bf16[128,4096]{1,0:T(8,128)(2,1)S(1)}, bf16[128,4096]{1,0:T(8,128)(2,1)S(1)}, u32[]{:S(2)}, u32[]{:S(2)}) collective-permute-start(bf16[128,4096]{1,0:T(8,128)(2,1)S(1)} %add_convert_fusion.1), channel_id=1, source_target_pairs={{0,99},{1,96},{2,97},{3,98},{32,3},{33,0},{34,1},{35,2},{64,35},{6... | collective-permute-start | bytes 3145736 | tf_op jit(solution)/shard_map/ppermute | solution.py:488
  120.1 2.5 %collective-permute-start.23 = (bf16[128,4096]{1,0:T(8,128)(2,1)S(1)}, bf16[128,4096]{1,0:T(8,128)(2,1)S(1)}, u32[]{:S(2)}, u32[]{:S(2)}) collective-permute-start(bf16[128,4096]{1,0:T(8,128)(2,1)S(1)} %add_convert_fusion.2), channel_id=1, source_target_pairs={{0,97},{1,98},{2,99},{3,96},{32,1},{33,2},{34,3},{35,0},{64,33},{6... | collective-permute-start | bytes 3145736 | tf_op jit(solution)/shard_map/ppermute | solution.py:487
  122.6 5.7 %collective-permute-done.21 = bf16[128,4096]{1,0:T(8,128)(2,1)S(1)} collective-permute-done((bf16[128,4096]{1,0:T(8,128)(2,1)S(1)}, bf16[128,4096]{1,0:T(8,128)(2,1)S(1)}, u32[]{:S(2)}, u32[]{:S(2)}) %collective-permute-start.21) | collective-permute-done | bytes 1048608 | tf_op jit(solution)/shard_map/ppermute | solution.py:481
  128.3 14.7 %collective-permute-done.25 = bf16[128,4096]{1,0:T(8,128)(2,1)S(1)} collective-permute-done((bf16[128,4096]{1,0:T(8,128)(2,1)S(1)}, bf16[128,4096]{1,0:T(8,128)(2,1)S(1)}, u32[]{:S(2)}, u32[]{:S(2)}) %collective-permute-start.25) | collective-permute-done | bytes 1048608 | tf_op jit(solution)/shard_map/ppermute | solution.py:488
  143.0 9.4 %collective-permute-done.23 = bf16[128,4096]{1,0:T(8,128)(2,1)S(1)} collective-permute-done((bf16[128,4096]{1,0:T(8,128)(2,1)S(1)}, bf16[128,4096]{1,0:T(8,128)(2,1)S(1)}, u32[]{:S(2)}, u32[]{:S(2)}) %collective-permute-start.23) | collective-permute-done | bytes 1048608 | tf_op jit(solution)/shard_map/ppermute | solution.py:487
  152.4 1.4 fusion
  (84 shorter events, 18.8 us)
Async XLA Ops:
  0.6 51.0 %copy-start = (bf16[1,128,4096]{2,1,0:T(8,128)(2,1)S(1)}, bf16[1,128,4096]{2,1,0:T(8,128)(2,1)}, u32[]{:S(2)}) copy-start(bf16[1,128,4096]{2,1,0:T(8,128)(2,1)} %param.13) | copy-start | bytes 3145732
  1.7 12.2 %collective-permute-start.6 = (bf16[512,256]{1,0:T(8,128)(2,1)S(1)}, bf16[512,256]{1,0:T(8,128)(2,1)}, u32[]{:S(2)}, u32[]{:S(2)}) collective-permute-start(bf16[512,256]{1,0:T(8,128)(2,1)S(1)} %pad_maximum_fusion.2.refs_0_), channel_id=1, source_target_pairs={{0,16},{4,20},{8,24},{12,28},{16,0},{20,4},{24,8},{28,12},{1,17},{... | collective-permute-start | bytes 786440 | tf_op jit(solution)/shard_map/ppermute | solution.py:421
  5.4 13.9 %collective-permute-start.7 = (bf16[512,256]{1,0:T(8,128)(2,1)S(1)}, bf16[512,256]{1,0:T(8,128)(2,1)S(1)}, u32[]{:S(2)}, u32[]{:S(2)}) collective-permute-start(bf16[512,256]{1,0:T(8,128)(2,1)S(1)} %pad_maximum_fusion.2.refs_0_), channel_id=1, source_target_pairs={{0,12},{4,0},{8,4},{12,8},{16,28},{20,16},{24,20},{28,24},{1,13},{... | collective-permute-start | bytes 786440 | tf_op jit(solution)/shard_map/ppermute | solution.py:424
  9.1 14.5 %collective-permute-start.9 = (bf16[512,256]{1,0:T(8,128)(2,1)S(1)}, bf16[512,256]{1,0:T(8,128)(2,1)}, u32[]{:S(2)}, u32[]{:S(2)}) collective-permute-start(bf16[512,256]{1,0:T(8,128)(2,1)S(1)} %pad_maximum_fusion.2.refs_0_), channel_id=1, source_target_pairs={{0,8},{4,12},{8,0},{12,4},{16,24},{20,28},{24,16},{28,20},{1,9},{5... | collective-permute-start | bytes 786440 | tf_op jit(solution)/shard_map/ppermute | solution.py:424
  11.2 14.7 %copy-start.14 = (bf16[64,4096]{1,0:T(8,128)(2,1)}, bf16[64,4096]{1,0:T(8,128)(2,1)S(1)}, u32[]{:S(2)}) copy-start(bf16[64,4096]{1,0:T(8,128)(2,1)S(1)} %get-tuple-element.48) | copy-start | bytes 1572868
  11.2 14.7 %collective-permute-start = (bf16[64,4096]{1,0:T(8,128)(2,1)S(1)}, bf16[64,4096]{1,0:T(8,128)(2,1)S(1)}, u32[]{:S(2)}, u32[]{:S(2)}) collective-permute-start(bf16[64,4096]{1,0:T(8,128)(2,1)S(1)} %get-tuple-element.48), channel_id=1, source_target_pairs={{0,1},{1,2},{2,3},{3,0},{4,5},{5,6},{6,7},{7,4},{8,9},{9,10},{10,1... | collective-permute-start | bytes 1572872 | tf_op jit(solution)/shard_map/ppermute | solution.py:413
  12.5 15.0 %collective-permute-start.3 = (bf16[64,4096]{1,0:T(8,128)(2,1)}, bf16[64,4096]{1,0:T(8,128)(2,1)S(1)}, u32[]{:S(2)}, u32[]{:S(2)}) collective-permute-start(bf16[64,4096]{1,0:T(8,128)(2,1)} %get-tuple-element.47), channel_id=1, source_target_pairs={{0,3},{1,0},{2,1},{3,2},{4,7},{5,4},{6,5},{7,6},{8,11},{9,8},{10,9... | collective-permute-start | bytes 1572872 | tf_op jit(solution)/shard_map/ppermute | solution.py:414
  14.0 10.0 %collective-permute-start.11 = (bf16[512,256]{1,0:T(8,128)(2,1)S(1)}, bf16[512,256]{1,0:T(8,128)(2,1)S(1)}, u32[]{:S(2)}, u32[]{:S(2)}) collective-permute-start(bf16[512,256]{1,0:T(8,128)(2,1)S(1)} %pad_maximum_fusion.2.refs_0_), channel_id=1, source_target_pairs={{0,4},{4,8},{8,12},{12,0},{16,20},{20,24},{24,28},{28,16},{1,5},{5... | collective-permute-start | bytes 786440 | tf_op jit(solution)/shard_map/ppermute | solution.py:424
  20.0 7.7 %collective-permute-start.8 = (bf16[512,256]{1,0:T(8,128)(2,1)}, bf16[512,256]{1,0:T(8,128)(2,1)S(1)}, u32[]{:S(2)}, u32[]{:S(2)}) collective-permute-start(bf16[512,256]{1,0:T(8,128)(2,1)} %collective-permute-done.6.refs_1_), channel_id=1, source_target_pairs={{0,12},{4,0},{8,4},{12,8},{16,28},{20,16},{24,20},{28,24},{1,13},{... | collective-permute-start | bytes 786440 | tf_op jit(solution)/shard_map/ppermute | solution.py:426
  23.6 7.5 %collective-permute-start.10 = (bf16[512,256]{1,0:T(8,128)(2,1)}, bf16[512,256]{1,0:T(8,128)(2,1)S(1)}, u32[]{:S(2)}, u32[]{:S(2)}) collective-permute-start(bf16[512,256]{1,0:T(8,128)(2,1)} %collective-permute-done.9.refs_4_), channel_id=1, source_target_pairs={{0,16},{4,20},{8,24},{12,28},{16,0},{20,4},{24,8},{28,12},{1,17},{... | collective-permute-start | bytes 786440 | tf_op jit(solution)/shard_map/ppermute | solution.py:427
  24.6 27.0 %collective-permute-start.1 = (bf16[64,4096]{1,0:T(8,128)(2,1)}, bf16[64,4096]{1,0:T(8,128)(2,1)S(1)}, u32[]{:S(2)}, u32[]{:S(2)}) collective-permute-start(bf16[64,4096]{1,0:T(8,128)(2,1)} %get-tuple-element.47), channel_id=1, source_target_pairs={{0,1},{1,2},{2,3},{3,0},{4,5},{5,6},{6,7},{7,4},{8,9},{9,10},{10,1... | collective-permute-start | bytes 1572872 | tf_op jit(solution)/shard_map/ppermute | solution.py:417
  26.0 25.7 %collective-permute-start.2 = (bf16[64,4096]{1,0:T(8,128)(2,1)}, bf16[64,4096]{1,0:T(8,128)(2,1)S(1)}, u32[]{:S(2)}, u32[]{:S(2)}) collective-permute-start(bf16[64,4096]{1,0:T(8,128)(2,1)} %copy-done.14), channel_id=1, source_target_pairs={{0,3},{1,0},{2,1},{3,2},{4,7},{5,4},{6,5},{7,6},{8,11},{9,8},{10,9... | collective-permute-start | bytes 1572872 | tf_op jit(solution)/shard_map/ppermute | solution.py:418
  27.5 8.2 %collective-permute-start.12 = (bf16[512,256]{1,0:T(8,128)(2,1)}, bf16[512,256]{1,0:T(8,128)(2,1)}, u32[]{:S(2)}, u32[]{:S(2)}) collective-permute-start(bf16[512,256]{1,0:T(8,128)(2,1)} %collective-permute-done.6.refs_1_), channel_id=1, source_target_pairs={{0,4},{4,8},{8,12},{12,0},{16,20},{20,24},{24,28},{28,16},{1,5},{5... | collective-permute-start | bytes 786440 | tf_op jit(solution)/shard_map/ppermute | solution.py:426
  28.5 23.2 %collective-permute-start.4 = (bf16[64,4096]{1,0:T(8,128)(2,1)S(1)}, bf16[64,4096]{1,0:T(8,128)(2,1)}, u32[]{:S(2)}, u32[]{:S(2)}) collective-permute-start(bf16[64,4096]{1,0:T(8,128)(2,1)S(1)} %collective-permute-done.refs_1_), channel_id=1, source_target_pairs={{0,1},{1,2},{2,3},{3,0},{4,5},{5,6},{6,7},{7,4},{8,9},{9,10},{10,1... | collective-permute-start | bytes 1572872 | tf_op jit(solution)/shard_map/ppermute | solution.py:415
  31.8 19.8 %collective-permute-start.5 = (bf16[64,4096]{1,0:T(8,128)(2,1)S(1)}, bf16[64,4096]{1,0:T(8,128)(2,1)}, u32[]{:S(2)}, u32[]{:S(2)}) collective-permute-start(bf16[64,4096]{1,0:T(8,128)(2,1)S(1)} %collective-permute-done.3.refs_4_), channel_id=1, source_target_pairs={{0,3},{1,0},{2,1},{3,2},{4,7},{5,4},{6,5},{7,6},{8,11},{9,8},{10,9... | collective-permute-start | bytes 1572872 | tf_op jit(solution)/shard_map/ppermute | solution.py:416
  35.7 16.0 %copy-start.1 = (bf16[1,512,4096]{2,1,0:T(8,128)(2,1)S(1)}, bf16[1,512,4096]{2,1,0:T(8,128)(2,1)}, u32[]{:S(2)}) copy-start(bf16[1,512,4096]{2,1,0:T(8,128)(2,1)} %param.17) | copy-start | bytes 12582916
  64.8 17.2 %collective-permute-start.19 = (bf16[2,512,128]{2,1,0:T(8,128)(2,1)S(1)}, bf16[2,512,128]{2,1,0:T(8,128)(2,1)S(1)}, u32[]{:S(2)}, u32[]{:S(2)}) collective-permute-start(bf16[2,512,128]{2,1,0:T(8,128)(2,1)S(1)} %get-tuple-element.42), channel_id=1, source_target_pairs={{0,12},{4,0},{8,4},{12,8},{16,28},{20,16},{24,20},{28,24},{1,13},{... | collective-permute-start | bytes 786440 | tf_op jit(solution)/shard_map/ppermute | solution.py:453
  65.6 17.2 %collective-permute-start.18 = (bf16[2,512,128]{2,1,0:T(8,128)(2,1)S(1)}, bf16[2,512,128]{2,1,0:T(8,128)(2,1)S(1)}, u32[]{:S(2)}, u32[]{:S(2)}) collective-permute-start(bf16[2,512,128]{2,1,0:T(8,128)(2,1)S(1)} %get-tuple-element.41), channel_id=1, source_target_pairs={{0,8},{4,12},{8,0},{12,4},{16,24},{20,28},{24,16},{28,20},{1,9},{5... | collective-permute-start | bytes 786440 | tf_op jit(solution)/shard_map/ppermute | solution.py:453
  65.6 17.2 %collective-permute-start.17 = (bf16[2,512,128]{2,1,0:T(8,128)(2,1)S(1)}, bf16[2,512,128]{2,1,0:T(8,128)(2,1)S(1)}, u32[]{:S(2)}, u32[]{:S(2)}) collective-permute-start(bf16[2,512,128]{2,1,0:T(8,128)(2,1)S(1)} %get-tuple-element.40), channel_id=1, source_target_pairs={{0,4},{4,8},{8,12},{12,0},{16,20},{20,24},{24,28},{28,16},{1,5},{5... | collective-permute-start | bytes 786440 | tf_op jit(solution)/shard_map/ppermute | solution.py:453
  78.2 21.2 %copy-start.15 = (bf16[1,4096,512]{2,1,0:T(8,128)(2,1)S(1)}, bf16[1,4096,512]{2,1,0:T(8,128)(2,1)}, u32[]{:S(2)}) copy-start(bf16[1,4096,512]{2,1,0:T(8,128)(2,1)} %param.14) | copy-start | bytes 12582916
  78.2 21.2 %copy-start.16 = (bf16[1,4096,128]{2,1,0:T(8,128)(2,1)S(1)}, bf16[1,4096,128]{2,1,0:T(8,128)(2,1)}, u32[]{:S(2)}) copy-start(bf16[1,4096,128]{2,1,0:T(8,128)(2,1)} %param.16) | copy-start | bytes 3145732
  78.2 21.2 %copy-start.17 = (bf16[1,4096,128]{2,1,0:T(8,128)(2,1)S(1)}, bf16[1,4096,128]{2,1,0:T(8,128)(2,1)}, u32[]{:S(2)}) copy-start(bf16[1,4096,128]{2,1,0:T(8,128)(2,1)} %param.15) | copy-start | bytes 3145732
  78.3 7.6 %collective-permute-start.15 = (bf16[2,512,128]{2,1,0:T(8,128)(2,1)S(1)}, bf16[2,512,128]{2,1,0:T(8,128)(2,1)S(1)}, u32[]{:S(2)}, u32[]{:S(2)}) collective-permute-start(bf16[2,512,128]{2,1,0:T(8,128)(2,1)S(1)} %get-tuple-element.38), channel_id=1, source_target_pairs={{0,12},{4,0},{8,4},{12,8},{16,28},{20,16},{24,20},{28,24},{1,13},{... | collective-permute-start | bytes 786440 | tf_op jit(solution)/shard_map/ppermute | solution.py:453
  80.7 6.8 %collective-permute-start.14 = (bf16[2,512,128]{2,1,0:T(8,128)(2,1)S(1)}, bf16[2,512,128]{2,1,0:T(8,128)(2,1)S(1)}, u32[]{:S(2)}, u32[]{:S(2)}) collective-permute-start(bf16[2,512,128]{2,1,0:T(8,128)(2,1)S(1)} %get-tuple-element.37), channel_id=1, source_target_pairs={{0,8},{4,12},{8,0},{12,4},{16,24},{20,28},{24,16},{28,20},{1,9},{5... | collective-permute-start | bytes 786440 | tf_op jit(solution)/shard_map/ppermute | solution.py:453
  82.0 11.5 %collective-permute-start.13 = (bf16[2,512,128]{2,1,0:T(8,128)(2,1)S(1)}, bf16[2,512,128]{2,1,0:T(8,128)(2,1)S(1)}, u32[]{:S(2)}, u32[]{:S(2)}) collective-permute-start(bf16[2,512,128]{2,1,0:T(8,128)(2,1)S(1)} %get-tuple-element.36), channel_id=1, source_target_pairs={{0,4},{4,8},{8,12},{12,0},{16,20},{20,24},{24,28},{28,16},{1,5},{5... | collective-permute-start | bytes 786440 | tf_op jit(solution)/shard_map/ppermute | solution.py:453
  82.9 11.0 %collective-permute-start.20 = (bf16[512,128]{1,0:T(8,128)(2,1)S(1)}, bf16[512,128]{1,0:T(8,128)(2,1)S(1)}, u32[]{:S(2)}, u32[]{:S(2)}) collective-permute-start(bf16[512,128]{1,0:T(8,128)(2,1)S(1)} %fusion.10), channel_id=1, source_target_pairs={{0,16},{4,20},{8,24},{12,28},{16,0},{20,4},{24,8},{28,12},{1,17},{... | collective-permute-start | bytes 393224 | tf_op jit(solution)/shard_map/ppermute | solution.py:463
  93.7 5.6 %collective-permute-start.16 = (bf16[512,128]{1,0:T(8,128)(2,1)S(1)}, bf16[512,128]{1,0:T(8,128)(2,1)S(1)}, u32[]{:S(2)}, u32[]{:S(2)}) collective-permute-start(bf16[512,128]{1,0:T(8,128)(2,1)S(1)} %fusion.9), channel_id=1, source_target_pairs={{0,16},{4,20},{8,24},{12,28},{16,0},{20,4},{24,8},{28,12},{1,17},{... | collective-permute-start | bytes 393224 | tf_op jit(solution)/shard_map/ppermute | solution.py:463
  104.2 11.1 %collective-permute-start.24 = (bf16[64,4096]{1,0:T(8,128)(2,1)S(1)}, bf16[64,4096]{1,0:T(8,128)(2,1)S(1)}, u32[]{:S(2)}, u32[]{:S(2)}) collective-permute-start(bf16[64,4096]{1,0:T(8,128)(2,1)S(1)} %get-tuple-element.46), channel_id=1, source_target_pairs={{0,3},{1,0},{2,1},{3,2},{4,7},{5,4},{6,5},{7,6},{8,11},{9,8},{10,9... | collective-permute-start | bytes 1572872 | tf_op jit(solution)/shard_map/ppermute | solution.py:479
  106.7 13.3 %collective-permute-start.22 = (bf16[64,4096]{1,0:T(8,128)(2,1)S(1)}, bf16[64,4096]{1,0:T(8,128)(2,1)S(1)}, u32[]{:S(2)}, u32[]{:S(2)}) collective-permute-start(bf16[64,4096]{1,0:T(8,128)(2,1)S(1)} %get-tuple-element.45), channel_id=1, source_target_pairs={{0,1},{1,2},{2,3},{3,0},{4,5},{5,6},{6,7},{7,4},{8,9},{9,10},{10,1... | collective-permute-start | bytes 1572872 | tf_op jit(solution)/shard_map/ppermute | solution.py:478
  110.5 17.8 %collective-permute-start.21 = (bf16[128,4096]{1,0:T(8,128)(2,1)S(1)}, bf16[128,4096]{1,0:T(8,128)(2,1)S(1)}, u32[]{:S(2)}, u32[]{:S(2)}) collective-permute-start(bf16[128,4096]{1,0:T(8,128)(2,1)S(1)} %convolution_convert_fusion.3), channel_id=1, source_target_pairs={{0,96},{32,0},{64,32},{96,64},{1,97},{33,1},{65,33},{97,65},{2,98}... | collective-permute-start | bytes 3145736 | tf_op jit(solution)/shard_map/ppermute | solution.py:481
  115.5 27.5 %collective-permute-start.25 = (bf16[128,4096]{1,0:T(8,128)(2,1)S(1)}, bf16[128,4096]{1,0:T(8,128)(2,1)S(1)}, u32[]{:S(2)}, u32[]{:S(2)}) collective-permute-start(bf16[128,4096]{1,0:T(8,128)(2,1)S(1)} %add_convert_fusion.1), channel_id=1, source_target_pairs={{0,99},{1,96},{2,97},{3,98},{32,3},{33,0},{34,1},{35,2},{64,35},{6... | collective-permute-start | bytes 3145736 | tf_op jit(solution)/shard_map/ppermute | solution.py:488
  120.1 32.2 %collective-permute-start.23 = (bf16[128,4096]{1,0:T(8,128)(2,1)S(1)}, bf16[128,4096]{1,0:T(8,128)(2,1)S(1)}, u32[]{:S(2)}, u32[]{:S(2)}) collective-permute-start(bf16[128,4096]{1,0:T(8,128)(2,1)S(1)} %add_convert_fusion.2), channel_id=1, source_target_pairs={{0,97},{1,98},{2,99},{3,96},{32,1},{33,2},{34,3},{35,0},{64,33},{6... | collective-permute-start | bytes 3145736 | tf_op jit(solution)/shard_map/ppermute | solution.py:487
  (12 other events, 26.1 us)

commit v4 on v3

--- a/solution.py
+++ b/solution.py
@@ -189,7 +189,7 @@
 
 
 def grad_call(rows, pieces, out_weight):
-    depth = 512
+    depth = 1024
     total = out_weight.shape[0]
     return pl.pallas_call(
         grad_kernel,
@@ -463,16 +463,23 @@
         received = send(total[1].astype(bf16), CTX, X_SWAP)
         return (total[0] + received.astype(f32)).astype(bf16)
 
+    def chunk_of(array, distance):
+        return lax.dynamic_slice_in_dim(array, ((tp + distance) % 4) * 128, 128, 0)
+
+    query_terms = []
+    for distance in range(4):
+        query_terms.append(dot_nt(chunk_of(query_grad, distance), query_weight[0]))
+    query_terms = lax.optimization_barrier(tuple(query_terms))
+
     value_grad = with_pair(value_sum)
     key_grad = with_pair(key_sum)
 
-    stacked = jnp.concatenate([query_grad, key_grad, value_grad], axis=1)
-    weights = jnp.concatenate([query_weight[0], key_weight[0], value_weight[0]], axis=1)
+    kv_grad = jnp.concatenate([key_grad, value_grad], axis=1)
+    kv_weights = jnp.concatenate([key_weight[0], value_weight[0]], axis=1)
 
     def term_of(distance):
-        start = ((tp + distance) % 4) * 128
-        rows = lax.dynamic_slice_in_dim(stacked, start, 128, 0)
-        return dot_nt(rows, weights).astype(bf16)
+        rows = chunk_of(kv_grad, distance)
+        return (query_terms[distance] + dot_nt(rows, kv_weights)).astype(bf16)
 
     far = term_of(2)
     from_left = send(far[:half_rows], TP, ring(4, 1))
@@ -480,13 +487,20 @@
     own_term = term_of(0)
     own = send(own_term, SECTION, ring(4, -1))
     right, left = lax.optimization_barrier((term_of(1), term_of(3)))
-    empty = jnp.zeros_like(from_left, dtype=f32)
-    right = (right.astype(f32) + jnp.concatenate([from_left.astype(f32), empty])).astype(bf16)
-    left = (left.astype(f32) + jnp.concatenate([empty, from_right.astype(f32)])).astype(bf16)
     joint = (SECTION, TP)
-    part_a = send(right, joint, joint_ring(1))
-    part_b = send(left, joint, joint_ring(-1))
-    sent = (own.astype(f32) + part_a.astype(f32) + part_b.astype(f32)).astype(bf16)
+    low_a = send(right[half_rows:], joint, joint_ring(1))
+    top_b = send(left[:half_rows], joint, joint_ring(-1))
+    top_a = (right[:half_rows].astype(f32) + from_left.astype(f32)).astype(bf16)
+    top_a = send(top_a, joint, joint_ring(1))
+    low_b = (left[half_rows:].astype(f32) + from_right.astype(f32)).astype(bf16)
+    low_b = send(low_b, joint, joint_ring(-1))
+    sent = jnp.concatenate(
+        [
+            own[:half_rows].astype(f32) + top_a.astype(f32) + top_b.astype(f32),
+            own[half_rows:].astype(f32) + low_a.astype(f32) + low_b.astype(f32),
+        ],
+        axis=0,
+    ).astype(bf16)
     return (sent[None], key_grad[None], value_grad[None])
 
 

time: 154 us -> 153 us (level)
  starting transfers between devices: 42.3 us -> 56.1 us
  waiting for transfers between devices: 50.8 us -> 37.6 us
  Pallas kernels: 35.7 us -> 33.7 us
    ppermute x2 -> x4, waiting for transfers between devices: 24.1 us -> 11.7 us  [the longest x1 6.8 us: per_device(): top_a = send(top_a, joint, joint_ring(1))]
    ppermute x2 -> x4, starting transfers between devices: 6.98 us -> 17.8 us  [the longest x1 9.81 us: per_device(): top_a = send(top_a, joint, joint_ring(1))]
    ppermute x1, waiting for transfers between devices: 0.01 us -> 8.31 us  [per_device(): from_right = send(far[half_rows:], TP, ring(4, -1))]
    ppermute x1, waiting for transfers between devices: 5.7 us -> 0.01 us  [per_device(): own = send(own_term, SECTION, ring(4, -1))]
    ppermute x2, starting transfers between devices: 1.44 us -> 5.43 us  [with_pair(): received = send(total[1].astype(bf16), CTX, X_SWAP)]
    ppermute x2, starting transfers between devices: 3.56 us -> 0.01 us  [per_device(): crossed[distance] = send(kv_pair, CTX, z_ring(shift))]
    ppermute x2, waiting for transfers between devices: 5.25 us -> 2.58 us  [with_pair(): received = send(total[1].astype(bf16), CTX, X_SWAP)]
    ppermute x2, waiting for transfers between devices: 0.29 us -> 2.88 us  [per_device(): crossed[distance] = send(kv_pair, CTX, z_ring(shift))]
  transfers between devices with their start and end apart: 26 -> 28, of which waited for: 10 -> 11; matrix products, arithmetic and copies ran while one was open for 6% -> 7% of each run, Pallas kernels for 15% -> 7%
where the time goes in v4:
time: 153 us; the launch traced here: 152 us
  starting transfers between devices  56.1 us (37%)
  waiting for transfers between devices  37.6 us (25%)
  Pallas kernels  33.7 us (22%)
  local copies, waits for them, and re-layouts  11 us (7%)
  matrix products  9.22 us (6%)
  other arithmetic  3.41 us (2%)
    pallas_call x1, Pallas kernels, key_call(): pl.pallas_call(key_kernel, grid_spec=pltpu.PrefetchScalarGridSpec(num_sca...  11.6 us
    pallas_call x1, Pallas kernels, forward_call(): pl.pallas_call(forward_kernel, grid_spec=pltpu.PrefetchScalarGridSpec(num...  10.9 us
    ppermute x1, starting transfers between devices, per_device(): top_a = send(top_a, joint, joint_ring(1))  9.81 us
    dot_general x8, matrix products, dot_nt(): lax.dot_general(lhs, rhs, (((1,), (1,)), ((), ())), preferred_element_typ...  9.22 us
    unnamed x38, local copies, waits for them, and re-layouts  8.34 us
    ppermute x1, waiting for transfers between devices, per_device(): from_right = send(far[half_rows:], TP, ring(4, -1))  8.31 us
    ppermute x1, starting transfers between devices, per_device(): top_b = send(left[:half_rows], joint, joint_ring(-1))  7.9 us
    ppermute x6, waiting for transfers between devices, along_z(): received = send(groups[distance], CTX, z_ring(shift))  7.68 us
  transfers between devices with their start and end apart: 28, of which 11 were waited for; matrix products, arithmetic and copies ran while one was open for 7% of the time, Pallas kernels for 7%

profile of v4, /device:TPU:1, one launch (start us, length us, event | category | flops | bytes accessed | tf_op | source)
XLA Modules:
  0.0 152.2 jit_solution(18005586323944457672)
XLA Ops:
  1.7 2.5 %collective-permute-start.11 = (bf16[512,256]{1,0:T(8,128)(2,1)S(1)}, bf16[512,256]{1,0:T(8,128)(2,1)S(1)}, u32[]{:S(2)}, u32[]{:S(2)}) collective-permute-start(bf16[512,256]{1,0:T(8,128)(2,1)S(1)} %pad_maximum_fusion.2.refs_0_), channel_id=1, source_target_pairs={{0,4},{4,8},{8,12},{12,0},{16,20},{20,24},{24,28},{28,16},{1,5},{5... | collective-permute-start | bytes 786440 | tf_op jit(solution)/shard_map/ppermute | solution.py:424
  4.2 3.3 %collective-permute-start.9 = (bf16[512,256]{1,0:T(8,128)(2,1)S(1)}, bf16[512,256]{1,0:T(8,128)(2,1)S(1)}, u32[]{:S(2)}, u32[]{:S(2)}) collective-permute-start(bf16[512,256]{1,0:T(8,128)(2,1)S(1)} %pad_maximum_fusion.2.refs_0_), channel_id=1, source_target_pairs={{0,8},{4,12},{8,0},{12,4},{16,24},{20,28},{24,16},{28,20},{1,9},{5... | collective-permute-start | bytes 786440 | tf_op jit(solution)/shard_map/ppermute | solution.py:424
  7.5 2.7 %collective-permute-start.6 = (bf16[512,256]{1,0:T(8,128)(2,1)S(1)}, bf16[512,256]{1,0:T(8,128)(2,1)}, u32[]{:S(2)}, u32[]{:S(2)}) collective-permute-start(bf16[512,256]{1,0:T(8,128)(2,1)S(1)} %pad_maximum_fusion.2.refs_0_), channel_id=1, source_target_pairs={{0,16},{4,20},{8,24},{12,28},{16,0},{20,4},{24,8},{28,12},{1,17},{... | collective-permute-start | bytes 786440 | tf_op jit(solution)/shard_map/ppermute | solution.py:421
  10.3 2.3 %slice_bitcast_fusion = (bf16[64,4096]{1,0:T(8,128)(2,1)}, bf16[64,4096]{1,0:T(8,128)(2,1)}) fusion(bf16[1,128,4096]{2,1,0:T(8,128)(2,1)} %param.13), kind=kLoop, calls=%fused_computation.26 | loop fusion | bytes 2097152 | tf_op jit(solution)/shard_map/slice | solution.py:412
  12.5 2.7 %collective-permute-start.3 = (bf16[64,4096]{1,0:T(8,128)(2,1)}, bf16[64,4096]{1,0:T(8,128)(2,1)S(1)}, u32[]{:S(2)}, u32[]{:S(2)}) collective-permute-start(bf16[64,4096]{1,0:T(8,128)(2,1)} %get-tuple-element.57), channel_id=1, source_target_pairs={{0,3},{1,0},{2,1},{3,2},{4,7},{5,4},{6,5},{7,6},{8,11},{9,8},{10,9... | collective-permute-start | bytes 1572872 | tf_op jit(solution)/shard_map/ppermute | solution.py:414
  16.7 2.2 %collective-permute-done.9.refs_4_ = bf16[512,256]{1,0:T(8,128)(2,1)S(1)} collective-permute-done((bf16[512,256]{1,0:T(8,128)(2,1)S(1)}, bf16[512,256]{1,0:T(8,128)(2,1)S(1)}, u32[]{:S(2)}, u32[]{:S(2)}) %collective-permute-start.9) | collective-permute-done | bytes 262176 | tf_op jit(solution)/shard_map/ppermute | solution.py:424
  18.9 2.7 %collective-permute-start.10 = (bf16[512,256]{1,0:T(8,128)(2,1)S(1)}, bf16[512,256]{1,0:T(8,128)(2,1)S(1)}, u32[]{:S(2)}, u32[]{:S(2)}) collective-permute-start(bf16[512,256]{1,0:T(8,128)(2,1)S(1)} %collective-permute-done.9.refs_4_), channel_id=1, source_target_pairs={{0,16},{4,20},{8,24},{12,28},{16,0},{20,4},{24,8},{28,12},{1,17},{... | collective-permute-start | bytes 786440 | tf_op jit(solution)/shard_map/ppermute | solution.py:427
  24.4 2.3 %collective-permute-done.10.refs_5_ = bf16[512,256]{1,0:T(8,128)(2,1)S(1)} collective-permute-done((bf16[512,256]{1,0:T(8,128)(2,1)S(1)}, bf16[512,256]{1,0:T(8,128)(2,1)S(1)}, u32[]{:S(2)}, u32[]{:S(2)}) %collective-permute-start.10) | collective-permute-done | bytes 262176 | tf_op jit(solution)/shard_map/ppermute | solution.py:427
  27.4 2.7 %collective-permute-start.2 = (bf16[64,4096]{1,0:T(8,128)(2,1)}, bf16[64,4096]{1,0:T(8,128)(2,1)S(1)}, u32[]{:S(2)}, u32[]{:S(2)}) collective-permute-start(bf16[64,4096]{1,0:T(8,128)(2,1)} %get-tuple-element.58), channel_id=1, source_target_pairs={{0,3},{1,0},{2,1},{3,2},{4,7},{5,4},{6,5},{7,6},{8,11},{9,8},{10,9... | collective-permute-start | bytes 1572872 | tf_op jit(solution)/shard_map/ppermute | solution.py:418
  30.9 2.4 %collective-permute-start.5 = (bf16[64,4096]{1,0:T(8,128)(2,1)S(1)}, bf16[64,4096]{1,0:T(8,128)(2,1)S(1)}, u32[]{:S(2)}, u32[]{:S(2)}) collective-permute-start(bf16[64,4096]{1,0:T(8,128)(2,1)S(1)} %collective-permute-done.3.refs_4_), channel_id=1, source_target_pairs={{0,3},{1,0},{2,1},{3,2},{4,7},{5,4},{6,5},{7,6},{8,11},{9,8},{10,9... | collective-permute-start | bytes 1572872 | tf_op jit(solution)/shard_map/ppermute | solution.py:416
  33.8 2.9 %collective-permute-done.8.refs_3_ = bf16[512,256]{1,0:T(8,128)(2,1)} collective-permute-done((bf16[512,256]{1,0:T(8,128)(2,1)}, bf16[512,256]{1,0:T(8,128)(2,1)}, u32[]{:S(2)}, u32[]{:S(2)}) %collective-permute-start.8) | collective-permute-done | bytes 262176 | tf_op jit(solution)/shard_map/ppermute | solution.py:426
  41.4 10.9 %shard_map.112 = (bf16[17,4,256,256]{3,2,1,0:T(8,128)(2,1)S(1)}, f32[2,128,1024]{2,1,0:T(8,128)S(1)}, f32[2,8,1024]{2,1,0:T(8,128)S(1)}, f32[17,1,1024]{2,1,0:T(1,128)S(1)}, bf16[16,256,256]{2,1,0:T(8,128)(2,1)S(1)}) custom-call(s32[1]{0:T(128)S(1)} %bitcast.54, s32[16]{0:T(128)S(1)} %reshape.115.ids_ref, bf16[512,256]{1,0:T(8,128)(2,1)S(1)} %pad_maximum_fusion.2.refs_0_, ...), custom_call_target="tpu_custom_call" | custom-call | flops 2281701376 | bytes 13631488 | tf_op jit(solution)/shard_map/pallas_call | solution.py:131
  52.4 5.1 %attn_grad.1.grad_ref = bf16[512,512]{1,0:T(8,128)(2,1)S(1)} custom-call(s32[7]{0:T(128)S(1)} %broadcast_multiply_fusion.rows_ref, bf16[128,4096]{1,0:T(8,128)(2,1)S(1)} %bitcast.50, bf16[64,4096]{1,0:T(8,128)(2,1)S(1)} %collective-permute-done.refs_1_, bf16[64,4096]{1,0:T(8,128)(2,1)S(1)} %collective-permute-done.1.refs_2_, ...), custom_call_target="tpu_custom_call" | custom-call | flops 2147483648 | bytes 9437184 | tf_op jit(solution)/shard_map/attn_grad/pallas_call | solution.py:194
  57.4 6.1 %attn_value_grad.1 = (bf16[2,512,128]{2,1,0:T(8,128)(2,1)S(1)}, bf16[2,512,128]{2,1,0:T(8,128)(2,1)S(1)}, bf16[2,512,128]{2,1,0:T(8,128)(2,1)S(1)}, bf16[2,512,128]{2,1,0:T(8,128)(2,1)S(1)}) custom-call(s32[1]{0:T(128)S(1)} %bitcast.55, s32[16]{0:T(128)S(1)} %reshape.115.ids_ref, bf16[512,512]{1,0:T(8,128)(2,1)S(1)} %attn_grad.1.grad_ref, ...), custom_call_target="tpu_custom_call" | custom-call | flops 1140850688 | bytes 11534336 | tf_op jit(solution)/shard_map/attn_value_grad/pallas_call | solution.py:260
  63.6 11.6 %shard_map.113 = (bf16[512,512]{1,0:T(8,128)(2,1)S(1)}, bf16[2,512,128]{2,1,0:T(8,128)(2,1)S(1)}, bf16[2,512,128]{2,1,0:T(8,128)(2,1)S(1)}, bf16[2,512,128]{2,1,0:T(8,128)(2,1)S(1)}, bf16[2,512,128]{2,1,0:T(8,128)(2,1)S(1)}) custom-call(s32[1]{0:T(128)S(1)} %bitcast.56, s32[16]{0:T(128)S(1)} %reshape.115.ids_ref, bf16[512,512]{1,0:T(8,128)(2,1)S(1)} %attn_grad.1.grad_ref, ...), custom_call_target="tpu_custom_call" | custom-call | flops 3422552064 | bytes 14680064 | tf_op jit(solution)/shard_map/pallas_call | solution.py:359
  75.3 2.4 %collective-permute-start.14 = (bf16[2,512,128]{2,1,0:T(8,128)(2,1)S(1)}, bf16[2,512,128]{2,1,0:T(8,128)(2,1)S(1)}, u32[]{:S(2)}, u32[]{:S(2)}) collective-permute-start(bf16[2,512,128]{2,1,0:T(8,128)(2,1)S(1)} %get-tuple-element.42), channel_id=1, source_target_pairs={{0,8},{4,12},{8,0},{12,4},{16,24},{20,28},{24,16},{28,20},{1,9},{5... | collective-permute-start | bytes 786440 | tf_op jit(solution)/shard_map/ppermute | solution.py:453
  80.3 1.5 fusion.4
  81.8 1.5 fusion.6
  83.3 1.5 fusion.8
  84.8 1.5 fusion.10
  86.3 2.1 %collective-permute-start.19 = (bf16[2,512,128]{2,1,0:T(8,128)(2,1)S(1)}, bf16[2,512,128]{2,1,0:T(8,128)(2,1)S(1)}, u32[]{:S(2)}, u32[]{:S(2)}) collective-permute-start(bf16[2,512,128]{2,1,0:T(8,128)(2,1)S(1)} %get-tuple-element.47), channel_id=1, source_target_pairs={{0,12},{4,0},{8,4},{12,8},{16,28},{20,16},{24,20},{28,24},{1,13},{... | collective-permute-start | bytes 786440 | tf_op jit(solution)/shard_map/ppermute | solution.py:453
  89.6 2.7 %collective-permute-start.16 = (bf16[512,128]{1,0:T(8,128)(2,1)S(1)}, bf16[512,128]{1,0:T(8,128)(2,1)S(1)}, u32[]{:S(2)}, u32[]{:S(2)}) collective-permute-start(bf16[512,128]{1,0:T(8,128)(2,1)S(1)} %fusion.18), channel_id=1, source_target_pairs={{0,16},{4,20},{8,24},{12,28},{16,0},{20,4},{24,8},{28,12},{1,17},{... | collective-permute-start | bytes 393224 | tf_op jit(solution)/shard_map/ppermute | solution.py:463
  92.3 3.3 %collective-permute-done.17 = bf16[2,512,128]{2,1,0:T(8,128)(2,1)S(1)} collective-permute-done((bf16[2,512,128]{2,1,0:T(8,128)(2,1)S(1)}, bf16[2,512,128]{2,1,0:T(8,128)(2,1)S(1)}, u32[]{:S(2)}, u32[]{:S(2)}) %collective-permute-start.17) | collective-permute-done | bytes 262176 | tf_op jit(solution)/shard_map/ppermute | solution.py:453
  96.6 2.4 %collective-permute-done.19 = bf16[2,512,128]{2,1,0:T(8,128)(2,1)S(1)} collective-permute-done((bf16[2,512,128]{2,1,0:T(8,128)(2,1)S(1)}, bf16[2,512,128]{2,1,0:T(8,128)(2,1)S(1)}, u32[]{:S(2)}, u32[]{:S(2)}) %collective-permute-start.19) | collective-permute-done | bytes 262176 | tf_op jit(solution)/shard_map/ppermute | solution.py:453
  99.1 2.8 %collective-permute-start.20 = (bf16[512,128]{1,0:T(8,128)(2,1)S(1)}, bf16[512,128]{1,0:T(8,128)(2,1)S(1)}, u32[]{:S(2)}, u32[]{:S(2)}) collective-permute-start(bf16[512,128]{1,0:T(8,128)(2,1)S(1)} %fusion.19), channel_id=1, source_target_pairs={{0,16},{4,20},{8,24},{12,28},{16,0},{20,4},{24,8},{28,12},{1,17},{... | collective-permute-start | bytes 393224 | tf_op jit(solution)/shard_map/ppermute | solution.py:463
  101.9 2.6 %collective-permute-done.20 = bf16[512,128]{1,0:T(8,128)(2,1)S(1)} collective-permute-done((bf16[512,128]{1,0:T(8,128)(2,1)S(1)}, bf16[512,128]{1,0:T(8,128)(2,1)S(1)}, u32[]{:S(2)}, u32[]{:S(2)}) %collective-permute-start.20) | collective-permute-done | bytes 131104 | tf_op jit(solution)/shard_map/ppermute | solution.py:463
  107.3 7.9 %collective-permute-start.24 = (bf16[64,4096]{1,0:T(8,128)(2,1)S(1)}, bf16[64,4096]{1,0:T(8,128)(2,1)S(1)}, u32[]{:S(2)}, u32[]{:S(2)}) collective-permute-start(bf16[64,4096]{1,0:T(8,128)(2,1)S(1)} %slice.65), channel_id=1, source_target_pairs={{0,99},{1,96},{2,97},{3,98},{32,3},{33,0},{34,1},{35,2},{64,35},{6... | collective-permute-start | bytes 1572872 | tf_op jit(solution)/shard_map/ppermute | solution.py:492
  117.2 3.2 %collective-permute-start.21 = (bf16[128,4096]{1,0:T(8,128)(2,1)S(1)}, bf16[128,4096]{1,0:T(8,128)(2,1)S(1)}, u32[]{:S(2)}, u32[]{:S(2)}) collective-permute-start(bf16[128,4096]{1,0:T(8,128)(2,1)S(1)} %fusion), channel_id=1, source_target_pairs={{0,96},{32,0},{64,32},{96,64},{1,97},{33,1},{65,33},{97,65},{2,98}... | collective-permute-start | bytes 3145736 | tf_op jit(solution)/shard_map/ppermute | solution.py:488
  120.5 9.8 %collective-permute-start.23 = (bf16[64,4096]{1,0:T(8,128)(2,1)S(1)}, bf16[64,4096]{1,0:T(8,128)(2,1)S(1)}, u32[]{:S(2)}, u32[]{:S(2)}) collective-permute-start(bf16[64,4096]{1,0:T(8,128)(2,1)S(1)} %add_convert_fusion.3), channel_id=1, source_target_pairs={{0,97},{1,98},{2,99},{3,96},{32,1},{33,2},{34,3},{35,0},{64,33},{6... | collective-permute-start | bytes 1572872 | tf_op jit(solution)/shard_map/ppermute | solution.py:494
  130.4 8.3 %collective-permute-done.26 = bf16[64,4096]{1,0:T(8,128)(2,1)S(1)} collective-permute-done((bf16[64,4096]{1,0:T(8,128)(2,1)S(1)}, bf16[64,4096]{1,0:T(8,128)(2,1)S(1)}, u32[]{:S(2)}, u32[]{:S(2)}) %collective-permute-start.26) | collective-permute-done | bytes 524320 | tf_op jit(solution)/shard_map/ppermute | solution.py:486
  138.9 6.8 %collective-permute-done.23 = bf16[64,4096]{1,0:T(8,128)(2,1)S(1)} collective-permute-done((bf16[64,4096]{1,0:T(8,128)(2,1)S(1)}, bf16[64,4096]{1,0:T(8,128)(2,1)S(1)}, u32[]{:S(2)}, u32[]{:S(2)}) %collective-permute-start.23) | collective-permute-done | bytes 524320 | tf_op jit(solution)/shard_map/ppermute | solution.py:494
  145.7 4.9 %collective-permute-done.27 = bf16[64,4096]{1,0:T(8,128)(2,1)S(1)} collective-permute-done((bf16[64,4096]{1,0:T(8,128)(2,1)S(1)}, bf16[64,4096]{1,0:T(8,128)(2,1)S(1)}, u32[]{:S(2)}, u32[]{:S(2)}) %collective-permute-start.27) | collective-permute-done | bytes 524320 | tf_op jit(solution)/shard_map/ppermute | solution.py:496
  (96 shorter events, 23.7 us)
Async XLA Ops:
  0.6 32.7 %copy-start.18 = (s32[8,2]{0,1:T(2,128)S(1)}, s32[8,2]{0,1:T(2,128)}, u32[]{:S(2)}) copy-start(s32[8,2]{0,1:T(2,128)} %param.9) | copy-start | bytes 196
  0.6 36.0 %copy-start.2 = (bf16[1,512,512]{2,1,0:T(8,128)(2,1)S(1)}, bf16[1,512,512]{2,1,0:T(8,128)(2,1)}, u32[]{:S(2)}) copy-start(bf16[1,512,512]{2,1,0:T(8,128)(2,1)} %param.10) | copy-start | bytes 1572868
  1.7 13.6 %collective-permute-start.11 = (bf16[512,256]{1,0:T(8,128)(2,1)S(1)}, bf16[512,256]{1,0:T(8,128)(2,1)S(1)}, u32[]{:S(2)}, u32[]{:S(2)}) collective-permute-start(bf16[512,256]{1,0:T(8,128)(2,1)S(1)} %pad_maximum_fusion.2.refs_0_), channel_id=1, source_target_pairs={{0,4},{4,8},{8,12},{12,0},{16,20},{20,24},{24,28},{28,16},{1,5},{5... | collective-permute-start | bytes 786440 | tf_op jit(solution)/shard_map/ppermute | solution.py:424
  4.2 14.6 %collective-permute-start.9 = (bf16[512,256]{1,0:T(8,128)(2,1)S(1)}, bf16[512,256]{1,0:T(8,128)(2,1)S(1)}, u32[]{:S(2)}, u32[]{:S(2)}) collective-permute-start(bf16[512,256]{1,0:T(8,128)(2,1)S(1)} %pad_maximum_fusion.2.refs_0_), channel_id=1, source_target_pairs={{0,8},{4,12},{8,0},{12,4},{16,24},{20,28},{24,16},{28,20},{1,9},{5... | collective-permute-start | bytes 786440 | tf_op jit(solution)/shard_map/ppermute | solution.py:424
  7.5 14.8 %collective-permute-start.6 = (bf16[512,256]{1,0:T(8,128)(2,1)S(1)}, bf16[512,256]{1,0:T(8,128)(2,1)}, u32[]{:S(2)}, u32[]{:S(2)}) collective-permute-start(bf16[512,256]{1,0:T(8,128)(2,1)S(1)} %pad_maximum_fusion.2.refs_0_), channel_id=1, source_target_pairs={{0,16},{4,20},{8,24},{12,28},{16,0},{20,4},{24,8},{28,12},{1,17},{... | collective-permute-start | bytes 786440 | tf_op jit(solution)/shard_map/ppermute | solution.py:421
  12.5 18.4 %collective-permute-start.3 = (bf16[64,4096]{1,0:T(8,128)(2,1)}, bf16[64,4096]{1,0:T(8,128)(2,1)S(1)}, u32[]{:S(2)}, u32[]{:S(2)}) collective-permute-start(bf16[64,4096]{1,0:T(8,128)(2,1)} %get-tuple-element.57), channel_id=1, source_target_pairs={{0,3},{1,0},{2,1},{3,2},{4,7},{5,4},{6,5},{7,6},{8,11},{9,8},{10,9... | collective-permute-start | bytes 1572872 | tf_op jit(solution)/shard_map/ppermute | solution.py:414
  15.3 18.0 %collective-permute-start = (bf16[64,4096]{1,0:T(8,128)(2,1)}, bf16[64,4096]{1,0:T(8,128)(2,1)S(1)}, u32[]{:S(2)}, u32[]{:S(2)}) collective-permute-start(bf16[64,4096]{1,0:T(8,128)(2,1)} %get-tuple-element.58), channel_id=1, source_target_pairs={{0,1},{1,2},{2,3},{3,0},{4,5},{5,6},{6,7},{7,4},{8,9},{9,10},{10,1... | collective-permute-start | bytes 1572872 | tf_op jit(solution)/shard_map/ppermute | solution.py:413
  16.0 6.4 %collective-permute-start.7 = (bf16[512,256]{1,0:T(8,128)(2,1)S(1)}, bf16[512,256]{1,0:T(8,128)(2,1)S(1)}, u32[]{:S(2)}, u32[]{:S(2)}) collective-permute-start(bf16[512,256]{1,0:T(8,128)(2,1)S(1)} %pad_maximum_fusion.2.refs_0_), channel_id=1, source_target_pairs={{0,12},{4,0},{8,4},{12,8},{16,28},{20,16},{24,20},{28,24},{1,13},{... | collective-permute-start | bytes 786440 | tf_op jit(solution)/shard_map/ppermute | solution.py:424
  18.9 7.8 %collective-permute-start.10 = (bf16[512,256]{1,0:T(8,128)(2,1)S(1)}, bf16[512,256]{1,0:T(8,128)(2,1)S(1)}, u32[]{:S(2)}, u32[]{:S(2)}) collective-permute-start(bf16[512,256]{1,0:T(8,128)(2,1)S(1)} %collective-permute-done.9.refs_4_), channel_id=1, source_target_pairs={{0,16},{4,20},{8,24},{12,28},{16,0},{20,4},{24,8},{28,12},{1,17},{... | collective-permute-start | bytes 786440 | tf_op jit(solution)/shard_map/ppermute | solution.py:427
  22.3 7.8 %collective-permute-start.12 = (bf16[512,256]{1,0:T(8,128)(2,1)}, bf16[512,256]{1,0:T(8,128)(2,1)S(1)}, u32[]{:S(2)}, u32[]{:S(2)}) collective-permute-start(bf16[512,256]{1,0:T(8,128)(2,1)} %collective-permute-done.6.refs_1_), channel_id=1, source_target_pairs={{0,4},{4,8},{8,12},{12,0},{16,20},{20,24},{24,28},{28,16},{1,5},{5... | collective-permute-start | bytes 786440 | tf_op jit(solution)/shard_map/ppermute | solution.py:426
  23.1 29.2 %collective-permute-start.1 = (bf16[64,4096]{1,0:T(8,128)(2,1)}, bf16[64,4096]{1,0:T(8,128)(2,1)S(1)}, u32[]{:S(2)}, u32[]{:S(2)}) collective-permute-start(bf16[64,4096]{1,0:T(8,128)(2,1)} %get-tuple-element.57), channel_id=1, source_target_pairs={{0,1},{1,2},{2,3},{3,0},{4,5},{5,6},{6,7},{7,4},{8,9},{9,10},{10,1... | collective-permute-start | bytes 1572872 | tf_op jit(solution)/shard_map/ppermute | solution.py:417
  27.4 24.9 %collective-permute-start.2 = (bf16[64,4096]{1,0:T(8,128)(2,1)}, bf16[64,4096]{1,0:T(8,128)(2,1)S(1)}, u32[]{:S(2)}, u32[]{:S(2)}) collective-permute-start(bf16[64,4096]{1,0:T(8,128)(2,1)} %get-tuple-element.58), channel_id=1, source_target_pairs={{0,3},{1,0},{2,1},{3,2},{4,7},{5,4},{6,5},{7,6},{8,11},{9,8},{10,9... | collective-permute-start | bytes 1572872 | tf_op jit(solution)/shard_map/ppermute | solution.py:418
  30.9 5.7 %collective-permute-start.8 = (bf16[512,256]{1,0:T(8,128)(2,1)}, bf16[512,256]{1,0:T(8,128)(2,1)}, u32[]{:S(2)}, u32[]{:S(2)}) collective-permute-start(bf16[512,256]{1,0:T(8,128)(2,1)} %collective-permute-done.6.refs_1_), channel_id=1, source_target_pairs={{0,12},{4,0},{8,4},{12,8},{16,28},{20,16},{24,20},{28,24},{1,13},{... | collective-permute-start | bytes 786440 | tf_op jit(solution)/shard_map/ppermute | solution.py:426
  30.9 21.4 %collective-permute-start.5 = (bf16[64,4096]{1,0:T(8,128)(2,1)S(1)}, bf16[64,4096]{1,0:T(8,128)(2,1)S(1)}, u32[]{:S(2)}, u32[]{:S(2)}) collective-permute-start(bf16[64,4096]{1,0:T(8,128)(2,1)S(1)} %collective-permute-done.3.refs_4_), channel_id=1, source_target_pairs={{0,3},{1,0},{2,1},{3,2},{4,7},{5,4},{6,5},{7,6},{8,11},{9,8},{10,9... | collective-permute-start | bytes 1572872 | tf_op jit(solution)/shard_map/ppermute | solution.py:416
  33.3 19.1 %collective-permute-start.4 = (bf16[64,4096]{1,0:T(8,128)(2,1)S(1)}, bf16[64,4096]{1,0:T(8,128)(2,1)}, u32[]{:S(2)}, u32[]{:S(2)}) collective-permute-start(bf16[64,4096]{1,0:T(8,128)(2,1)S(1)} %collective-permute-done.refs_1_), channel_id=1, source_target_pairs={{0,1},{1,2},{2,3},{3,0},{4,5},{5,6},{6,7},{7,4},{8,9},{9,10},{10,1... | collective-permute-start | bytes 1572872 | tf_op jit(solution)/shard_map/ppermute | solution.py:415
  63.6 16.7 %copy-start.13 = (bf16[1,4096,512]{2,1,0:T(8,128)(2,1)S(1)}, bf16[1,4096,512]{2,1,0:T(8,128)(2,1)}, u32[]{:S(2)}) copy-start(bf16[1,4096,512]{2,1,0:T(8,128)(2,1)} %param.14) | copy-start | bytes 12582916
  75.2 11.0 %collective-permute-start.13 = (bf16[2,512,128]{2,1,0:T(8,128)(2,1)S(1)}, bf16[2,512,128]{2,1,0:T(8,128)(2,1)S(1)}, u32[]{:S(2)}, u32[]{:S(2)}) collective-permute-start(bf16[2,512,128]{2,1,0:T(8,128)(2,1)S(1)} %get-tuple-element.41), channel_id=1, source_target_pairs={{0,4},{4,8},{8,12},{12,0},{16,20},{20,24},{24,28},{28,16},{1,5},{5... | collective-permute-start | bytes 786440 | tf_op jit(solution)/shard_map/ppermute | solution.py:453
  75.3 13.1 %collective-permute-start.14 = (bf16[2,512,128]{2,1,0:T(8,128)(2,1)S(1)}, bf16[2,512,128]{2,1,0:T(8,128)(2,1)S(1)}, u32[]{:S(2)}, u32[]{:S(2)}) collective-permute-start(bf16[2,512,128]{2,1,0:T(8,128)(2,1)S(1)} %get-tuple-element.42), channel_id=1, source_target_pairs={{0,8},{4,12},{8,0},{12,4},{16,24},{20,28},{24,16},{28,20},{1,9},{5... | collective-permute-start | bytes 786440 | tf_op jit(solution)/shard_map/ppermute | solution.py:453
  77.7 11.8 %collective-permute-start.15 = (bf16[2,512,128]{2,1,0:T(8,128)(2,1)S(1)}, bf16[2,512,128]{2,1,0:T(8,128)(2,1)S(1)}, u32[]{:S(2)}, u32[]{:S(2)}) collective-permute-start(bf16[2,512,128]{2,1,0:T(8,128)(2,1)S(1)} %get-tuple-element.43), channel_id=1, source_target_pairs={{0,12},{4,0},{8,4},{12,8},{16,28},{20,16},{24,20},{28,24},{1,13},{... | collective-permute-start | bytes 786440 | tf_op jit(solution)/shard_map/ppermute | solution.py:453
  78.0 17.7 %collective-permute-start.17 = (bf16[2,512,128]{2,1,0:T(8,128)(2,1)S(1)}, bf16[2,512,128]{2,1,0:T(8,128)(2,1)S(1)}, u32[]{:S(2)}, u32[]{:S(2)}) collective-permute-start(bf16[2,512,128]{2,1,0:T(8,128)(2,1)S(1)} %get-tuple-element.45), channel_id=1, source_target_pairs={{0,4},{4,8},{8,12},{12,0},{16,20},{20,24},{24,28},{28,16},{1,5},{5... | collective-permute-start | bytes 786440 | tf_op jit(solution)/shard_map/ppermute | solution.py:453
  79.1 17.4 %collective-permute-start.18 = (bf16[2,512,128]{2,1,0:T(8,128)(2,1)S(1)}, bf16[2,512,128]{2,1,0:T(8,128)(2,1)S(1)}, u32[]{:S(2)}, u32[]{:S(2)}) collective-permute-start(bf16[2,512,128]{2,1,0:T(8,128)(2,1)S(1)} %get-tuple-element.46), channel_id=1, source_target_pairs={{0,8},{4,12},{8,0},{12,4},{16,24},{20,28},{24,16},{28,20},{1,9},{5... | collective-permute-start | bytes 786440 | tf_op jit(solution)/shard_map/ppermute | solution.py:453
  86.3 12.7 %collective-permute-start.19 = (bf16[2,512,128]{2,1,0:T(8,128)(2,1)S(1)}, bf16[2,512,128]{2,1,0:T(8,128)(2,1)S(1)}, u32[]{:S(2)}, u32[]{:S(2)}) collective-permute-start(bf16[2,512,128]{2,1,0:T(8,128)(2,1)S(1)} %get-tuple-element.47), channel_id=1, source_target_pairs={{0,12},{4,0},{8,4},{12,8},{16,28},{20,16},{24,20},{28,24},{1,13},{... | collective-permute-start | bytes 786440 | tf_op jit(solution)/shard_map/ppermute | solution.py:453
  89.5 15.0 %copy-start.15 = (bf16[1,4096,128]{2,1,0:T(8,128)(2,1)S(1)}, bf16[1,4096,128]{2,1,0:T(8,128)(2,1)}, u32[]{:S(2)}) copy-start(bf16[1,4096,128]{2,1,0:T(8,128)(2,1)} %param.15) | copy-start | bytes 3145732
  89.6 12.2 %collective-permute-start.16 = (bf16[512,128]{1,0:T(8,128)(2,1)S(1)}, bf16[512,128]{1,0:T(8,128)(2,1)S(1)}, u32[]{:S(2)}, u32[]{:S(2)}) collective-permute-start(bf16[512,128]{1,0:T(8,128)(2,1)S(1)} %fusion.18), channel_id=1, source_target_pairs={{0,16},{4,20},{8,24},{12,28},{16,0},{20,4},{24,8},{28,12},{1,17},{... | collective-permute-start | bytes 393224 | tf_op jit(solution)/shard_map/ppermute | solution.py:463
  99.1 5.4 %collective-permute-start.20 = (bf16[512,128]{1,0:T(8,128)(2,1)S(1)}, bf16[512,128]{1,0:T(8,128)(2,1)S(1)}, u32[]{:S(2)}, u32[]{:S(2)}) collective-permute-start(bf16[512,128]{1,0:T(8,128)(2,1)S(1)} %fusion.19), channel_id=1, source_target_pairs={{0,16},{4,20},{8,24},{12,28},{16,0},{20,4},{24,8},{28,12},{1,17},{... | collective-permute-start | bytes 393224 | tf_op jit(solution)/shard_map/ppermute | solution.py:463
  106.3 14.1 %collective-permute-start.22 = (bf16[64,4096]{1,0:T(8,128)(2,1)S(1)}, bf16[64,4096]{1,0:T(8,128)(2,1)S(1)}, u32[]{:S(2)}, u32[]{:S(2)}) collective-permute-start(bf16[64,4096]{1,0:T(8,128)(2,1)S(1)} %get-tuple-element.55), channel_id=1, source_target_pairs={{0,1},{1,2},{2,3},{3,0},{4,5},{5,6},{6,7},{7,4},{8,9},{9,10},{10,1... | collective-permute-start | bytes 1572872 | tf_op jit(solution)/shard_map/ppermute | solution.py:485
  107.3 31.5 %collective-permute-start.24 = (bf16[64,4096]{1,0:T(8,128)(2,1)S(1)}, bf16[64,4096]{1,0:T(8,128)(2,1)S(1)}, u32[]{:S(2)}, u32[]{:S(2)}) collective-permute-start(bf16[64,4096]{1,0:T(8,128)(2,1)S(1)} %slice.65), channel_id=1, source_target_pairs={{0,99},{1,96},{2,97},{3,98},{32,3},{33,0},{34,1},{35,2},{64,35},{6... | collective-permute-start | bytes 1572872 | tf_op jit(solution)/shard_map/ppermute | solution.py:492
  115.2 23.6 %collective-permute-start.25 = (bf16[64,4096]{1,0:T(8,128)(2,1)S(1)}, bf16[64,4096]{1,0:T(8,128)(2,1)S(1)}, u32[]{:S(2)}, u32[]{:S(2)}) collective-permute-start(bf16[64,4096]{1,0:T(8,128)(2,1)S(1)} %slice.67), channel_id=1, source_target_pairs={{0,97},{1,98},{2,99},{3,96},{32,1},{33,2},{34,3},{35,0},{64,33},{6... | collective-permute-start | bytes 1572872 | tf_op jit(solution)/shard_map/ppermute | solution.py:491
  115.2 23.4 %collective-permute-start.26 = (bf16[64,4096]{1,0:T(8,128)(2,1)S(1)}, bf16[64,4096]{1,0:T(8,128)(2,1)S(1)}, u32[]{:S(2)}, u32[]{:S(2)}) collective-permute-start(bf16[64,4096]{1,0:T(8,128)(2,1)S(1)} %get-tuple-element.56), channel_id=1, source_target_pairs={{0,3},{1,0},{2,1},{3,2},{4,7},{5,4},{6,5},{7,6},{8,11},{9,8},{10,9... | collective-permute-start | bytes 1572872 | tf_op jit(solution)/shard_map/ppermute | solution.py:486
  117.2 33.4 %collective-permute-start.21 = (bf16[128,4096]{1,0:T(8,128)(2,1)S(1)}, bf16[128,4096]{1,0:T(8,128)(2,1)S(1)}, u32[]{:S(2)}, u32[]{:S(2)}) collective-permute-start(bf16[128,4096]{1,0:T(8,128)(2,1)S(1)} %fusion), channel_id=1, source_target_pairs={{0,96},{32,0},{64,32},{96,64},{1,97},{33,1},{65,33},{97,65},{2,98}... | collective-permute-start | bytes 3145736 | tf_op jit(solution)/shard_map/ppermute | solution.py:488
  120.5 25.2 %collective-permute-start.23 = (bf16[64,4096]{1,0:T(8,128)(2,1)S(1)}, bf16[64,4096]{1,0:T(8,128)(2,1)S(1)}, u32[]{:S(2)}, u32[]{:S(2)}) collective-permute-start(bf16[64,4096]{1,0:T(8,128)(2,1)S(1)} %add_convert_fusion.3), channel_id=1, source_target_pairs={{0,97},{1,98},{2,99},{3,96},{32,1},{33,2},{34,3},{35,0},{64,33},{6... | collective-permute-start | bytes 1572872 | tf_op jit(solution)/shard_map/ppermute | solution.py:494
  138.8 11.8 %collective-permute-start.27 = (bf16[64,4096]{1,0:T(8,128)(2,1)S(1)}, bf16[64,4096]{1,0:T(8,128)(2,1)S(1)}, u32[]{:S(2)}, u32[]{:S(2)}) collective-permute-start(bf16[64,4096]{1,0:T(8,128)(2,1)S(1)} %add_convert_fusion.1), channel_id=1, source_target_pairs={{0,99},{1,96},{2,97},{3,98},{32,3},{33,0},{34,1},{35,2},{64,35},{6... | collective-permute-start | bytes 1572872 | tf_op jit(solution)/shard_map/ppermute | solution.py:496
  (15 other events, 71.7 us)

commit v5 on v4

--- a/solution.py
+++ b/solution.py
@@ -211,7 +211,6 @@
             bytes_accessed=9 << 20,
             transcendentals=0,
         ),
-        name="attn_grad",
     )(rows, *pieces, out_weight)
 
 
@@ -429,6 +428,9 @@
     for distance in (1, 2, 3):
         kv_chunks += [along[distance], crossed[distance]]
 
+    sent_key_weight = send(key_weight[0], SECTION, ring(4, -1))
+    sent_value_weight = send(value_weight[0], SECTION, ring(4, -1))
+
     index = jnp.arange(8, dtype=jnp.int32)
     source = ((own_x + index % 2) % 2) * 4 + (own_z + index // 2) % 4
     table = jnp.arange(8, dtype=jnp.int32)
@@ -469,7 +471,9 @@
     query_terms = []
     for distance in range(4):
         query_terms.append(dot_nt(chunk_of(query_grad, distance), query_weight[0]))
+    query_terms[0] = query_terms[0].astype(bf16)
     query_terms = lax.optimization_barrier(tuple(query_terms))
+    own = send(query_terms[0], SECTION, ring(4, -1))
 
     value_grad = with_pair(value_sum)
     key_grad = with_pair(key_sum)
@@ -484,20 +488,21 @@
     far = term_of(2)
     from_left = send(far[:half_rows], TP, ring(4, 1))
     from_right = send(far[half_rows:], TP, ring(4, -1))
-    own_term = term_of(0)
-    own = send(own_term, SECTION, ring(4, -1))
     right, left = lax.optimization_barrier((term_of(1), term_of(3)))
     joint = (SECTION, TP)
     low_a = send(right[half_rows:], joint, joint_ring(1))
     top_b = send(left[:half_rows], joint, joint_ring(-1))
+    rows = send(chunk_of(kv_grad, 0), SECTION, ring(4, -1))
+    own = own.astype(f32) + dot_nt(rows[:, :HD], sent_key_weight)
+    own = lax.optimization_barrier(own + dot_nt(rows[:, HD:], sent_value_weight))
     top_a = (right[:half_rows].astype(f32) + from_left.astype(f32)).astype(bf16)
     top_a = send(top_a, joint, joint_ring(1))
     low_b = (left[half_rows:].astype(f32) + from_right.astype(f32)).astype(bf16)
     low_b = send(low_b, joint, joint_ring(-1))
     sent = jnp.concatenate(
         [
-            own[:half_rows].astype(f32) + top_a.astype(f32) + top_b.astype(f32),
-            own[half_rows:].astype(f32) + low_a.astype(f32) + low_b.astype(f32),
+            own[:half_rows] + top_a.astype(f32) + top_b.astype(f32),
+            own[half_rows:] + low_a.astype(f32) + low_b.astype(f32),
         ],
         axis=0,
     ).astype(bf16)

time: 153 us -> 179 us (1.17)
  waiting for transfers between devices: 37.6 us -> 63.8 us
    ppermute x1, waiting for transfers between devices: 8.31 us -> 21.2 us  [per_device(): from_right = send(far[half_rows:], TP, ring(4, -1))]
    ppermute x1, waiting for transfers between devices: 0.01 us -> 12.7 us  [per_device(): low_a = send(right[half_rows:], joint, joint_ring(1))]
    ppermute x1, starting transfers between devices: 9.81 us -> 0.72 us  [per_device(): top_a = send(top_a, joint, joint_ring(1))]
    ppermute x6, waiting for transfers between devices: 7.68 us -> 12.8 us  [along_z(): received = send(groups[distance], CTX, z_ring(shift))]
    ppermute x1, waiting for transfers between devices: 4.91 us -> 0.01 us  [per_device(): low_b = send(low_b, joint, joint_ring(-1))]
    ppermute x1 -> x4, starting transfers between devices: 3.18 us -> 7.55 us  [the longest x1 3.99 us: per_device(): own = send(query_terms[0], SECTION, ring(4, -1))]
    ppermute x2, starting transfers between devices: 0.01 us -> 3.56 us  [per_device(): crossed[distance] = send(kv_pair, CTX, z_ring(shift))]
    ppermute x1, starting transfers between devices: 7.9 us -> 11.3 us  [per_device(): top_b = send(left[:half_rows], joint, joint_ring(-1))]
  transfers between devices with their start and end apart: 28 -> 31, of which waited for: 11 -> 13; matrix products, arithmetic and copies ran while one was open for 7% -> 7% of each run, Pallas kernels for 7% -> 19%
where the time goes in v5:
time: 179 us; the launch traced here: 178 us
  waiting for transfers between devices  63.8 us (36%)
  starting transfers between devices  57.2 us (32%)
  Pallas kernels  33.8 us (19%)
  matrix products  9.4 us (5%)
  local copies, waits for them, and re-layouts  9.34 us (5%)
  other arithmetic  3.38 us (2%)
    ppermute x1, waiting for transfers between devices, per_device(): from_right = send(far[half_rows:], TP, ring(4, -1))  21.2 us
    ppermute x6, waiting for transfers between devices, along_z(): received = send(groups[distance], CTX, z_ring(shift))  12.8 us
    ppermute x1, waiting for transfers between devices, per_device(): low_a = send(right[half_rows:], joint, joint_ring(1))  12.7 us
    pallas_call x1, Pallas kernels, key_call(): pl.pallas_call(key_kernel, grid_spec=pltpu.PrefetchScalarGridSpec(num_sca...  11.6 us
    ppermute x1, starting transfers between devices, per_device(): top_b = send(left[:half_rows], joint, joint_ring(-1))  11.3 us
    pallas_call x1, Pallas kernels, forward_call(): pl.pallas_call(forward_kernel, grid_spec=pltpu.PrefetchScalarGridSpec(num...  11 us
    dot_general x9, matrix products, dot_nt(): lax.dot_general(lhs, rhs, (((1,), (1,)), ((), ())), preferred_element_typ...  9.4 us
    ppermute x6, starting transfers between devices, along_z(): received = send(groups[distance], CTX, z_ring(shift))  6.84 us
  transfers between devices with their start and end apart: 31, of which 13 were waited for; matrix products, arithmetic and copies ran while one was open for 7% of the time, Pallas kernels for 19%

profile of v5, /device:TPU:1, one launch (start us, length us, event | category | flops | bytes accessed | tf_op | source)
XLA Modules:
  0.0 177.9 jit_solution(3712931189842942358)
XLA Ops:
  1.7 3.6 %collective-permute-start.6 = (bf16[512,256]{1,0:T(8,128)(2,1)S(1)}, bf16[512,256]{1,0:T(8,128)(2,1)}, u32[]{:S(2)}, u32[]{:S(2)}) collective-permute-start(bf16[512,256]{1,0:T(8,128)(2,1)S(1)} %pad_maximum_fusion.5.refs_0_), channel_id=1, source_target_pairs={{0,16},{4,20},{8,24},{12,28},{16,0},{20,4},{24,8},{28,12},{1,17},{... | collective-permute-start | bytes 786440 | tf_op jit(solution)/shard_map/ppermute | solution.py:420
  5.4 3.8 %collective-permute-start.7 = (bf16[512,256]{1,0:T(8,128)(2,1)S(1)}, bf16[512,256]{1,0:T(8,128)(2,1)S(1)}, u32[]{:S(2)}, u32[]{:S(2)}) collective-permute-start(bf16[512,256]{1,0:T(8,128)(2,1)S(1)} %pad_maximum_fusion.5.refs_0_), channel_id=1, source_target_pairs={{0,12},{4,0},{8,4},{12,8},{16,28},{20,16},{24,20},{28,24},{1,13},{... | collective-permute-start | bytes 786440 | tf_op jit(solution)/shard_map/ppermute | solution.py:423
  9.1 2.3 %slice_bitcast_fusion = (bf16[64,4096]{1,0:T(8,128)(2,1)}, bf16[64,4096]{1,0:T(8,128)(2,1)}) fusion(bf16[1,128,4096]{2,1,0:T(8,128)(2,1)} %param.13), kind=kLoop, calls=%fused_computation.29 | loop fusion | bytes 2097152 | tf_op jit(solution)/shard_map/slice | solution.py:411
  14.8 4.5 %collective-permute-done.7.refs_2_ = bf16[512,256]{1,0:T(8,128)(2,1)S(1)} collective-permute-done((bf16[512,256]{1,0:T(8,128)(2,1)S(1)}, bf16[512,256]{1,0:T(8,128)(2,1)S(1)}, u32[]{:S(2)}, u32[]{:S(2)}) %collective-permute-start.7) | collective-permute-done | bytes 262176 | tf_op jit(solution)/shard_map/ppermute | solution.py:423
  20.0 3.6 %collective-permute-start.8 = (bf16[512,256]{1,0:T(8,128)(2,1)}, bf16[512,256]{1,0:T(8,128)(2,1)S(1)}, u32[]{:S(2)}, u32[]{:S(2)}) collective-permute-start(bf16[512,256]{1,0:T(8,128)(2,1)} %collective-permute-done.6.refs_1_), channel_id=1, source_target_pairs={{0,12},{4,0},{8,4},{12,8},{16,28},{20,16},{24,20},{28,24},{1,13},{... | collective-permute-start | bytes 786440 | tf_op jit(solution)/shard_map/ppermute | solution.py:425
  25.9 1.4 collective-permute-start.2
  31.7 2.7 %collective-permute-start.5 = (bf16[64,4096]{1,0:T(8,128)(2,1)S(1)}, bf16[64,4096]{1,0:T(8,128)(2,1)}, u32[]{:S(2)}, u32[]{:S(2)}) collective-permute-start(bf16[64,4096]{1,0:T(8,128)(2,1)S(1)} %collective-permute-done.3.refs_4_), channel_id=1, source_target_pairs={{0,3},{1,0},{2,1},{3,2},{4,7},{5,4},{6,5},{7,6},{8,11},{9,8},{10,9... | collective-permute-start | bytes 1572872 | tf_op jit(solution)/shard_map/ppermute | solution.py:415
  34.9 3.3 %collective-permute-start.23 = (bf16[4096,128]{1,0:T(8,128)(2,1)}, bf16[4096,128]{1,0:T(8,128)(2,1)S(1)}, u32[]{:S(2)}, u32[]{:S(2)}) collective-permute-start(bf16[4096,128]{1,0:T(8,128)(2,1)} %bitcast.59), channel_id=1, source_target_pairs={{0,96},{32,0},{64,32},{96,64},{1,97},{33,1},{65,33},{97,65},{2,98}... | collective-permute-start | bytes 3145736 | tf_op jit(solution)/shard_map/ppermute | solution.py:431
  42.0 11.0 %shard_map.113 = (bf16[17,4,256,256]{3,2,1,0:T(8,128)(2,1)S(1)}, f32[2,128,1024]{2,1,0:T(8,128)S(1)}, f32[2,8,1024]{2,1,0:T(8,128)S(1)}, f32[17,1,1024]{2,1,0:T(1,128)S(1)}, bf16[16,256,256]{2,1,0:T(8,128)(2,1)S(1)}) custom-call(s32[1]{0:T(128)S(1)} %bitcast.56, s32[16]{0:T(128)S(1)} %reshape.115.ids_ref, bf16[512,256]{1,0:T(8,128)(2,1)S(1)} %pad_maximum_fusion.5.refs_0_, ...), custom_call_target="tpu_custom_call" | custom-call | flops 2281701376 | bytes 13631488 | tf_op jit(solution)/shard_map/pallas_call | solution.py:131
  53.3 5.1 %shard_map.112.grad_ref = bf16[512,512]{1,0:T(8,128)(2,1)S(1)} custom-call(s32[7]{0:T(128)S(1)} %broadcast_multiply_fusion.rows_ref, bf16[128,4096]{1,0:T(8,128)(2,1)S(1)} %bitcast.52, bf16[64,4096]{1,0:T(8,128)(2,1)S(1)} %collective-permute-done.refs_1_, bf16[64,4096]{1,0:T(8,128)(2,1)S(1)} %collective-permute-done.1.refs_2_, ...), custom_call_target="tpu_custom_call" | custom-call | flops 2147483648 | bytes 9437184 | tf_op jit(solution)/shard_map/pallas_call | solution.py:194
  58.4 6.2 %attn_value_grad.1 = (bf16[2,512,128]{2,1,0:T(8,128)(2,1)S(1)}, bf16[2,512,128]{2,1,0:T(8,128)(2,1)S(1)}, bf16[2,512,128]{2,1,0:T(8,128)(2,1)S(1)}, bf16[2,512,128]{2,1,0:T(8,128)(2,1)S(1)}) custom-call(s32[1]{0:T(128)S(1)} %bitcast.57, s32[16]{0:T(128)S(1)} %reshape.115.ids_ref, bf16[512,512]{1,0:T(8,128)(2,1)S(1)} %shard_map.112.grad_ref, ...), custom_call_target="tpu_custom_call" | custom-call | flops 1140850688 | bytes 11534336 | tf_op jit(solution)/shard_map/attn_value_grad/pallas_call | solution.py:259
  64.6 11.6 %shard_map.114 = (bf16[512,512]{1,0:T(8,128)(2,1)S(1)}, bf16[2,512,128]{2,1,0:T(8,128)(2,1)S(1)}, bf16[2,512,128]{2,1,0:T(8,128)(2,1)S(1)}, bf16[2,512,128]{2,1,0:T(8,128)(2,1)S(1)}, bf16[2,512,128]{2,1,0:T(8,128)(2,1)S(1)}) custom-call(s32[1]{0:T(128)S(1)} %bitcast.58, s32[16]{0:T(128)S(1)} %reshape.115.ids_ref, bf16[512,512]{1,0:T(8,128)(2,1)S(1)} %shard_map.112.grad_ref, ...), custom_call_target="tpu_custom_call" | custom-call | flops 3422552064 | bytes 14680064 | tf_op jit(solution)/shard_map/pallas_call | solution.py:358
  76.2 1.5 fusion.7
  77.7 1.5 fusion.5
  79.2 1.5 fusion.3
  81.4 1.6 collective-permute-start.15
  83.6 1.5 convolution_convert_fusion
  85.1 2.1 %collective-permute-done.16 = bf16[2,512,128]{2,1,0:T(8,128)(2,1)S(1)} collective-permute-done((bf16[2,512,128]{2,1,0:T(8,128)(2,1)S(1)}, bf16[2,512,128]{2,1,0:T(8,128)(2,1)S(1)}, u32[]{:S(2)}, u32[]{:S(2)}) %collective-permute-start.16) | collective-permute-done | bytes 262176 | tf_op jit(solution)/shard_map/ppermute | solution.py:455
  87.2 2.2 %collective-permute-start.20 = (bf16[2,512,128]{2,1,0:T(8,128)(2,1)S(1)}, bf16[2,512,128]{2,1,0:T(8,128)(2,1)S(1)}, u32[]{:S(2)}, u32[]{:S(2)}) collective-permute-start(bf16[2,512,128]{2,1,0:T(8,128)(2,1)S(1)} %get-tuple-element.47), channel_id=1, source_target_pairs={{0,12},{4,0},{8,4},{12,8},{16,28},{20,16},{24,20},{28,24},{1,13},{... | collective-permute-start | bytes 786440 | tf_op jit(solution)/shard_map/ppermute | solution.py:455
  89.5 1.7 collective-permute-start.19
  91.2 7.2 %collective-permute-done.14 = bf16[2,512,128]{2,1,0:T(8,128)(2,1)S(1)} collective-permute-done((bf16[2,512,128]{2,1,0:T(8,128)(2,1)S(1)}, bf16[2,512,128]{2,1,0:T(8,128)(2,1)S(1)}, u32[]{:S(2)}, u32[]{:S(2)}) %collective-permute-start.14) | collective-permute-done | bytes 262176 | tf_op jit(solution)/shard_map/ppermute | solution.py:455
  98.7 4.0 %collective-permute-start.13 = (bf16[128,4096]{1,0:T(8,128)(2,1)S(1)}, bf16[128,4096]{1,0:T(8,128)(2,1)S(1)}, u32[]{:S(2)}, u32[]{:S(2)}) collective-permute-start(bf16[128,4096]{1,0:T(8,128)(2,1)S(1)} %convolution_convert_fusion), channel_id=1, source_target_pairs={{0,96},{32,0},{64,32},{96,64},{1,97},{33,1},{65,33},{97,65},{2,98}... | collective-permute-start | bytes 3145736 | tf_op jit(solution)/shard_map/ppermute | solution.py:476
  102.7 2.5 %collective-permute-start.17 = (bf16[512,128]{1,0:T(8,128)(2,1)S(1)}, bf16[512,128]{1,0:T(8,128)(2,1)S(1)}, u32[]{:S(2)}, u32[]{:S(2)}) collective-permute-start(bf16[512,128]{1,0:T(8,128)(2,1)S(1)} %fusion.20), channel_id=1, source_target_pairs={{0,16},{4,20},{8,24},{12,28},{16,0},{20,4},{24,8},{28,12},{1,17},{... | collective-permute-start | bytes 393224 | tf_op jit(solution)/shard_map/ppermute | solution.py:465
  105.1 3.3 %collective-permute-done.18 = bf16[2,512,128]{2,1,0:T(8,128)(2,1)S(1)} collective-permute-done((bf16[2,512,128]{2,1,0:T(8,128)(2,1)S(1)}, bf16[2,512,128]{2,1,0:T(8,128)(2,1)S(1)}, u32[]{:S(2)}, u32[]{:S(2)}) %collective-permute-start.18) | collective-permute-done | bytes 262176 | tf_op jit(solution)/shard_map/ppermute | solution.py:455
  108.5 2.5 %collective-permute-start.21 = (bf16[512,128]{1,0:T(8,128)(2,1)S(1)}, bf16[512,128]{1,0:T(8,128)(2,1)S(1)}, u32[]{:S(2)}, u32[]{:S(2)}) collective-permute-start(bf16[512,128]{1,0:T(8,128)(2,1)S(1)} %fusion.21), channel_id=1, source_target_pairs={{0,16},{4,20},{8,24},{12,28},{16,0},{20,4},{24,8},{28,12},{1,17},{... | collective-permute-start | bytes 393224 | tf_op jit(solution)/shard_map/ppermute | solution.py:465
  111.1 4.3 %collective-permute-done.21 = bf16[512,128]{1,0:T(8,128)(2,1)S(1)} collective-permute-done((bf16[512,128]{1,0:T(8,128)(2,1)S(1)}, bf16[512,128]{1,0:T(8,128)(2,1)S(1)}, u32[]{:S(2)}, u32[]{:S(2)}) %collective-permute-start.21) | collective-permute-done | bytes 131104 | tf_op jit(solution)/shard_map/ppermute | solution.py:465
  118.2 11.3 %collective-permute-start.27 = (bf16[64,4096]{1,0:T(8,128)(2,1)S(1)}, bf16[64,4096]{1,0:T(8,128)(2,1)S(1)}, u32[]{:S(2)}, u32[]{:S(2)}) collective-permute-start(bf16[64,4096]{1,0:T(8,128)(2,1)S(1)} %slice.73), channel_id=1, source_target_pairs={{0,99},{1,96},{2,97},{3,98},{32,3},{33,0},{34,1},{35,2},{64,35},{6... | collective-permute-start | bytes 1572872 | tf_op jit(solution)/shard_map/ppermute | solution.py:494
  130.3 21.2 %collective-permute-done.29 = bf16[64,4096]{1,0:T(8,128)(2,1)S(1)} collective-permute-done((bf16[64,4096]{1,0:T(8,128)(2,1)S(1)}, bf16[64,4096]{1,0:T(8,128)(2,1)S(1)}, u32[]{:S(2)}, u32[]{:S(2)}) %collective-permute-start.29) | collective-permute-done | bytes 524320 | tf_op jit(solution)/shard_map/ppermute | solution.py:490
  151.7 1.8 %collective-permute-start.28 = (bf16[64,4096]{1,0:T(8,128)(2,1)S(1)}, bf16[64,4096]{1,0:T(8,128)(2,1)S(1)}, u32[]{:S(2)}, u32[]{:S(2)}) collective-permute-start(bf16[64,4096]{1,0:T(8,128)(2,1)S(1)} %slice.75), channel_id=1, source_target_pairs={{0,97},{1,98},{2,99},{3,96},{32,1},{33,2},{34,3},{35,0},{64,33},{6... | collective-permute-start | bytes 1572872 | tf_op jit(solution)/shard_map/ppermute | solution.py:493
  155.2 1.9 %collective-permute-start.30 = (bf16[64,4096]{1,0:T(8,128)(2,1)S(1)}, bf16[64,4096]{1,0:T(8,128)(2,1)S(1)}, u32[]{:S(2)}, u32[]{:S(2)}) collective-permute-start(bf16[64,4096]{1,0:T(8,128)(2,1)S(1)} %add_convert_fusion), channel_id=1, source_target_pairs={{0,99},{1,96},{2,97},{3,98},{32,3},{33,0},{34,1},{35,2},{64,35},{6... | collective-permute-start | bytes 1572872 | tf_op jit(solution)/shard_map/ppermute | solution.py:501
  158.1 12.7 %collective-permute-done.28 = bf16[64,4096]{1,0:T(8,128)(2,1)S(1)} collective-permute-done((bf16[64,4096]{1,0:T(8,128)(2,1)S(1)}, bf16[64,4096]{1,0:T(8,128)(2,1)S(1)}, u32[]{:S(2)}, u32[]{:S(2)}) %collective-permute-start.28) | collective-permute-done | bytes 524320 | tf_op jit(solution)/shard_map/ppermute | solution.py:493
  170.8 5.6 %collective-permute-done.26 = bf16[64,4096]{1,0:T(8,128)(2,1)S(1)} collective-permute-done((bf16[64,4096]{1,0:T(8,128)(2,1)S(1)}, bf16[64,4096]{1,0:T(8,128)(2,1)S(1)}, u32[]{:S(2)}, u32[]{:S(2)}) %collective-permute-start.26) | collective-permute-done | bytes 524320 | tf_op jit(solution)/shard_map/ppermute | solution.py:499
  (100 shorter events, 26.1 us)
Async XLA Ops:
  0.6 37.6 %copy-start.2 = (bf16[1,512,512]{2,1,0:T(8,128)(2,1)S(1)}, bf16[1,512,512]{2,1,0:T(8,128)(2,1)}, u32[]{:S(2)}) copy-start(bf16[1,512,512]{2,1,0:T(8,128)(2,1)} %param.10) | copy-start | bytes 1572868
  1.7 12.4 %collective-permute-start.6 = (bf16[512,256]{1,0:T(8,128)(2,1)S(1)}, bf16[512,256]{1,0:T(8,128)(2,1)}, u32[]{:S(2)}, u32[]{:S(2)}) collective-permute-start(bf16[512,256]{1,0:T(8,128)(2,1)S(1)} %pad_maximum_fusion.5.refs_0_), channel_id=1, source_target_pairs={{0,16},{4,20},{8,24},{12,28},{16,0},{20,4},{24,8},{28,12},{1,17},{... | collective-permute-start | bytes 786440 | tf_op jit(solution)/shard_map/ppermute | solution.py:420
  5.4 13.9 %collective-permute-start.7 = (bf16[512,256]{1,0:T(8,128)(2,1)S(1)}, bf16[512,256]{1,0:T(8,128)(2,1)S(1)}, u32[]{:S(2)}, u32[]{:S(2)}) collective-permute-start(bf16[512,256]{1,0:T(8,128)(2,1)S(1)} %pad_maximum_fusion.5.refs_0_), channel_id=1, source_target_pairs={{0,12},{4,0},{8,4},{12,8},{16,28},{20,16},{24,20},{28,24},{1,13},{... | collective-permute-start | bytes 786440 | tf_op jit(solution)/shard_map/ppermute | solution.py:423
  9.1 14.4 %collective-permute-start.9 = (bf16[512,256]{1,0:T(8,128)(2,1)S(1)}, bf16[512,256]{1,0:T(8,128)(2,1)}, u32[]{:S(2)}, u32[]{:S(2)}) collective-permute-start(bf16[512,256]{1,0:T(8,128)(2,1)S(1)} %pad_maximum_fusion.5.refs_0_), channel_id=1, source_target_pairs={{0,8},{4,12},{8,0},{12,4},{16,24},{20,28},{24,16},{28,20},{1,9},{5... | collective-permute-start | bytes 786440 | tf_op jit(solution)/shard_map/ppermute | solution.py:423
  11.4 14.5 %collective-permute-start = (bf16[64,4096]{1,0:T(8,128)(2,1)}, bf16[64,4096]{1,0:T(8,128)(2,1)S(1)}, u32[]{:S(2)}, u32[]{:S(2)}) collective-permute-start(bf16[64,4096]{1,0:T(8,128)(2,1)} %get-tuple-element.58), channel_id=1, source_target_pairs={{0,1},{1,2},{2,3},{3,0},{4,5},{5,6},{6,7},{7,4},{8,9},{9,10},{10,1... | collective-permute-start | bytes 1572872 | tf_op jit(solution)/shard_map/ppermute | solution.py:412
  12.7 14.7 %collective-permute-start.3 = (bf16[64,4096]{1,0:T(8,128)(2,1)}, bf16[64,4096]{1,0:T(8,128)(2,1)S(1)}, u32[]{:S(2)}, u32[]{:S(2)}) collective-permute-start(bf16[64,4096]{1,0:T(8,128)(2,1)} %get-tuple-element.57), channel_id=1, source_target_pairs={{0,3},{1,0},{2,1},{3,2},{4,7},{5,4},{6,5},{7,6},{8,11},{9,8},{10,9... | collective-permute-start | bytes 1572872 | tf_op jit(solution)/shard_map/ppermute | solution.py:413
  14.1 9.8 %collective-permute-start.11 = (bf16[512,256]{1,0:T(8,128)(2,1)S(1)}, bf16[512,256]{1,0:T(8,128)(2,1)S(1)}, u32[]{:S(2)}, u32[]{:S(2)}) collective-permute-start(bf16[512,256]{1,0:T(8,128)(2,1)S(1)} %pad_maximum_fusion.5.refs_0_), channel_id=1, source_target_pairs={{0,4},{4,8},{8,12},{12,0},{16,20},{20,24},{24,28},{28,16},{1,5},{5... | collective-permute-start | bytes 786440 | tf_op jit(solution)/shard_map/ppermute | solution.py:423
  20.0 7.7 %collective-permute-start.8 = (bf16[512,256]{1,0:T(8,128)(2,1)}, bf16[512,256]{1,0:T(8,128)(2,1)S(1)}, u32[]{:S(2)}, u32[]{:S(2)}) collective-permute-start(bf16[512,256]{1,0:T(8,128)(2,1)} %collective-permute-done.6.refs_1_), channel_id=1, source_target_pairs={{0,12},{4,0},{8,4},{12,8},{16,28},{20,16},{24,20},{28,24},{1,13},{... | collective-permute-start | bytes 786440 | tf_op jit(solution)/shard_map/ppermute | solution.py:425
  23.6 7.5 %collective-permute-start.10 = (bf16[512,256]{1,0:T(8,128)(2,1)}, bf16[512,256]{1,0:T(8,128)(2,1)S(1)}, u32[]{:S(2)}, u32[]{:S(2)}) collective-permute-start(bf16[512,256]{1,0:T(8,128)(2,1)} %collective-permute-done.9.refs_4_), channel_id=1, source_target_pairs={{0,16},{4,20},{8,24},{12,28},{16,0},{20,4},{24,8},{28,12},{1,17},{... | collective-permute-start | bytes 786440 | tf_op jit(solution)/shard_map/ppermute | solution.py:426
  24.6 28.4 %collective-permute-start.1 = (bf16[64,4096]{1,0:T(8,128)(2,1)}, bf16[64,4096]{1,0:T(8,128)(2,1)S(1)}, u32[]{:S(2)}, u32[]{:S(2)}) collective-permute-start(bf16[64,4096]{1,0:T(8,128)(2,1)} %get-tuple-element.57), channel_id=1, source_target_pairs={{0,1},{1,2},{2,3},{3,0},{4,5},{5,6},{6,7},{7,4},{8,9},{9,10},{10,1... | collective-permute-start | bytes 1572872 | tf_op jit(solution)/shard_map/ppermute | solution.py:416
  25.9 27.4 %collective-permute-start.2 = (bf16[64,4096]{1,0:T(8,128)(2,1)}, bf16[64,4096]{1,0:T(8,128)(2,1)S(1)}, u32[]{:S(2)}, u32[]{:S(2)}) collective-permute-start(bf16[64,4096]{1,0:T(8,128)(2,1)} %get-tuple-element.58), channel_id=1, source_target_pairs={{0,3},{1,0},{2,1},{3,2},{4,7},{5,4},{6,5},{7,6},{8,11},{9,8},{10,9... | collective-permute-start | bytes 1572872 | tf_op jit(solution)/shard_map/ppermute | solution.py:417
  27.3 7.6 %collective-permute-start.12 = (bf16[512,256]{1,0:T(8,128)(2,1)}, bf16[512,256]{1,0:T(8,128)(2,1)}, u32[]{:S(2)}, u32[]{:S(2)}) collective-permute-start(bf16[512,256]{1,0:T(8,128)(2,1)} %collective-permute-done.6.refs_1_), channel_id=1, source_target_pairs={{0,4},{4,8},{8,12},{12,0},{16,20},{20,24},{24,28},{28,16},{1,5},{5... | collective-permute-start | bytes 786440 | tf_op jit(solution)/shard_map/ppermute | solution.py:425
  28.4 24.9 %collective-permute-start.4 = (bf16[64,4096]{1,0:T(8,128)(2,1)S(1)}, bf16[64,4096]{1,0:T(8,128)(2,1)S(1)}, u32[]{:S(2)}, u32[]{:S(2)}) collective-permute-start(bf16[64,4096]{1,0:T(8,128)(2,1)S(1)} %collective-permute-done.refs_1_), channel_id=1, source_target_pairs={{0,1},{1,2},{2,3},{3,0},{4,5},{5,6},{6,7},{7,4},{8,9},{9,10},{10,1... | collective-permute-start | bytes 1572872 | tf_op jit(solution)/shard_map/ppermute | solution.py:414
  31.7 21.6 %collective-permute-start.5 = (bf16[64,4096]{1,0:T(8,128)(2,1)S(1)}, bf16[64,4096]{1,0:T(8,128)(2,1)}, u32[]{:S(2)}, u32[]{:S(2)}) collective-permute-start(bf16[64,4096]{1,0:T(8,128)(2,1)S(1)} %collective-permute-done.3.refs_4_), channel_id=1, source_target_pairs={{0,3},{1,0},{2,1},{3,2},{4,7},{5,4},{6,5},{7,6},{8,11},{9,8},{10,9... | collective-permute-start | bytes 1572872 | tf_op jit(solution)/shard_map/ppermute | solution.py:415
  34.9 116.7 %collective-permute-start.23 = (bf16[4096,128]{1,0:T(8,128)(2,1)}, bf16[4096,128]{1,0:T(8,128)(2,1)S(1)}, u32[]{:S(2)}, u32[]{:S(2)}) collective-permute-start(bf16[4096,128]{1,0:T(8,128)(2,1)} %bitcast.59), channel_id=1, source_target_pairs={{0,96},{32,0},{64,32},{96,64},{1,97},{33,1},{65,33},{97,65},{2,98}... | collective-permute-start | bytes 3145736 | tf_op jit(solution)/shard_map/ppermute | solution.py:431
  53.0 100.4 %collective-permute-start.24 = (bf16[4096,128]{1,0:T(8,128)(2,1)S(1)}, bf16[4096,128]{1,0:T(8,128)(2,1)S(1)}, u32[]{:S(2)}, u32[]{:S(2)}) collective-permute-start(bf16[4096,128]{1,0:T(8,128)(2,1)S(1)} %bitcast.63), channel_id=1, source_target_pairs={{0,96},{32,0},{64,32},{96,64},{1,97},{33,1},{65,33},{97,65},{2,98}... | collective-permute-start | bytes 3145736 | tf_op jit(solution)/shard_map/ppermute | solution.py:432
  80.7 6.5 %collective-permute-start.16 = (bf16[2,512,128]{2,1,0:T(8,128)(2,1)S(1)}, bf16[2,512,128]{2,1,0:T(8,128)(2,1)S(1)}, u32[]{:S(2)}, u32[]{:S(2)}) collective-permute-start(bf16[2,512,128]{2,1,0:T(8,128)(2,1)S(1)} %get-tuple-element.43), channel_id=1, source_target_pairs={{0,12},{4,0},{8,4},{12,8},{16,28},{20,16},{24,20},{28,24},{1,13},{... | collective-permute-start | bytes 786440 | tf_op jit(solution)/shard_map/ppermute | solution.py:455
  81.4 8.1 %collective-permute-start.15 = (bf16[2,512,128]{2,1,0:T(8,128)(2,1)S(1)}, bf16[2,512,128]{2,1,0:T(8,128)(2,1)S(1)}, u32[]{:S(2)}, u32[]{:S(2)}) collective-permute-start(bf16[2,512,128]{2,1,0:T(8,128)(2,1)S(1)} %get-tuple-element.42), channel_id=1, source_target_pairs={{0,8},{4,12},{8,0},{12,4},{16,24},{20,28},{24,16},{28,20},{1,9},{5... | collective-permute-start | bytes 786440 | tf_op jit(solution)/shard_map/ppermute | solution.py:455
  83.0 15.4 %collective-permute-start.14 = (bf16[2,512,128]{2,1,0:T(8,128)(2,1)S(1)}, bf16[2,512,128]{2,1,0:T(8,128)(2,1)S(1)}, u32[]{:S(2)}, u32[]{:S(2)}) collective-permute-start(bf16[2,512,128]{2,1,0:T(8,128)(2,1)S(1)} %get-tuple-element.41), channel_id=1, source_target_pairs={{0,4},{4,8},{8,12},{12,0},{16,20},{20,24},{24,28},{28,16},{1,5},{5... | collective-permute-start | bytes 786440 | tf_op jit(solution)/shard_map/ppermute | solution.py:455
  87.2 11.5 %collective-permute-start.20 = (bf16[2,512,128]{2,1,0:T(8,128)(2,1)S(1)}, bf16[2,512,128]{2,1,0:T(8,128)(2,1)S(1)}, u32[]{:S(2)}, u32[]{:S(2)}) collective-permute-start(bf16[2,512,128]{2,1,0:T(8,128)(2,1)S(1)} %get-tuple-element.47), channel_id=1, source_target_pairs={{0,12},{4,0},{8,4},{12,8},{16,28},{20,16},{24,20},{28,24},{1,13},{... | collective-permute-start | bytes 786440 | tf_op jit(solution)/shard_map/ppermute | solution.py:455
  89.5 13.2 %collective-permute-start.19 = (bf16[2,512,128]{2,1,0:T(8,128)(2,1)S(1)}, bf16[2,512,128]{2,1,0:T(8,128)(2,1)S(1)}, u32[]{:S(2)}, u32[]{:S(2)}) collective-permute-start(bf16[2,512,128]{2,1,0:T(8,128)(2,1)S(1)} %get-tuple-element.46), channel_id=1, source_target_pairs={{0,8},{4,12},{8,0},{12,4},{16,24},{20,28},{24,16},{28,20},{1,9},{5... | collective-permute-start | bytes 786440 | tf_op jit(solution)/shard_map/ppermute | solution.py:455
  98.4 10.0 %collective-permute-start.18 = (bf16[2,512,128]{2,1,0:T(8,128)(2,1)S(1)}, bf16[2,512,128]{2,1,0:T(8,128)(2,1)S(1)}, u32[]{:S(2)}, u32[]{:S(2)}) collective-permute-start(bf16[2,512,128]{2,1,0:T(8,128)(2,1)S(1)} %get-tuple-element.45), channel_id=1, source_target_pairs={{0,4},{4,8},{8,12},{12,0},{16,20},{20,24},{24,28},{28,16},{1,5},{5... | collective-permute-start | bytes 786440 | tf_op jit(solution)/shard_map/ppermute | solution.py:455
  98.7 59.0 %collective-permute-start.13 = (bf16[128,4096]{1,0:T(8,128)(2,1)S(1)}, bf16[128,4096]{1,0:T(8,128)(2,1)S(1)}, u32[]{:S(2)}, u32[]{:S(2)}) collective-permute-start(bf16[128,4096]{1,0:T(8,128)(2,1)S(1)} %convolution_convert_fusion), channel_id=1, source_target_pairs={{0,96},{32,0},{64,32},{96,64},{1,97},{33,1},{65,33},{97,65},{2,98}... | collective-permute-start | bytes 3145736 | tf_op jit(solution)/shard_map/ppermute | solution.py:476
  102.7 8.3 %collective-permute-start.17 = (bf16[512,128]{1,0:T(8,128)(2,1)S(1)}, bf16[512,128]{1,0:T(8,128)(2,1)S(1)}, u32[]{:S(2)}, u32[]{:S(2)}) collective-permute-start(bf16[512,128]{1,0:T(8,128)(2,1)S(1)} %fusion.20), channel_id=1, source_target_pairs={{0,16},{4,20},{8,24},{12,28},{16,0},{20,4},{24,8},{28,12},{1,17},{... | collective-permute-start | bytes 393224 | tf_op jit(solution)/shard_map/ppermute | solution.py:465
  108.5 6.8 %collective-permute-start.21 = (bf16[512,128]{1,0:T(8,128)(2,1)S(1)}, bf16[512,128]{1,0:T(8,128)(2,1)S(1)}, u32[]{:S(2)}, u32[]{:S(2)}) collective-permute-start(bf16[512,128]{1,0:T(8,128)(2,1)S(1)} %fusion.21), channel_id=1, source_target_pairs={{0,16},{4,20},{8,24},{12,28},{16,0},{20,4},{24,8},{28,12},{1,17},{... | collective-permute-start | bytes 393224 | tf_op jit(solution)/shard_map/ppermute | solution.py:465
  116.3 13.3 %collective-permute-start.25 = (bf16[64,4096]{1,0:T(8,128)(2,1)S(1)}, bf16[64,4096]{1,0:T(8,128)(2,1)S(1)}, u32[]{:S(2)}, u32[]{:S(2)}) collective-permute-start(bf16[64,4096]{1,0:T(8,128)(2,1)S(1)} %get-tuple-element.55), channel_id=1, source_target_pairs={{0,1},{1,2},{2,3},{3,0},{4,5},{5,6},{6,7},{7,4},{8,9},{9,10},{10,1... | collective-permute-start | bytes 1572872 | tf_op jit(solution)/shard_map/ppermute | solution.py:489
  118.2 39.9 %collective-permute-start.27 = (bf16[64,4096]{1,0:T(8,128)(2,1)S(1)}, bf16[64,4096]{1,0:T(8,128)(2,1)S(1)}, u32[]{:S(2)}, u32[]{:S(2)}) collective-permute-start(bf16[64,4096]{1,0:T(8,128)(2,1)S(1)} %slice.73), channel_id=1, source_target_pairs={{0,99},{1,96},{2,97},{3,98},{32,3},{33,0},{34,1},{35,2},{64,35},{6... | collective-permute-start | bytes 1572872 | tf_op jit(solution)/shard_map/ppermute | solution.py:494
  129.6 21.9 %collective-permute-start.29 = (bf16[64,4096]{1,0:T(8,128)(2,1)S(1)}, bf16[64,4096]{1,0:T(8,128)(2,1)S(1)}, u32[]{:S(2)}, u32[]{:S(2)}) collective-permute-start(bf16[64,4096]{1,0:T(8,128)(2,1)S(1)} %get-tuple-element.56), channel_id=1, source_target_pairs={{0,3},{1,0},{2,1},{3,2},{4,7},{5,4},{6,5},{7,6},{8,11},{9,8},{10,9... | collective-permute-start | bytes 1572872 | tf_op jit(solution)/shard_map/ppermute | solution.py:490
  151.5 3.7 %collective-permute-start.22 = (bf16[128,256]{1,0:T(8,128)(2,1)S(1)}, bf16[128,256]{1,0:T(8,128)(2,1)S(1)}, u32[]{:S(2)}, u32[]{:S(2)}) collective-permute-start(bf16[128,256]{1,0:T(8,128)(2,1)S(1)} %fusion.28), channel_id=1, source_target_pairs={{0,96},{32,0},{64,32},{96,64},{1,97},{33,1},{65,33},{97,65},{2,98}... | collective-permute-start | bytes 196616 | tf_op jit(solution)/shard_map/ppermute | solution.py:495
  151.7 19.2 %collective-permute-start.28 = (bf16[64,4096]{1,0:T(8,128)(2,1)S(1)}, bf16[64,4096]{1,0:T(8,128)(2,1)S(1)}, u32[]{:S(2)}, u32[]{:S(2)}) collective-permute-start(bf16[64,4096]{1,0:T(8,128)(2,1)S(1)} %slice.75), channel_id=1, source_target_pairs={{0,97},{1,98},{2,99},{3,96},{32,1},{33,2},{34,3},{35,0},{64,33},{6... | collective-permute-start | bytes 1572872 | tf_op jit(solution)/shard_map/ppermute | solution.py:493
  153.5 23.0 %collective-permute-start.26 = (bf16[64,4096]{1,0:T(8,128)(2,1)S(1)}, bf16[64,4096]{1,0:T(8,128)(2,1)S(1)}, u32[]{:S(2)}, u32[]{:S(2)}) collective-permute-start(bf16[64,4096]{1,0:T(8,128)(2,1)S(1)} %add_convert_fusion.1), channel_id=1, source_target_pairs={{0,97},{1,98},{2,99},{3,96},{32,1},{33,2},{34,3},{35,0},{64,33},{6... | collective-permute-start | bytes 1572872 | tf_op jit(solution)/shard_map/ppermute | solution.py:499
  155.2 21.2 %collective-permute-start.30 = (bf16[64,4096]{1,0:T(8,128)(2,1)S(1)}, bf16[64,4096]{1,0:T(8,128)(2,1)S(1)}, u32[]{:S(2)}, u32[]{:S(2)}) collective-permute-start(bf16[64,4096]{1,0:T(8,128)(2,1)S(1)} %add_convert_fusion), channel_id=1, source_target_pairs={{0,99},{1,96},{2,97},{3,98},{32,3},{33,0},{34,1},{35,2},{64,35},{6... | collective-permute-start | bytes 1572872 | tf_op jit(solution)/shard_map/ppermute | solution.py:501
  (16 other events, 135.4 us)
